TPU v7x, 256 devices: a whole 4x4x8 slice. The times are simulated.
256 devices in a mesh: store: 16 (over y, x_hi, core), dept: 16 (over z, x_lo).
Axes of the slice: x: 4 (x_hi: 2, x_lo: 2; x = x_hi * 2 + x_lo), y: 4, z: 8, core: 2. Of those that a mesh axis runs over, the one named last changes fastest.
Arguments:
- history: bfloat16 [4096, 384, 512], P('store', 'dept'), may hold values from -400 to 400, as said below
- input_layer_matrix: bfloat16 [512, 512], replicated, may hold values from -0.375 to 0.375
- middle_layer_matrix: bfloat16 [512, 512], replicated, may hold values from -0.375 to 0.375
- final_layer_matrix: bfloat16 [512, 28], replicated, may hold values from -0.375 to 0.375
Outputs:
- reconciled: float32 [4096, 10752], P('store', 'dept')
- store_gap: float32 [28, 4096], P(None, 'store')
- item_gap: float32 [28, 384], P(None, 'dept')
Inputs may be any that keep to these rules, and one draw needn't show every extreme that they name: `history`: daily sales histories.
All inputs are finite; a program needn't handle non-finite values.
Results may differ from a plain program's by a relative error of at most 0.0065.
The roundings to bfloat16 on the way count: a program that leaves them out, or rounds other values in their place, can miss the bound.
Values sent between devices are 32-bit elements; how exact they have to be, the bound alone decides.
No kernel may reach another device: no remote copies, remote signals or barrier semaphores. Data moves between devices by JAX's collectives and lax.ppermute only.
A program may use at most 64 MiB of HBM per device.

v0:
```python
import math

import jax
import jax.numpy as jnp
from jax import lax
from jax.sharding import PartitionSpec as P


def predictor_function(sequence_grid, input_layer_matrix, middle_layer_matrix, final_layer_matrix):
    values = sequence_grid.astype(jnp.float32)
    root_mean = jnp.sqrt(jnp.mean(values * values, axis=-1, keepdims=True) + 1e-05)
    scaled = (values / root_mean).astype(jnp.bfloat16)
    hidden_one = jax.nn.relu(
        jnp.dot(scaled, input_layer_matrix, preferred_element_type=jnp.float32)
    ).astype(jnp.bfloat16)
    hidden_two = jax.nn.relu(
        jnp.dot(hidden_one, middle_layer_matrix, preferred_element_type=jnp.float32)
    ).astype(jnp.bfloat16)
    return jnp.dot(hidden_two, final_layer_matrix, preferred_element_type=jnp.float32) * root_mean


def body(history, input_layer_matrix, middle_layer_matrix, final_layer_matrix):
    store_row_set, item_columns, history_count = history.shape
    horizon = final_layer_matrix.shape[1]
    widened_entries = history.astype(jnp.float32)
    store_part = jnp.sum(widened_entries, axis=1)
    item_part = jnp.sum(widened_entries, axis=0)
    product_past_sales = lax.psum(item_part, "store")
    outlet_past_sales = lax.psum(store_part, "dept")
    outlet_estimate = predictor_function(
        outlet_past_sales, input_layer_matrix, middle_layer_matrix, final_layer_matrix
    )
    product_estimate = predictor_function(
        product_past_sales, input_layer_matrix, middle_layer_matrix, final_layer_matrix
    )
    finest_tier = predictor_function(
        history.reshape(store_row_set * item_columns, history_count),
        input_layer_matrix,
        middle_layer_matrix,
        final_layer_matrix,
    )
    finest_tier = finest_tier.reshape(store_row_set, item_columns, horizon)
    row_part = jnp.sum(finest_tier, axis=1)
    col_part = jnp.sum(finest_tier, axis=0)
    row_sum = lax.psum(row_part, "dept")
    col_sum = lax.psum(col_part, "store")
    store_err = outlet_estimate - row_sum
    item_err = product_estimate - col_sum
    err_s = lax.psum(jnp.sum(store_err, axis=0), "store")
    err_i = lax.psum(jnp.sum(item_err, axis=0), "dept")
    item_count = float(item_columns * lax.axis_size("dept"))
    store_count = float(store_row_set * lax.axis_size("store"))
    denominator = 1.0 + item_count + store_count
    shift_s = (err_s * (1.0 + store_count) - store_count * err_i) / denominator
    shift_i = ((1.0 + item_count) * err_i - item_count * err_s) / denominator
    store_shift = (store_err - shift_i) / (1.0 + item_count)
    item_shift = (item_err - shift_s) / (1.0 + store_count)
    reconciled = finest_tier + store_shift[:, None, :] + item_shift[None, :, :]
    store_gap = (store_err / math.sqrt(item_count)).T
    item_gap = (item_err / math.sqrt(store_count)).T
    return (reconciled.reshape(store_row_set, item_columns * horizon), store_gap, item_gap)


def solution(mesh):
    return jax.shard_map(
        body,
        mesh=mesh,
        in_specs=(P("store", "dept", None), P(), P(), P()),
        out_specs=(P("store", "dept"), P(None, "store"), P(None, "dept")),
        check_vma=False,
    )
```

profile of v0, /device:TPU:1, one launch (start us, length us, event | category | flops | bytes accessed | tf_op | source)
XLA Modules:
  0.0 231.8 jit_solution(3153932601823036586)
XLA Ops:
  7.2 0.0 copy-start
  7.2 0.0 all-reduce.4.cloned.1.call-start
  7.2 6.6 %convert_reduce_fusion = (f32[24,512]{1,0:T(8,128)S(1)}, f32[256,24]{1,0:T(8,128)S(1)}, f32[256,512]{1,0:T(8,128)}) fusion(bf16[256,24,512]{2,1,0:T(8,128)(2,1)} %param.4), kind=kLoop, calls=%fused_computation.5 | loop fusion | flops 15579136 | bytes 6889472 | tf_op jit(solution)/shard_map/reduce_sum | solution.py:27
  13.8 0.0 all-reduce.4.cloned.1.call-update
  13.9 0.1 sqrt.28
  14.0 0.0 copy-start.1
  14.0 7.2 %fusion = bf16[6144,512]{1,0:T(8,128)(2,1)} fusion(bf16[256,24,512]{2,1,0:T(8,128)(2,1)} %param.4, f32[6144]{0:T(1024)S(1)} %sqrt.28), kind=kLoop, calls=%fused_computation.1 | loop fusion | flops 9437184 | bytes 12607488 | tf_op jit(solution)/shard_map/convert_element_type | solution.py:12
  21.3 0.0 copy-done
  21.3 0.0 copy-done.1
  21.3 0.0 copy-start.2
  21.3 10.4 %maximum_convert_fusion = bf16[6144,512]{1,0:T(8,128)(2,1)} fusion(bf16[512,512]{1,0:T(8,128)(2,1)S(1)} %copy-done, bf16[6144,512]{1,0:T(8,128)(2,1)} %fusion, bf16[512,512]{1,0:T(8,128)(2,1)S(1)} %copy-done.1), kind=kOutput, calls=%fused_computation.2 | convolution fusion | flops 6455033856 | bytes 13631488 | tf_op jit(solution)/shard_map/dot_general | solution.py:17
  31.7 0.0 copy-done.2
  31.7 4.7 %convolution_multiply_fusion = f32[6144,28]{0,1:T(8,128)S(1)} fusion(bf16[6144,512]{1,0:T(8,128)(2,1)} %maximum_convert_fusion, bf16[512,28]{0,1:T(8,128)(2,1)S(1)} %copy-done.2, f32[6144]{0:T(1024)S(1)} %sqrt.28), kind=kOutput, calls=%fused_computation.7 | convolution fusion | flops 176332800 | bytes 7032832 | tf_op jit(solution)/shard_map/dot_general | solution.py:19
  36.4 4.4 %reshape.57 = f32[256,24,28]{1,0,2:T(8,128)} reshape(f32[6144,28]{0,1:T(8,128)S(1)} %convolution_multiply_fusion) | data formatting | bytes 1376256 | tf_op jit(solution)/shard_map/reshape | solution.py:42
  40.8 3.1 %fusion.17 = (f32[24,28]{0,1:T(8,128)S(1)}, f32[256,28]{0,1:T(8,128)S(1)}) fusion(f32[256,24,28]{1,0,2:T(8,128)} %reshape.57), kind=kLoop, calls=%fused_computation.42 | loop fusion | flops 336224 | bytes 719488 | tf_op jit(solution)/shard_map/reduce_sum | solution.py:44
  43.9 0.1 copy.15
  44.0 65.5 %all-reduce.1 = (f32[24,28]{1,0:T(8,128)S(1)}, f32[24,512]{1,0:T(8,128)S(1)}) all-reduce(f32[24,28]{1,0:T(8,128)S(1)} %copy.15, f32[24,512]{1,0:T(8,128)S(1)} %get-tuple-element.12), channel_id=1, replica_groups=mesh['store'=16,'dept'=16] {'store'}, use_global_device_ids=true, to_apply=%region_10.11 | all-reduce | flops 12960 | bytes 103680 | tf_op jit(solution)/shard_map/psum | solution.py:46
  109.5 0.1 multiply_reduce_fusion.2
  109.6 2.2 copy.14
  111.8 2.4 %reshape.56 = f32[256,672]{1,0:T(8,128)S(1)} reshape(f32[6144,28]{1,0:T(8,128)} %copy.14) | data formatting | bytes 1376256 | tf_op jit(solution)/shard_map/reshape | solution.py:42
  114.3 0.4 fusion.5
  114.6 0.2 fusion.18
  114.8 53.4 %all-reduce = (f32[256,28]{0,1:T(8,128)S(1)}, f32[28]{0:T(128)S(1)}) all-reduce(f32[256,28]{0,1:T(8,128)S(1)} %get-tuple-element.16, f32[28]{0:T(128)S(1)} %get-tuple-element.27), channel_id=1, replica_groups=mesh['store'=16,'dept'=16] {'dept'}, use_global_device_ids=true, to_apply=%region_5.6 | all-reduce | flops 7196 | bytes 57568 | tf_op jit(solution)/shard_map/psum | solution.py:45
  168.2 0.0 all-reduce.4.cloned.1.call-done
  168.2 1.2 multiply_reduce_fusion.1
  169.4 1.6 fusion.3
  171.0 0.3 fusion.19
  171.3 50.7 %psum.47 = f32[28]{0:T(128)S(1)} all-reduce(f32[28]{0:T(128)S(1)} %get-tuple-element.29), channel_id=1, replica_groups=mesh['store'=16,'dept'=16] {'store'}, use_global_device_ids=true, to_apply=%region_14.15 | all-reduce | flops 28 | bytes 224 | tf_op jit(solution)/shard_map/psum | solution.py:49
  222.0 0.6 multiply_bitcast_fusion.1
  222.6 0.1 add.73
  222.7 0.6 multiply_bitcast_fusion
  223.3 0.1 add.70
  223.4 0.1 add.71
  223.5 0.3 copy.16
  223.8 0.1 add_add_fusion
  223.9 1.1 copy.17
  (4 shorter events, 0.1 us)
Async XLA Ops:
  7.2 14.1 %copy-start = (bf16[512,512]{1,0:T(8,128)(2,1)S(1)}, bf16[512,512]{1,0:T(8,128)(2,1)}, u32[]{:S(2)}) copy-start(bf16[512,512]{1,0:T(8,128)(2,1)} %param.6) | copy-start | bytes 1572868
  7.2 161.0 %all-reduce.4.cloned.1.call-start = ((), (), s32[]{:S(2)}) async-start(), calls=%async_computation | async-start | bytes 1048576 | tf_op jit(solution)/shard_map/psum | solution.py:29
  14.0 7.3 %copy-start.1 = (bf16[512,512]{1,0:T(8,128)(2,1)S(1)}, bf16[512,512]{1,0:T(8,128)(2,1)}, u32[]{:S(2)}) copy-start(bf16[512,512]{1,0:T(8,128)(2,1)} %param.5) | copy-start | bytes 1572868
  21.3 10.4 %copy-start.2 = (bf16[512,28]{0,1:T(8,128)(2,1)S(1)}, bf16[512,28]{0,1:T(8,128)(2,1)}, u32[]{:S(2)}) copy-start(bf16[512,28]{0,1:T(8,128)(2,1)} %param.7) | copy-start | bytes 86020
Sparse Core Ops, SparseCore 0:
  14.0 130.8 all-reduce.3
where the time goes:
time: 232 us
  blocking collectives  170 us (73%)
  other arithmetic  19.6 us (8%)
  matrix products  17.5 us (8%)
  between operations  14.1 us (6%)
  local copies, waits for them, and re-layouts  10.9 us (5%)
    psum x1, blocking collectives, body(): col_sum = lax.psum(col_part, 'store')  65.5 us
    psum x1, blocking collectives, body(): row_sum = lax.psum(row_part, 'dept')  53.4 us
    psum x1, blocking collectives, body(): err_s = lax.psum(jnp.sum(store_err, axis=0), 'store')  50.7 us
    dot_general x3, matrix products, predictor_function(): jnp.dot(hidden_one, middle_layer_matrix, preferred_element_type=jnp.float32)  12.4 us
    convert_element_type x1, other arithmetic, predictor_function(): scaled = (values / root_mean).astype(jnp.bfloat16)  7.24 us
    reshape x2, local copies, waits for them, and re-layouts, body(): finest_tier = finest_tier.reshape(store_row_set, item_columns, horizon)  6.88 us
    reduce_sum x1, other arithmetic, body(): item_part = jnp.sum(widened_entries, axis=0)  6.59 us
    dot_general x3, matrix products, predictor_function(): jnp.dot(hidden_two, final_layer_matrix, preferred_element_type=jnp.float32)  5.15 us
  transfers between devices with their start and end apart: 1, of which 0 were waited for; matrix products, arithmetic and copies ran while one was open for 15% of the time, Pallas kernels for 0%

commit v1 on v0

v1 whole, which is shorter than its diff:
```python
import functools
import math

import jax
import jax.numpy as jnp
from jax import lax
from jax.experimental import pallas as pl
from jax.experimental.pallas import tpu as pltpu
from jax.sharding import PartitionSpec as P

F32 = jnp.float32
BF16 = jnp.bfloat16
LANES = 128
GROUP = 32
VMEM_LIMIT = 50 * 1024 * 1024


def whole(n):
    return [pl.BlockSpec(memory_space=pltpu.VMEM)] * n


def params(semantics=None):
    return pltpu.CompilerParams(
        dimension_semantics=semantics, vmem_limit_bytes=VMEM_LIMIT
    )


def forecaster(x, w1, w2, w3):
    var = jnp.sum(x * x, axis=-1, keepdims=True) * (1.0 / x.shape[-1]) + 1e-05
    inv = lax.rsqrt(var)
    z = (x * inv).astype(BF16)
    a = jnp.maximum(jnp.dot(z, w1, preferred_element_type=F32), 0.0).astype(BF16)
    b = jnp.maximum(jnp.dot(a, w2, preferred_element_type=F32), 0.0).astype(BF16)
    return jnp.dot(b, w3, preferred_element_type=F32) * (var * inv)


def sums_kernel(h_ref, store_ref, item_ref):
    x = h_ref[...].astype(F32)
    store_ref[...] = jnp.sum(x, axis=1)

    @pl.when(pl.program_id(0) == 0)
    def _():
        item_ref[...] = jnp.zeros_like(item_ref)

    item_ref[: x.shape[1], :] += jnp.sum(x, axis=0)


def history_sums(history, item_rows, block):
    stores, items, days = history.shape
    return pl.pallas_call(
        sums_kernel,
        grid=(stores // block,),
        in_specs=[pl.BlockSpec((block, items, days), lambda i: (i, 0, 0))],
        out_specs=[
            pl.BlockSpec((block, days), lambda i: (i, 0)),
            pl.BlockSpec((item_rows, days), lambda i: (0, 0)),
        ],
        out_shape=[
            jax.ShapeDtypeStruct((stores, days), F32),
            jax.ShapeDtypeStruct((item_rows, days), F32),
        ],
        compiler_params=params(("arbitrary",)),
        cost_estimate=pl.CostEstimate(
            flops=2 * history.size, bytes_accessed=2 * history.size, transcendentals=0
        ),
        name="history_sums",
    )(history)


def base_kernel(horizon, part, h_ref, w1_ref, w2_ref, w3_ref, base_ref, row_ref, col_ref, y_ref):
    block, items, days = h_ref.shape
    w1, w2, w3 = w1_ref[...], w2_ref[...], w3_ref[...]
    for p in range(block // part):
        x = h_ref[p * part : (p + 1) * part].astype(F32).reshape(part * items, days)
        y_ref[p * part * items : (p + 1) * part * items, :] = forecaster(x, w1, w2, w3)
    y = y_ref[...].reshape(block, items, LANES)
    row_ref[...] = jnp.sum(y, axis=1)

    @pl.when(pl.program_id(0) == 0)
    def _():
        col_ref[...] = jnp.zeros_like(col_ref)

    col_ref[...] += jnp.sum(y, axis=0)
    lane = lax.broadcasted_iota(jnp.int32, (block, LANES), 1)
    tiles = [None] * pl.cdiv(items * horizon, LANES)

    def add(t, v):
        tiles[t] = v if tiles[t] is None else tiles[t] + v

    for i in range(items):
        v = y_ref[pl.ds(i, block, stride=items), :]
        t, off = divmod(i * horizon, LANES)
        if off:
            v = pltpu.roll(v, off, axis=1)
        if off + horizon > LANES:
            add(t, jnp.where(lane >= off, v, 0.0))
            add(t + 1, jnp.where(lane < off, v, 0.0))
        else:
            add(t, v)
    for t, v in enumerate(tiles):
        width = min(LANES, items * horizon - t * LANES)
        base_ref[:, t * LANES : t * LANES + width] = v[:, :width]


def base_forecasts(history, w1, w2, w3, horizon, block, part):
    stores, items, days = history.shape
    hid = w1.shape[1]
    rows = stores * items
    fixed = lambda shape: pl.BlockSpec(shape, lambda i: (0, 0))
    return pl.pallas_call(
        functools.partial(base_kernel, horizon, part),
        grid=(stores // block,),
        in_specs=[
            pl.BlockSpec((block, items, days), lambda i: (i, 0, 0)),
            fixed(w1.shape),
            fixed(w2.shape),
            fixed(w3.shape),
        ],
        out_specs=[
            pl.BlockSpec((block, items * horizon), lambda i: (i, 0)),
            pl.BlockSpec((block, LANES), lambda i: (i, 0)),
            fixed((items, LANES)),
        ],
        out_shape=[
            jax.ShapeDtypeStruct((stores, items * horizon), F32),
            jax.ShapeDtypeStruct((stores, LANES), F32),
            jax.ShapeDtypeStruct((items, LANES), F32),
        ],
        scratch_shapes=[pltpu.VMEM((block * items, LANES), F32)],
        compiler_params=params(("arbitrary",)),
        cost_estimate=pl.CostEstimate(
            flops=2 * rows * (days * hid + hid * hid + hid * LANES),
            bytes_accessed=2 * history.size + 4 * stores * items * horizon,
            transcendentals=0,
        ),
        name="base_forecasts",
    )(history, w1, w2, w3)


def totals_kernel(s_ref, i_ref, w1_ref, w2_ref, w3_ref, col_ref, fc_ref, pay_ref):
    peers, chunk, days = s_ref.shape
    per = i_ref.shape[1]
    xs = s_ref[0]
    xi = i_ref[0]
    for p in range(1, peers):
        xs = xs + s_ref[p]
        xi = xi + i_ref[p]
    pad = jnp.zeros((8 - per, days), F32)
    x = jnp.concatenate([xs, xi, pad], axis=0)
    y = forecaster(x, w1_ref[...], w2_ref[...], w3_ref[...])
    fc = y[:chunk]
    fi = y[chunk : chunk + per]
    fc_ref[...] = fc
    col = col_ref[...]
    sums = (
        jnp.sum(fc, axis=0, keepdims=True)
        + pltpu.roll(jnp.sum(fi, axis=0, keepdims=True), GROUP, axis=1)
        + pltpu.roll(jnp.sum(col, axis=0, keepdims=True), 2 * GROUP, axis=1)
    )
    forecasts = fi[0:1]
    for k in range(1, per):
        forecasts = forecasts + pltpu.roll(fi[k : k + 1], k * GROUP, axis=1)
    n = col.shape[0] // 4
    packed = col[0:n]
    for k in range(1, 4):
        packed = packed + pltpu.roll(col[k * n : (k + 1) * n], k * GROUP, axis=1)
    for p in range(peers):
        pay_ref[p, 0:n, :] = packed
        pay_ref[p, n : n + 1, :] = sums
        pay_ref[p, n + 1 : n + 2, :] = forecasts


def totals(store_parts, item_parts, w1, w2, w3, col):
    peers, chunk, _ = store_parts.shape
    return pl.pallas_call(
        totals_kernel,
        in_specs=whole(6),
        out_specs=whole(2),
        out_shape=[
            jax.ShapeDtypeStruct((chunk, LANES), F32),
            jax.ShapeDtypeStruct((peers, 8, LANES), F32),
        ],
        compiler_params=params(),
        name="totals",
    )(store_parts, item_parts, w1, w2, w3, col)


def middle_kernel(fc_ref, row_ref, got_ref, pay_ref):
    peers, chunk, _ = row_ref.shape
    row = row_ref[0]
    for p in range(1, peers):
        row = row + row_ref[p]
    n = 6
    sums = got_ref[0, n : n + 1, :]
    for p in range(1, got_ref.shape[0]):
        sums = sums + got_ref[p, n : n + 1, :]
    err = fc_ref[...] - row
    q = chunk // 4
    packed = err[0:q]
    for k in range(1, 4):
        packed = packed + pltpu.roll(err[k * q : (k + 1) * q], k * GROUP, axis=1)
    for p in range(peers):
        pay_ref[p, 0:q, :] = packed
        pay_ref[p, q : q + 1, :] = sums


def middle(fc, row_parts, got):
    peers = row_parts.shape[0]
    return pl.pallas_call(
        middle_kernel,
        in_specs=whole(3),
        out_specs=whole(1)[0],
        out_shape=jax.ShapeDtypeStruct((peers, 8, LANES), F32),
        compiler_params=params(),
        name="middle",
    )(fc, row_parts, got)


def final_kernel(horizon, item_count, store_count, base_ref, one_ref, two_ref, out_ref, sgap_ref, igap_ref, err_ref):
    stores, width = base_ref.shape
    items = width // horizon
    peers = two_ref.shape[0]
    lane1 = lax.broadcasted_iota(jnp.int32, (1, LANES), 1)
    valid1 = lane1 < horizon

    n = items // 4
    per = items // (items // 2)
    colp = one_ref[0, 0:n, :]
    for p in range(1, one_ref.shape[0]):
        colp = colp + one_ref[p, 0:n, :]
    groups = []
    for k in range(4):
        g = colp if k == 0 else pltpu.roll(colp, LANES - k * GROUP, axis=1)
        groups.append(jnp.where(valid1, g, 0.0))
    col = jnp.concatenate(groups, axis=0)
    rows = []
    for i in range(items):
        p, k = divmod(i, per)
        g = one_ref[p, n + 1 : n + 2, :]
        if k:
            g = pltpu.roll(g, LANES - k * GROUP, axis=1)
        rows.append(jnp.where(valid1, g, 0.0))
    item_err = jnp.concatenate(rows, axis=0) - col

    q = stores // peers // 4
    sums = two_ref[0, q : q + 1, :]
    for p in range(1, peers):
        sums = sums + two_ref[p, q : q + 1, :]
    total = pltpu.roll(sums, LANES - 2 * GROUP, axis=1)
    err_s = jnp.where(valid1, sums - total, 0.0)
    err_i = jnp.where(valid1, pltpu.roll(sums, LANES - GROUP, axis=1) - total, 0.0)
    for k in range(4):
        for p in range(peers):
            g = two_ref[p, 0:q, :]
            if k:
                g = pltpu.roll(g, LANES - k * GROUP, axis=1)
            r = p * 4 * q + k * q
            err_ref[r : r + q, :] = jnp.where(valid1, g, 0.0)
    store_err = err_ref[...]

    denominator = 1.0 + item_count + store_count
    shift_s = (err_s * (1.0 + store_count) - store_count * err_i) / denominator
    shift_i = ((1.0 + item_count) * err_i - item_count * err_s) / denominator
    store_shift = (store_err - shift_i) / (1.0 + item_count)
    item_shift = (item_err - shift_s) / (1.0 + store_count)

    day = lax.broadcasted_iota(jnp.int32, (LANES, LANES), 0)
    lane = lax.broadcasted_iota(jnp.int32, (LANES, LANES), 1)
    which = lax.broadcasted_iota(jnp.int32, (items, LANES), 0)
    lane_i = lax.broadcasted_iota(jnp.int32, (items, LANES), 1)
    for t in range(pl.cdiv(width, LANES)):
        first = (t * LANES) // horizon
        place = lane + (t * LANES - first * horizon) - day
        one_hot = jnp.zeros((LANES, LANES), F32)
        for m in range(LANES // horizon + 2):
            one_hot = jnp.where((place == m * horizon) & (day < horizon), 1.0, one_hot)
        spread = functools.partial(
            jnp.dot, precision=lax.Precision.HIGHEST, preferred_element_type=F32
        )
        a = spread(store_shift, one_hot)
        b = spread(item_shift, one_hot)
        pos = lane_i + t * LANES - which * horizon
        b = jnp.sum(jnp.where((pos >= 0) & (pos < horizon), b, 0.0), axis=0, keepdims=True)
        w = min(LANES, width - t * LANES)
        out_ref[:, t * LANES : t * LANES + w] = (
            base_ref[:, t * LANES : t * LANES + w] + a[:, :w] + b[:, :w]
        )
    sgap_ref[...] = (store_err * (1.0 / math.sqrt(item_count))).T[:horizon, :]
    padded = jnp.concatenate([item_err, jnp.zeros((LANES - items, LANES), F32)], axis=0)
    igap_ref[...] = (padded * (1.0 / math.sqrt(store_count))).T[:horizon, :items]


def final(base, one, two, horizon, item_count, store_count):
    stores, width = base.shape
    items = width // horizon
    return pl.pallas_call(
        functools.partial(final_kernel, horizon, item_count, store_count),
        in_specs=whole(3),
        out_specs=whole(3),
        out_shape=[
            jax.ShapeDtypeStruct((stores, width), F32),
            jax.ShapeDtypeStruct((horizon, stores), F32),
            jax.ShapeDtypeStruct((horizon, items), F32),
        ],
        scratch_shapes=[pltpu.VMEM((stores, LANES), F32)],
        compiler_params=params(),
        name="final",
    )(base, one, two)


def exchange(x, axis):
    return lax.all_to_all(x, axis, 0, 0, tiled=True)


def body(history, w1, w2, final_layer_matrix):
    stores, items, days = history.shape
    horizon = final_layer_matrix.shape[1]
    n_store, n_dept = lax.axis_size("store"), lax.axis_size("dept")
    per = pl.cdiv(items, n_store)
    w3 = jnp.pad(final_layer_matrix, ((0, 0), (0, LANES - horizon)))

    store_part, item_part = history_sums(history, per * n_store, 32)
    store_parts = exchange(store_part.reshape(n_dept, stores // n_dept, days), "dept")
    item_parts = exchange(item_part.reshape(n_store, per, days), "store")
    base, row_part, col_part = base_forecasts(history, w1, w2, w3, horizon, 32, 8)
    row_parts = exchange(row_part.reshape(n_dept, stores // n_dept, LANES), "dept")
    fc, pay_one = totals(store_parts, item_parts, w1, w2, w3, col_part)
    one = exchange(pay_one, "store")
    pay_two = middle(fc, row_parts, one)
    two = exchange(pay_two, "dept")
    return final(base, one, two, horizon, float(items * n_dept), float(stores * n_store))


def solution(mesh):
    return jax.shard_map(
        body,
        mesh=mesh,
        in_specs=(P("store", "dept", None), P(), P(), P()),
        out_specs=(P("store", "dept"), P(None, "store"), P(None, "dept")),
        check_vma=False,
    )
```

time: 232 us -> 94.2 us (0.41)
  blocking collectives: 170 us -> 38.7 us
  Pallas kernels: 0 us -> 28.5 us
  other arithmetic: 19.6 us -> 0 us
  matrix products: 17.5 us -> 0 us
  starting transfers between devices: 0.04 us -> 15.9 us
  between operations: 14.1 us -> 0.71 us
  local copies, waits for them, and re-layouts: 10.9 us -> 2 us
  waiting for transfers between devices: 0.02 us -> 7.93 us
    psum x3 -> x0, blocking collectives: 170 us -> none  [the longest x1 65.5 us: body(): col_sum = lax.psum(col_part, 'store')]
    all_to_all x0 -> x3, blocking collectives: none -> 38.7 us  [exchange(): return lax.all_to_all(x, axis, 0, 0, tiled=True)]
    pallas_call x0 -> x5, Pallas kernels: none -> 28.5 us  [the longest x1 19.1 us: base_forecasts(): pl.pallas_call(functools.partial(base_kernel, horizon, part), grid=(store...]
    dot_general x6 -> x0, matrix products: 17.5 us -> none  [the longest x3 12.4 us: predictor_function(): jnp.dot(hidden_one, middle_layer_matrix, preferred_element_type=jnp.float32)]
    all_to_all x0 -> x2, starting transfers between devices: none -> 15.9 us  [exchange(): return lax.all_to_all(x, axis, 0, 0, tiled=True)]
    reduce_sum x4 -> x0, other arithmetic: 10.9 us -> none  [the longest x1 6.59 us: body(): item_part = jnp.sum(widened_entries, axis=0)]
    all_to_all x0 -> x2, waiting for transfers between devices: none -> 7.93 us  [exchange(): return lax.all_to_all(x, axis, 0, 0, tiled=True)]
    convert_element_type x1 -> x0, other arithmetic: 7.24 us -> none  [predictor_function(): scaled = (values / root_mean).astype(jnp.bfloat16)]
  transfers between devices with their start and end apart: 1 -> 2, of which waited for: 0 -> 1; matrix products, arithmetic and copies ran while one was open for 15% -> 0% of each run, Pallas kernels for 0% -> 21%
where the time goes in v1:
time: 94.2 us; the launch traced here: 93.7 us
  blocking collectives  38.7 us (41%)
  Pallas kernels  28.5 us (30%)
  starting transfers between devices  15.9 us (17%)
  waiting for transfers between devices  7.93 us (8%)
  local copies, waits for them, and re-layouts  2 us (2%)
    all_to_all x3, blocking collectives, exchange(): return lax.all_to_all(x, axis, 0, 0, tiled=True)  38.7 us
    pallas_call x1, Pallas kernels, base_forecasts(): pl.pallas_call(functools.partial(base_kernel, horizon, part), grid=(store...  19.1 us
    all_to_all x2, starting transfers between devices, exchange(): return lax.all_to_all(x, axis, 0, 0, tiled=True)  15.9 us
    all_to_all x2, waiting for transfers between devices, exchange(): return lax.all_to_all(x, axis, 0, 0, tiled=True)  7.93 us
    pallas_call x1, Pallas kernels, history_sums(): pl.pallas_call(sums_kernel, grid=(stores // block,), in_specs=[pl.BlockSp...  7.13 us
  transfers between devices with their start and end apart: 2, of which 1 were waited for; matrix products, arithmetic and copies ran while one was open for 0% of the time, Pallas kernels for 21%

profile of v1, /device:TPU:1, one launch (start us, length us, event | category | flops | bytes accessed | tf_op | source)
XLA Modules:
  0.0 93.7 jit_solution(10450349044730528118)
XLA Ops:
  0.6 0.0 copy-start.2
  0.6 0.0 copy-start.1
  0.7 0.0 copy-start
  0.7 7.1 %history_sums.1 = (f32[256,512]{1,0:T(8,128)}, f32[32,512]{1,0:T(8,128)S(1)}) custom-call(bf16[256,24,512]{2,1,0:T(8,128)(2,1)} %h_ref.3), custom_call_target="tpu_custom_call" | custom-call | flops 6291456 | bytes 6291456 | tf_op jit(solution)/shard_map/history_sums/pallas_call | solution.py:50
  7.8 15.6 %all_to_all.25.i_ref = f32[16,2,512]{2,1,0:T(2,128)S(1)} all-to-all(f32[16,2,512]{2,1,0:T(2,128)S(1)} %reshape.16), channel_id=1, replica_groups=mesh['store'=16,'dept'=16] {'store'}, dimensions={0} | all-to-all | bytes 131072 | tf_op jit(solution)/shard_map/all_to_all | solution.py:312
  23.4 8.3 %all-to-all-start = ((f32[16,16,512]{2,1,0:T(8,128)}), f32[16,16,512]{2,1,0:T(8,128)S(1)}, u32[]{:S(2)}, u32[]{:S(2)}) async-start(f32[16,16,512]{2,1,0:T(8,128)} %bitcast), calls=%async_computation | async-start | bytes 1048576 | tf_op jit(solution)/shard_map/all_to_all | solution.py:312
  31.7 0.0 copy-done.2
  31.7 0.1 copy.7
  31.9 0.0 copy-done.1
  31.9 0.0 copy-done
  31.9 19.1 %base_forecasts.1 = (f32[256,672]{1,0:T(8,128)S(1)}, f32[256,128]{1,0:T(8,128)}, f32[24,128]{1,0:T(8,128)S(1)}) custom-call(bf16[256,24,512]{2,1,0:T(8,128)(2,1)} %h_ref.3, bf16[512,512]{1,0:T(8,128)(2,1)S(1)} %copy-done, bf16[512,512]{1,0:T(8,128)(2,1)S(1)} %copy-done.1, bf16[512,128]{1,0:T(8,128)(2,1)S(1)} %pad.4.w3_ref), custom_call_target="tpu_custom_call" | custom-call | flops 7247757312 | bytes 6979584 | tf_op jit(solution)/shard_map/base_forecasts/pallas_call | solution.py:110
  51.0 0.0 all-to-all-done.s_ref
  51.0 7.6 %all-to-all-start.3 = ((f32[16,16,128]{2,1,0:T(8,128)}), f32[16,16,128]{2,1,0:T(8,128)S(1)}, u32[]{:S(2)}, u32[]{:S(2)}) async-start(f32[16,16,128]{2,1,0:T(8,128)} %bitcast.1), calls=%async_computation.3 | async-start | bytes 262144 | tf_op jit(solution)/shard_map/all_to_all | solution.py:312
  58.6 0.6 totals.1
  59.2 7.9 %all-to-all-done.3.row_ref = f32[16,16,128]{2,1,0:T(8,128)S(1)} async-done(((f32[16,16,128]{2,1,0:T(8,128)}), f32[16,16,128]{2,1,0:T(8,128)S(1)}, u32[]{:S(2)}, u32[]{:S(2)}) %all-to-all-start.3) | async-done | bytes 131104 | tf_op jit(solution)/shard_map/all_to_all | solution.py:312
  67.2 12.6 %all_to_all.26.got_ref.one_ref = f32[16,8,128]{2,1,0:T(8,128)S(1)} all-to-all(f32[16,8,128]{2,1,0:T(8,128)S(1)} %get-tuple-element.14), channel_id=1, replica_groups=mesh['store'=16,'dept'=16] {'store'}, dimensions={0} | all-to-all | bytes 131072 | tf_op jit(solution)/shard_map/all_to_all | solution.py:312
  79.7 0.1 middle.1
  79.8 10.5 %all_to_all.27.two_ref = f32[16,8,128]{2,1,0:T(8,128)S(1)} all-to-all(f32[16,8,128]{2,1,0:T(8,128)S(1)} %middle.1), channel_id=1, replica_groups=mesh['store'=16,'dept'=16] {'dept'}, dimensions={0} | all-to-all | bytes 131072 | tf_op jit(solution)/shard_map/all_to_all | solution.py:312
  90.4 1.6 %final.1 = (f32[256,672]{1,0:T(8,128)S(1)}, f32[28,256]{1,0:T(8,128)}, f32[28,24]{1,0:T(8,128)S(1)}) custom-call(f32[256,672]{1,0:T(8,128)S(1)} %get-tuple-element.10.base_ref, f32[16,8,128]{2,1,0:T(8,128)S(1)} %all_to_all.26.got_ref.one_ref, f32[16,8,128]{2,1,0:T(8,128)S(1)} %all_to_all.27.two_ref), custom_call_target="tpu_custom_call" | custom-call | tf_op jit(solution)/shard_map/final/pallas_call | solution.py:296
  91.9 1.1 %copy.8 = f32[256,672]{0,1:T(8,128)} copy(f32[256,672]{1,0:T(8,128)S(1)} %get-tuple-element.17) | data formatting | bytes 1376256 | tf_op jit(solution)/shard_map/final/pallas_call | solution.py:296
  93.0 0.7 copy.9
  (2 shorter events, 0.1 us)
Async XLA Ops:
  0.6 31.1 %copy-start.2 = (bf16[512,28]{0,1:T(8,128)(2,1)S(1)}, bf16[512,28]{0,1:T(8,128)(2,1)}, u32[]{:S(2)}) copy-start(bf16[512,28]{0,1:T(8,128)(2,1)} %param.7) | copy-start | bytes 86020
  0.6 31.3 %copy-start.1 = (bf16[512,512]{1,0:T(8,128)(2,1)S(1)}, bf16[512,512]{1,0:T(8,128)(2,1)}, u32[]{:S(2)}) copy-start(bf16[512,512]{1,0:T(8,128)(2,1)} %w2_ref.3) | copy-start | bytes 1572868
  0.7 31.3 %copy-start = (bf16[512,512]{1,0:T(8,128)(2,1)S(1)}, bf16[512,512]{1,0:T(8,128)(2,1)}, u32[]{:S(2)}) copy-start(bf16[512,512]{1,0:T(8,128)(2,1)} %w1_ref.3) | copy-start | bytes 1572868
  23.4 27.6 %all-to-all-start = ((f32[16,16,512]{2,1,0:T(8,128)}), f32[16,16,512]{2,1,0:T(8,128)S(1)}, u32[]{:S(2)}, u32[]{:S(2)}) async-start(f32[16,16,512]{2,1,0:T(8,128)} %bitcast), calls=%async_computation | async-start | bytes 1048576 | tf_op jit(solution)/shard_map/all_to_all | solution.py:312
  51.0 16.1 %all-to-all-start.3 = ((f32[16,16,128]{2,1,0:T(8,128)}), f32[16,16,128]{2,1,0:T(8,128)S(1)}, u32[]{:S(2)}, u32[]{:S(2)}) async-start(f32[16,16,128]{2,1,0:T(8,128)} %bitcast.1), calls=%async_computation.3 | async-start | bytes 262144 | tf_op jit(solution)/shard_map/all_to_all | solution.py:312

commit v2 on v0

v2 whole, which is shorter than its diff:
```python
import functools
import math

import jax
import jax.numpy as jnp
from jax import lax
from jax.experimental import pallas as pl
from jax.experimental.pallas import tpu as pltpu
from jax.sharding import PartitionSpec as P

F32 = jnp.float32
BF16 = jnp.bfloat16
LANES = 128
GROUP = 32
VMEM_LIMIT = 50 * 1024 * 1024


def whole(n):
    return [pl.BlockSpec(memory_space=pltpu.VMEM)] * n


def params(semantics=None, limit=VMEM_LIMIT):
    return pltpu.CompilerParams(dimension_semantics=semantics, vmem_limit_bytes=limit)


def relu(x):
    return jnp.maximum(x.astype(BF16), 0)


def forecaster(x, w1, w2, w3):
    var = jnp.sum(x * x, axis=-1, keepdims=True) * (1.0 / x.shape[-1]) + 1e-05
    inv = lax.rsqrt(var)
    z = (x * inv).astype(BF16)
    a = relu(jnp.dot(z, w1, preferred_element_type=F32))
    b = relu(jnp.dot(a, w2, preferred_element_type=F32))
    return jnp.dot(b, w3, preferred_element_type=F32) * (var * inv)


def widen(w3_ref, w3_wide):
    horizon = w3_ref.shape[0]
    w3_wide[...] = jnp.zeros_like(w3_wide)
    w3_wide[:, :horizon] = w3_ref[...].astype(F32).T.astype(BF16)


def pack_rows(x):
    n = x.shape[0] // 4
    out = x[0:n]
    for k in range(1, 4):
        out = out + pltpu.roll(x[k * n : (k + 1) * n], k * GROUP, axis=1)
    return out


def bottom_kernel(chunk, part, h_ref, w1_ref, w2_ref, w3_ref, pay_ref, item_ref, col_ref, y_ref, w3_wide):
    block, items, days = h_ref.shape
    step = pl.program_id(0)

    @pl.when(step == 0)
    def _():
        widen(w3_ref, w3_wide)
        item_ref[...] = jnp.zeros_like(item_ref)
        col_ref[...] = jnp.zeros_like(col_ref)

    w1, w2, w3 = w1_ref[...], w2_ref[...], w3_wide[...]
    tiles = days // LANES
    for p in range(block // part):
        x = h_ref[p * part : (p + 1) * part].astype(F32)
        by_store = jnp.sum(x, axis=1)
        item_ref[...] += jnp.sum(x, axis=0)
        y = forecaster(x.reshape(part * items, days), w1, w2, w3)
        y_ref[p * part * items : (p + 1) * part * items, :] = y
        y = y.reshape(part, items, LANES)
        row = jnp.sum(y, axis=1)
        col_ref[...] += jnp.sum(y, axis=0)
        for q in range(part // chunk):
            peer = p * (part // chunk) + q
            for t in range(tiles):
                pay_ref[peer, t * chunk : (t + 1) * chunk, :] = by_store[
                    q * chunk : (q + 1) * chunk, t * LANES : (t + 1) * LANES
                ]
            pay_ref[peer, tiles * chunk : tiles * chunk + chunk // 4, :] = pack_rows(
                row[q * chunk : (q + 1) * chunk]
            )


def bottom(history, w1, w2, w3, peers, block, part):
    stores, items, days = history.shape
    hid = w1.shape[1]
    rows = stores * items
    chunk = stores // peers
    pay_rows = (days // LANES) * chunk + 8
    fixed = lambda shape: pl.BlockSpec(shape, lambda i: (0,) * len(shape))
    return pl.pallas_call(
        functools.partial(bottom_kernel, chunk, part),
        grid=(stores // block,),
        in_specs=[
            pl.BlockSpec((block, items, days), lambda i: (i, 0, 0)),
            fixed(w1.shape),
            fixed(w2.shape),
            fixed(w3.shape),
        ],
        out_specs=[
            pl.BlockSpec((block // chunk, pay_rows, LANES), lambda i: (i, 0, 0)),
            fixed((items, days)),
            fixed((items, LANES)),
            pl.BlockSpec((block * items, LANES), lambda i: (i, 0)),
        ],
        out_shape=[
            jax.ShapeDtypeStruct((peers, pay_rows, LANES), F32),
            jax.ShapeDtypeStruct((items, days), F32),
            jax.ShapeDtypeStruct((items, LANES), F32),
            jax.ShapeDtypeStruct((rows, LANES), F32),
        ],
        scratch_shapes=[pltpu.VMEM((hid, LANES), BF16)],
        compiler_params=params(("arbitrary",), 58 * 1024 * 1024),
        cost_estimate=pl.CostEstimate(
            flops=2 * rows * (days * hid + hid * hid + hid * LANES),
            bytes_accessed=2 * history.size + 4 * rows * LANES,
            transcendentals=0,
        ),
        name="bottom",
    )(history, w1, w2, w3)


def arrange_kernel(horizon, items, y_ref, out_ref):
    stores = y_ref.shape[0] // items
    lane = lax.broadcasted_iota(jnp.int32, (stores, LANES), 1)
    tiles = [None] * pl.cdiv(items * horizon, LANES)

    def add(t, v):
        tiles[t] = v if tiles[t] is None else tiles[t] + v

    for i in range(items):
        v = y_ref[pl.ds(i, stores, stride=items), :]
        t, off = divmod(i * horizon, LANES)
        if off:
            v = pltpu.roll(v, off, axis=1)
        if off + horizon > LANES:
            add(t, jnp.where(lane >= off, v, 0.0))
            add(t + 1, jnp.where(lane < off, v, 0.0))
        else:
            add(t, v)
    for t, v in enumerate(tiles):
        height = min(LANES, items * horizon - t * LANES)
        out_ref[t * LANES : t * LANES + height, :] = v.T[:height]


def arrange(y, items, horizon):
    rows = y.shape[0]
    return pl.pallas_call(
        functools.partial(arrange_kernel, horizon, items),
        in_specs=whole(1),
        out_specs=whole(1)[0],
        out_shape=jax.ShapeDtypeStruct((items * horizon, rows // items), F32),
        compiler_params=params(),
        cost_estimate=pl.CostEstimate(
            flops=rows * LANES * 4, bytes_accessed=rows * LANES * 4, transcendentals=0
        ),
        name="arrange",
    )(y)


def totals_kernel(chunk, s_ref, i_ref, w1_ref, w2_ref, w3_ref, col_ref, err_ref, item_ref, pay_ref, w3_wide):
    days = w1_ref.shape[0]
    widen(w3_ref, w3_wide)
    got = s_ref[0]
    for p in range(1, s_ref.shape[0]):
        got = got + s_ref[p]
    tiles = days // LANES
    x = jnp.concatenate([got[t * chunk : (t + 1) * chunk] for t in range(tiles)], axis=1)
    x = jnp.concatenate([x, i_ref[...]], axis=0)
    y = forecaster(x, w1_ref[...], w2_ref[...], w3_wide[...])
    fc = y[:chunk]
    fi = y[chunk:]
    item_ref[...] = fi
    q = chunk // 4
    err_ref[0:q, :] = pack_rows(fc) - got[tiles * chunk : tiles * chunk + q]
    err_ref[q : q + 1, :] = pltpu.roll(jnp.sum(fi, axis=0, keepdims=True), GROUP, axis=1)
    col = col_ref[...]
    sums = jnp.sum(fc, axis=0, keepdims=True) + pltpu.roll(
        jnp.sum(col, axis=0, keepdims=True), 2 * GROUP, axis=1
    )
    packed = pack_rows(col)
    n = packed.shape[0]
    for p in range(pay_ref.shape[0]):
        pay_ref[p, 0:n, :] = packed
        pay_ref[p, n : n + 1, :] = sums


def totals(store_parts, item_hist, w1, w2, w3, col, chunk, item_peers):
    items = item_hist.shape[0]
    return pl.pallas_call(
        functools.partial(totals_kernel, chunk),
        in_specs=whole(6),
        out_specs=whole(3),
        out_shape=[
            jax.ShapeDtypeStruct((8, LANES), F32),
            jax.ShapeDtypeStruct((items, LANES), F32),
            jax.ShapeDtypeStruct((item_peers, 8, LANES), F32),
        ],
        scratch_shapes=[pltpu.VMEM((w1.shape[1], LANES), BF16)],
        compiler_params=params(),
        name="totals",
    )(store_parts, item_hist, w1, w2, w3, col)


def middle_kernel(chunk, n, err_ref, got_ref, pay_ref):
    q = chunk // 4
    sums = err_ref[q : q + 1, :]
    for p in range(got_ref.shape[0]):
        sums = sums + got_ref[p, n : n + 1, :]
    err = err_ref[0:q, :]
    for p in range(pay_ref.shape[0]):
        pay_ref[p, 0:q, :] = err
        pay_ref[p, q : q + 1, :] = sums


def middle(err, got, chunk, items, peers):
    return pl.pallas_call(
        functools.partial(middle_kernel, chunk, items // 4),
        in_specs=whole(2),
        out_specs=whole(1)[0],
        out_shape=jax.ShapeDtypeStruct((peers, 8, LANES), F32),
        compiler_params=params(),
        name="middle",
    )(err, got)


def final_kernel(horizon, item_count, store_count, base_ref, item_ref, one_ref, two_ref, out_ref, sgap_ref, igap_ref, err_ref):
    width, stores = base_ref.shape
    items = width // horizon
    peers = two_ref.shape[0]
    valid1 = lax.broadcasted_iota(jnp.int32, (1, LANES), 1) < horizon

    def group(x, k):
        if k:
            x = pltpu.roll(x, LANES - k * GROUP, axis=1)
        return jnp.where(valid1, x, 0.0)

    n = items // 4
    colp = one_ref[0, 0:n, :]
    for p in range(1, one_ref.shape[0]):
        colp = colp + one_ref[p, 0:n, :]
    col = jnp.concatenate([group(colp, k) for k in range(4)], axis=0)
    item_err = item_ref[...] - col

    q = stores // peers // 4
    sums = two_ref[0, q : q + 1, :]
    for p in range(1, peers):
        sums = sums + two_ref[p, q : q + 1, :]
    total = group(sums, 2)
    err_s = group(sums, 0) - total
    err_i = group(sums, 1) - total
    for p in range(peers):
        for k in range(4):
            r = (p * 4 + k) * q
            err_ref[r : r + q, :] = group(two_ref[p, 0:q, :], k)
    store_err = err_ref[...].T[:horizon]

    denominator = 1.0 + item_count + store_count
    shift_s = (err_s * (1.0 + store_count) - store_count * err_i) / denominator
    shift_i = ((1.0 + item_count) * err_i - item_count * err_s) / denominator
    item_shift = (item_err - shift_s) / (1.0 + store_count)
    columns = jnp.concatenate(
        [item_shift, shift_i, jnp.zeros((LANES - items - 1, LANES), F32)], axis=0
    ).T[:horizon]
    store_shift = (store_err - columns[:, items : items + 1]) / (1.0 + item_count)

    a = jnp.concatenate([store_shift, store_shift], axis=0)
    b = jnp.concatenate([columns, pltpu.roll(columns, LANES - 1, axis=1)], axis=0)
    for j in range(items // 2):
        rows = slice(2 * j * horizon, (2 * j + 2) * horizon)
        out_ref[rows, :] = base_ref[rows, :] + a + b[:, 2 * j : 2 * j + 1]
    sgap_ref[...] = store_err * (1.0 / math.sqrt(item_count))
    igap_ref[...] = item_err[:, :horizon] * (1.0 / math.sqrt(store_count))


def final(base, item_fc, one, two, horizon, item_count, store_count):
    width, stores = base.shape
    items = width // horizon
    return pl.pallas_call(
        functools.partial(final_kernel, horizon, item_count, store_count),
        in_specs=whole(4),
        out_specs=whole(3),
        out_shape=[
            jax.ShapeDtypeStruct((width, stores), F32),
            jax.ShapeDtypeStruct((horizon, stores), F32),
            jax.ShapeDtypeStruct((items, horizon), F32),
        ],
        scratch_shapes=[pltpu.VMEM((stores, LANES), F32)],
        compiler_params=params(),
        name="final",
    )(base, item_fc, one, two)


def exchange(x, axis):
    return lax.all_to_all(x, axis, 0, 0, tiled=True)


def add_over(x, axis, flips):
    for flip in flips:
        pairs = [(i, i ^ flip) for i in range(lax.axis_size(axis))]
        x = x + lax.ppermute(x, axis, pairs)
    return x


def body(history, w1, w2, final_layer_matrix):
    stores, items, _ = history.shape
    horizon = final_layer_matrix.shape[1]
    n_store, n_dept = lax.axis_size("store"), lax.axis_size("dept")
    chunk = stores // n_dept
    w3 = final_layer_matrix.T

    pay, item_part, col, y = bottom(history, w1, w2, w3, n_dept, 64, 32)
    store_parts = exchange(pay, "dept")
    item_hist = add_over(item_part, "store", (1, 2, 4, 12))
    base = arrange(y, items, horizon)
    err, item_fc, pay_one = totals(store_parts, item_hist, w1, w2, w3, col, chunk, n_store)
    one = exchange(pay_one, "store")
    pay_two = middle(err, one, chunk, items, n_dept)
    two = exchange(pay_two, "dept")
    out, store_gap, item_gap = final(
        base, item_fc, one, two, horizon, float(items * n_dept), float(stores * n_store)
    )
    return out.T, store_gap, item_gap.T


def solution(mesh):
    return jax.shard_map(
        body,
        mesh=mesh,
        in_specs=(P("store", "dept", None), P(), P(), P()),
        out_specs=(P("store", "dept"), P(None, "store"), P(None, "dept")),
        check_vma=False,
    )
```

time: 232 us -> 76.6 us (0.33)
  blocking collectives: 170 us -> 16.6 us
  starting transfers between devices: 0.04 us -> 23.9 us
  other arithmetic: 19.6 us -> 0.83 us
  Pallas kernels: 0 us -> 18.1 us
  matrix products: 17.5 us -> 0 us
  waiting for transfers between devices: 0.02 us -> 13.4 us
  between operations: 14.1 us -> 0.72 us
  local copies, waits for them, and re-layouts: 10.9 us -> 2.6 us
    psum x3 -> x0, blocking collectives: 170 us -> none  [the longest x1 65.5 us: body(): col_sum = lax.psum(col_part, 'store')]
    pallas_call x0 -> x5, Pallas kernels: none -> 18.1 us  [the longest x1 14.4 us: bottom(): pl.pallas_call(functools.partial(bottom_kernel, chunk, part), grid=(store...]
    dot_general x6 -> x0, matrix products: 17.5 us -> none  [the longest x3 12.4 us: predictor_function(): jnp.dot(hidden_one, middle_layer_matrix, preferred_element_type=jnp.float32)]
    all_to_all x0 -> x1, blocking collectives: none -> 16.6 us  [exchange(): return lax.all_to_all(x, axis, 0, 0, tiled=True)]
    all_to_all x0 -> x2, starting transfers between devices: none -> 16.2 us  [exchange(): return lax.all_to_all(x, axis, 0, 0, tiled=True)]
    reduce_sum x4 -> x0, other arithmetic: 10.9 us -> none  [the longest x1 6.59 us: body(): item_part = jnp.sum(widened_entries, axis=0)]
    ppermute x0 -> x4, starting transfers between devices: none -> 7.69 us  [add_over(): x = x + lax.ppermute(x, axis, pairs)]
    convert_element_type x1 -> x0, other arithmetic: 7.24 us -> none  [predictor_function(): scaled = (values / root_mean).astype(jnp.bfloat16)]
  transfers between devices with their start and end apart: 1 -> 6, of which waited for: 0 -> 6; matrix products, arithmetic and copies ran while one was open for 15% -> 1% of each run, Pallas kernels for 0% -> 1%
where the time goes in v2:
time: 76.6 us; the launch traced here: 76.2 us
  starting transfers between devices  23.9 us (31%)
  Pallas kernels  18.1 us (24%)
  blocking collectives  16.6 us (22%)
  waiting for transfers between devices  13.4 us (17%)
  local copies, waits for them, and re-layouts  2.6 us (3%)
  other arithmetic  0.83 us (1%)
    all_to_all x1, blocking collectives, exchange(): return lax.all_to_all(x, axis, 0, 0, tiled=True)  16.6 us
    all_to_all x2, starting transfers between devices, exchange(): return lax.all_to_all(x, axis, 0, 0, tiled=True)  16.2 us
    pallas_call x1, Pallas kernels, bottom(): pl.pallas_call(functools.partial(bottom_kernel, chunk, part), grid=(store...  14.4 us
    ppermute x4, starting transfers between devices, add_over(): x = x + lax.ppermute(x, axis, pairs)  7.69 us
    ppermute x4, waiting for transfers between devices, add_over(): x = x + lax.ppermute(x, axis, pairs)  7.16 us
    all_to_all x2, waiting for transfers between devices, exchange(): return lax.all_to_all(x, axis, 0, 0, tiled=True)  6.2 us
    unnamed x10, local copies, waits for them, and re-layouts  2.6 us
  transfers between devices with their start and end apart: 6, of which 6 were waited for; matrix products, arithmetic and copies ran while one was open for 1% of the time, Pallas kernels for 1%

profile of v2, /device:TPU:1, one launch (start us, length us, event | category | flops | bytes accessed | tf_op | source)
XLA Modules:
  0.0 76.2 jit_solution(11883089827208592367)
XLA Ops:
  0.6 0.0 copy-start.1
  0.6 0.0 copy-start.2
  0.7 0.0 copy-start.3
  0.7 14.4 %bottom.1 = (f32[16,72,128]{2,1,0:T(8,128)}, f32[24,512]{1,0:T(8,128)}, f32[24,128]{1,0:T(8,128)}, f32[6144,128]{1,0:T(8,128)}) custom-call(bf16[256,24,512]{2,1,0:T(8,128)(2,1)} %h_ref.1, bf16[512,512]{1,0:T(8,128)(2,1)} %w1_ref.3, bf16[512,512]{1,0:T(8,128)(2,1)} %w2_ref.3, bf16[28,512]{1,0:T(8,128)(2,1)} %bitcast.3), custom_call_target="tpu_custom_call" | custom-call | flops 7247757312 | bytes 9437184 | tf_op jit(solution)/shard_map/bottom/pallas_call | solution.py:92
  15.1 10.1 %all-to-all-start = ((f32[16,72,128]{2,1,0:T(8,128)}), f32[16,72,128]{2,1,0:T(8,128)S(1)}, u32[]{:S(2)}, u32[]{:S(2)}) async-start(f32[16,72,128]{2,1,0:T(8,128)} %get-tuple-element.14), calls=%async_computation | async-start | bytes 1179648 | tf_op jit(solution)/shard_map/all_to_all | solution.py:296
  25.1 1.0 %collective-permute-start = (f32[24,512]{1,0:T(8,128)}, f32[24,512]{1,0:T(8,128)S(1)}, u32[]{:S(2)}, u32[]{:S(2)}) collective-permute-start(f32[24,512]{1,0:T(8,128)} %get-tuple-element.15), channel_id=1, source_target_pairs={{0,16},{16,0},{32,48},{48,32},{64,80},{80,64},{96,112},{112,96},{1... | collective-permute-start | bytes 147464 | tf_op jit(solution)/shard_map/ppermute | solution.py:302
  26.2 1.1 %collective-permute-done = f32[24,512]{1,0:T(8,128)S(1)} collective-permute-done((f32[24,512]{1,0:T(8,128)}, f32[24,512]{1,0:T(8,128)S(1)}, u32[]{:S(2)}, u32[]{:S(2)}) %collective-permute-start) | collective-permute-done | bytes 49184 | tf_op jit(solution)/shard_map/ppermute | solution.py:302
  27.3 0.8 %add.12 = f32[24,512]{1,0:T(8,128)S(1)} add(f32[24,512]{1,0:T(8,128)} %get-tuple-element.15, f32[24,512]{1,0:T(8,128)S(1)} %collective-permute-done) | non-fusion elementwise | flops 12288 | bytes 147456 | tf_op jit(solution)/shard_map/add | solution.py:302
  28.1 2.5 %collective-permute-start.1 = (f32[24,512]{1,0:T(8,128)S(1)}, f32[24,512]{1,0:T(8,128)S(1)}, u32[]{:S(2)}, u32[]{:S(2)}) collective-permute-start(f32[24,512]{1,0:T(8,128)S(1)} %add.12), channel_id=1, source_target_pairs={{0,32},{16,48},{32,0},{48,16},{64,96},{80,112},{96,64},{112,80},{1... | collective-permute-start | bytes 147464 | tf_op jit(solution)/shard_map/ppermute | solution.py:302
  30.5 2.4 %collective-permute-done.1 = f32[24,512]{1,0:T(8,128)S(1)} collective-permute-done((f32[24,512]{1,0:T(8,128)S(1)}, f32[24,512]{1,0:T(8,128)S(1)}, u32[]{:S(2)}, u32[]{:S(2)}) %collective-permute-start.1) | collective-permute-done | bytes 49184 | tf_op jit(solution)/shard_map/ppermute | solution.py:302
  32.9 1.4 %collective-permute-start.2 = (f32[24,512]{1,0:T(8,128)S(1)}, f32[24,512]{1,0:T(8,128)S(1)}, u32[]{:S(2)}, u32[]{:S(2)}) collective-permute-start(f32[24,512]{1,0:T(8,128)S(1)} %add.13), channel_id=1, source_target_pairs={{0,64},{16,80},{32,96},{48,112},{64,0},{80,16},{96,32},{112,48},{1... | collective-permute-start | bytes 147464 | tf_op jit(solution)/shard_map/ppermute | solution.py:302
  34.3 1.9 %collective-permute-done.2 = f32[24,512]{1,0:T(8,128)S(1)} collective-permute-done((f32[24,512]{1,0:T(8,128)S(1)}, f32[24,512]{1,0:T(8,128)S(1)}, u32[]{:S(2)}, u32[]{:S(2)}) %collective-permute-start.2) | collective-permute-done | bytes 49184 | tf_op jit(solution)/shard_map/ppermute | solution.py:302
  36.2 2.8 %collective-permute-start.3 = (f32[24,512]{1,0:T(8,128)S(1)}, f32[24,512]{1,0:T(8,128)S(1)}, u32[]{:S(2)}, u32[]{:S(2)}) collective-permute-start(f32[24,512]{1,0:T(8,128)S(1)} %add.14), channel_id=1, source_target_pairs={{0,192},{16,208},{32,224},{48,240},{64,128},{80,144},{96,160},{112... | collective-permute-start | bytes 147464 | tf_op jit(solution)/shard_map/ppermute | solution.py:302
  39.0 1.8 %collective-permute-done.3 = f32[24,512]{1,0:T(8,128)S(1)} collective-permute-done((f32[24,512]{1,0:T(8,128)S(1)}, f32[24,512]{1,0:T(8,128)S(1)}, u32[]{:S(2)}, u32[]{:S(2)}) %collective-permute-start.3) | collective-permute-done | bytes 49184 | tf_op jit(solution)/shard_map/ppermute | solution.py:302
  40.8 1.2 %all-to-all-done.s_ref = f32[16,72,128]{2,1,0:T(8,128)S(1)} async-done(((f32[16,72,128]{2,1,0:T(8,128)}), f32[16,72,128]{2,1,0:T(8,128)S(1)}, u32[]{:S(2)}, u32[]{:S(2)}) %all-to-all-start) | async-done | bytes 589856 | tf_op jit(solution)/shard_map/all_to_all | solution.py:296
  42.1 0.0 copy-done.1
  42.1 0.0 copy-done.2
  42.1 0.0 copy-done.3
  42.1 0.0 copy-start.4
  42.1 0.7 copy-done.4
  42.8 0.6 totals.1
  43.4 16.6 %all_to_all.15.got_ref.one_ref = f32[16,8,128]{2,1,0:T(8,128)S(1)} all-to-all(f32[16,8,128]{2,1,0:T(8,128)S(1)} %get-tuple-element.18), channel_id=1, replica_groups=mesh['store'=16,'dept'=16] {'store'}, dimensions={0} | all-to-all | bytes 131072 | tf_op jit(solution)/shard_map/all_to_all | solution.py:296
  60.1 0.7 middle.1
  60.7 6.2 %all-to-all-start.2 = ((f32[16,8,128]{2,1,0:T(8,128)}), f32[16,8,128]{2,1,0:T(8,128)S(1)}, u32[]{:S(2)}, u32[]{:S(2)}) async-start(f32[16,8,128]{2,1,0:T(8,128)} %middle.1), calls=%async_computation.2 | async-start | bytes 131072 | tf_op jit(solution)/shard_map/all_to_all | solution.py:296
  66.9 0.0 copy-start
  66.9 1.9 %copy-done = f32[6144,128]{1,0:T(8,128)S(1)} copy-done((f32[6144,128]{1,0:T(8,128)S(1)}, f32[6144,128]{1,0:T(8,128)}, u32[]{:S(2)}) %copy-start) | copy-done | bytes 3145752
  68.8 1.0 %arrange.1.base_ref = f32[672,256]{1,0:T(8,128)S(1)} custom-call(f32[6144,128]{1,0:T(8,128)S(1)} %copy-done), custom_call_target="tpu_custom_call" | custom-call | flops 3145728 | bytes 3145728 | tf_op jit(solution)/shard_map/arrange/pallas_call | solution.py:149
  69.8 5.0 %all-to-all-done.2.two_ref = f32[16,8,128]{2,1,0:T(8,128)S(1)} async-done(((f32[16,8,128]{2,1,0:T(8,128)}), f32[16,8,128]{2,1,0:T(8,128)S(1)}, u32[]{:S(2)}, u32[]{:S(2)}) %all-to-all-start.2) | async-done | bytes 65568 | tf_op jit(solution)/shard_map/all_to_all | solution.py:296
  74.8 1.4 %final.1 = (f32[672,256]{1,0:T(8,128)}, f32[28,256]{1,0:T(8,128)}, f32[24,28]{1,0:T(8,128)}) custom-call(f32[672,256]{1,0:T(8,128)S(1)} %arrange.1.base_ref, f32[24,128]{1,0:T(8,128)S(1)} %get-tuple-element.17.item_ref, f32[16,8,128]{2,1,0:T(8,128)S(1)} %all_to_all.15.got_ref.one_ref, f32[16,8,128]{2,1,0:T(8,128)S(1)} %all-to-all-done.2.two_ref), custom_call_target="tpu_custom_call" | custom-call | tf_op jit(solution)/shard_map/final/pallas_call | solution.py:280
  (3 shorter events, 0.0 us)
Async XLA Ops:
  0.6 41.4 %copy-start.1 = (bf16[512,512]{1,0:T(8,128)(2,1)S(1)}, bf16[512,512]{1,0:T(8,128)(2,1)}, u32[]{:S(2)}) copy-start(bf16[512,512]{1,0:T(8,128)(2,1)} %w1_ref.3) | copy-start | bytes 1572868
  0.6 41.4 %copy-start.2 = (bf16[512,512]{1,0:T(8,128)(2,1)S(1)}, bf16[512,512]{1,0:T(8,128)(2,1)}, u32[]{:S(2)}) copy-start(bf16[512,512]{1,0:T(8,128)(2,1)} %w2_ref.3) | copy-start | bytes 1572868
  0.7 41.4 %copy-start.3 = (bf16[512,28]{0,1:T(8,128)(2,1)S(1)}, bf16[512,28]{0,1:T(8,128)(2,1)}, u32[]{:S(2)}) copy-start(bf16[512,28]{0,1:T(8,128)(2,1)} %param.7) | copy-start | bytes 86020
  15.1 27.0 %all-to-all-start = ((f32[16,72,128]{2,1,0:T(8,128)}), f32[16,72,128]{2,1,0:T(8,128)S(1)}, u32[]{:S(2)}, u32[]{:S(2)}) async-start(f32[16,72,128]{2,1,0:T(8,128)} %get-tuple-element.14), calls=%async_computation | async-start | bytes 1179648 | tf_op jit(solution)/shard_map/all_to_all | solution.py:296
  25.1 2.1 %collective-permute-start = (f32[24,512]{1,0:T(8,128)}, f32[24,512]{1,0:T(8,128)S(1)}, u32[]{:S(2)}, u32[]{:S(2)}) collective-permute-start(f32[24,512]{1,0:T(8,128)} %get-tuple-element.15), channel_id=1, source_target_pairs={{0,16},{16,0},{32,48},{48,32},{64,80},{80,64},{96,112},{112,96},{1... | collective-permute-start | bytes 147464 | tf_op jit(solution)/shard_map/ppermute | solution.py:302
  28.1 4.8 %collective-permute-start.1 = (f32[24,512]{1,0:T(8,128)S(1)}, f32[24,512]{1,0:T(8,128)S(1)}, u32[]{:S(2)}, u32[]{:S(2)}) collective-permute-start(f32[24,512]{1,0:T(8,128)S(1)} %add.12), channel_id=1, source_target_pairs={{0,32},{16,48},{32,0},{48,16},{64,96},{80,112},{96,64},{112,80},{1... | collective-permute-start | bytes 147464 | tf_op jit(solution)/shard_map/ppermute | solution.py:302
  32.9 3.3 %collective-permute-start.2 = (f32[24,512]{1,0:T(8,128)S(1)}, f32[24,512]{1,0:T(8,128)S(1)}, u32[]{:S(2)}, u32[]{:S(2)}) collective-permute-start(f32[24,512]{1,0:T(8,128)S(1)} %add.13), channel_id=1, source_target_pairs={{0,64},{16,80},{32,96},{48,112},{64,0},{80,16},{96,32},{112,48},{1... | collective-permute-start | bytes 147464 | tf_op jit(solution)/shard_map/ppermute | solution.py:302
  36.2 4.6 %collective-permute-start.3 = (f32[24,512]{1,0:T(8,128)S(1)}, f32[24,512]{1,0:T(8,128)S(1)}, u32[]{:S(2)}, u32[]{:S(2)}) collective-permute-start(f32[24,512]{1,0:T(8,128)S(1)} %add.14), channel_id=1, source_target_pairs={{0,192},{16,208},{32,224},{48,240},{64,128},{80,144},{96,160},{112... | collective-permute-start | bytes 147464 | tf_op jit(solution)/shard_map/ppermute | solution.py:302
  42.1 0.7 copy-start.4
  60.7 14.1 %all-to-all-start.2 = ((f32[16,8,128]{2,1,0:T(8,128)}), f32[16,8,128]{2,1,0:T(8,128)S(1)}, u32[]{:S(2)}, u32[]{:S(2)}) async-start(f32[16,8,128]{2,1,0:T(8,128)} %middle.1), calls=%async_computation.2 | async-start | bytes 131072 | tf_op jit(solution)/shard_map/all_to_all | solution.py:296
  66.9 1.9 %copy-start = (f32[6144,128]{1,0:T(8,128)S(1)}, f32[6144,128]{1,0:T(8,128)}, u32[]{:S(2)}) copy-start(f32[6144,128]{1,0:T(8,128)} %get-tuple-element.13.y_ref) | copy-start | bytes 9437188

commit v3 on v2

--- a/solution.py
+++ b/solution.py
@@ -12,15 +12,19 @@
 BF16 = jnp.bfloat16
 LANES = 128
 GROUP = 32
-VMEM_LIMIT = 50 * 1024 * 1024
+MIB = 1024 * 1024
 
 
 def whole(n):
     return [pl.BlockSpec(memory_space=pltpu.VMEM)] * n
 
 
-def params(semantics=None, limit=VMEM_LIMIT):
-    return pltpu.CompilerParams(dimension_semantics=semantics, vmem_limit_bytes=limit)
+def params(mib):
+    return pltpu.CompilerParams(vmem_limit_bytes=mib * MIB)
+
+
+def stay(x):
+    return pltpu.with_memory_space_constraint(x, pltpu.HBM)
 
 
 def relu(x):
@@ -108,17 +112,17 @@
             jax.ShapeDtypeStruct((peers, pay_rows, LANES), F32),
             jax.ShapeDtypeStruct((items, days), F32),
             jax.ShapeDtypeStruct((items, LANES), F32),
-            jax.ShapeDtypeStruct((rows, LANES), F32),
+            pltpu.HBM((rows, LANES), F32),
         ],
         scratch_shapes=[pltpu.VMEM((hid, LANES), BF16)],
-        compiler_params=params(("arbitrary",), 58 * 1024 * 1024),
+        compiler_params=params(24),
         cost_estimate=pl.CostEstimate(
             flops=2 * rows * (days * hid + hid * hid + hid * LANES),
             bytes_accessed=2 * history.size + 4 * rows * LANES,
             transcendentals=0,
         ),
         name="bottom",
-    )(history, w1, w2, w3)
+    )(stay(history), stay(w1), stay(w2), stay(w3))
 
 
 def arrange_kernel(horizon, items, y_ref, out_ref):
@@ -151,7 +155,7 @@
         in_specs=whole(1),
         out_specs=whole(1)[0],
         out_shape=jax.ShapeDtypeStruct((items * horizon, rows // items), F32),
-        compiler_params=params(),
+        compiler_params=params(12),
         cost_estimate=pl.CostEstimate(
             flops=rows * LANES * 4, bytes_accessed=rows * LANES * 4, transcendentals=0
         ),
@@ -198,7 +202,7 @@
             jax.ShapeDtypeStruct((item_peers, 8, LANES), F32),
         ],
         scratch_shapes=[pltpu.VMEM((w1.shape[1], LANES), BF16)],
-        compiler_params=params(),
+        compiler_params=params(8),
         name="totals",
     )(store_parts, item_hist, w1, w2, w3, col)
 
@@ -220,7 +224,7 @@
         in_specs=whole(2),
         out_specs=whole(1)[0],
         out_shape=jax.ShapeDtypeStruct((peers, 8, LANES), F32),
-        compiler_params=params(),
+        compiler_params=params(2),
         name="middle",
     )(err, got)
 
@@ -287,7 +291,7 @@
             jax.ShapeDtypeStruct((items, horizon), F32),
         ],
         scratch_shapes=[pltpu.VMEM((stores, LANES), F32)],
-        compiler_params=params(),
+        compiler_params=params(6),
         name="final",
     )(base, item_fc, one, two)
 
@@ -296,11 +300,15 @@
     return lax.all_to_all(x, axis, 0, 0, tiled=True)
 
 
-def add_over(x, axis, flips):
-    for flip in flips:
-        pairs = [(i, i ^ flip) for i in range(lax.axis_size(axis))]
-        x = x + lax.ppermute(x, axis, pairs)
-    return x
+def partner(x, axis, flip):
+    return lax.ppermute(x, axis, [(i, i ^ flip) for i in range(lax.axis_size(axis))])
+
+
+def add_over_stores(x):
+    x = x + partner(x, "store", 1)
+    x = x + partner(x, "store", 2)
+    near, far, across = (partner(x, "store", flip) for flip in (4, 12, 8))
+    return (x + across) + (near + far)
 
 
 def body(history, w1, w2, final_layer_matrix):
@@ -312,8 +320,8 @@
 
     pay, item_part, col, y = bottom(history, w1, w2, w3, n_dept, 64, 32)
     store_parts = exchange(pay, "dept")
-    item_hist = add_over(item_part, "store", (1, 2, 4, 12))
-    base = arrange(y, items, horizon)
+    item_hist = add_over_stores(item_part)
+    base, item_hist = lax.optimization_barrier((arrange(stay(y), items, horizon), item_hist))
     err, item_fc, pay_one = totals(store_parts, item_hist, w1, w2, w3, col, chunk, n_store)
     one = exchange(pay_one, "store")
     pay_two = middle(err, one, chunk, items, n_dept)

time: 76.6 us -> 71.8 us (0.937)
  blocking collectives: 16.6 us -> 27.5 us
  waiting for transfers between devices: 13.4 us -> 5.95 us
  starting transfers between devices: 23.9 us -> 18 us
  local copies, waits for them, and re-layouts: 2.6 us -> 0.01 us
  Pallas kernels: 18.1 us -> 19.4 us
  other arithmetic: 0.83 us -> 0.03 us
    all_to_all x1 -> x2, blocking collectives: 16.6 us -> 27.5 us  [exchange(): return lax.all_to_all(x, axis, 0, 0, tiled=True)]
    all_to_all x2 -> x1, starting transfers between devices: 16.2 us -> 10 us  [exchange(): return lax.all_to_all(x, axis, 0, 0, tiled=True)]
    all_to_all x2 -> x1, waiting for transfers between devices: 6.2 us -> 2.25 us  [exchange(): return lax.all_to_all(x, axis, 0, 0, tiled=True)]
    ppermute x4 -> x5, waiting for transfers between devices: 7.16 us -> 3.7 us  [partner(): lax.ppermute(x, axis, [(i, i ^ flip) for i in range(lax.axis_size(axis))])]
    unnamed x10 -> x6, local copies, waits for them, and re-layouts: 2.6 us -> 0.01 us
    pallas_call x1, Pallas kernels: 1.05 us -> 2.93 us  [arrange(): pl.pallas_call(functools.partial(arrange_kernel, horizon, items), in_spec...]
    add x4 -> x3, other arithmetic: 0.83 us -> 0.03 us  [the longest x1 0.02 us: add_over_stores(): return x + across + (near + far)]
    ppermute x4 -> x5, starting transfers between devices: 7.69 us -> 7.97 us  [partner(): lax.ppermute(x, axis, [(i, i ^ flip) for i in range(lax.axis_size(axis))])]
  transfers between devices with their start and end apart: 6 -> 6, of which waited for: 6 -> 4; matrix products, arithmetic and copies ran while one was open for 1% -> 0% of each run, Pallas kernels for 1% -> 4%
where the time goes in v3:
time: 71.8 us; the launch traced here: 71.5 us
  blocking collectives  27.5 us (38%)
  Pallas kernels  19.4 us (27%)
  starting transfers between devices  18 us (25%)
  waiting for transfers between devices  5.95 us (8%)
    all_to_all x2, blocking collectives, exchange(): return lax.all_to_all(x, axis, 0, 0, tiled=True)  27.5 us
    pallas_call x1, Pallas kernels, bottom(): pl.pallas_call(functools.partial(bottom_kernel, chunk, part), grid=(store...  14.4 us
    all_to_all x1, starting transfers between devices, exchange(): return lax.all_to_all(x, axis, 0, 0, tiled=True)  10 us
    ppermute x5, starting transfers between devices, partner(): lax.ppermute(x, axis, [(i, i ^ flip) for i in range(lax.axis_size(axis))])  7.97 us
    ppermute x5, waiting for transfers between devices, partner(): lax.ppermute(x, axis, [(i, i ^ flip) for i in range(lax.axis_size(axis))])  3.7 us
    pallas_call x1, Pallas kernels, arrange(): pl.pallas_call(functools.partial(arrange_kernel, horizon, items), in_spec...  2.93 us
    all_to_all x1, waiting for transfers between devices, exchange(): return lax.all_to_all(x, axis, 0, 0, tiled=True)  2.25 us
  transfers between devices with their start and end apart: 6, of which 4 were waited for; matrix products, arithmetic and copies ran while one was open for 0% of the time, Pallas kernels for 4%

profile of v3, /device:TPU:1, one launch (start us, length us, event | category | flops | bytes accessed | tf_op | source)
XLA Modules:
  0.0 71.5 jit_solution(3968842570525901707)
XLA Ops:
  0.6 0.0 copy-start
  0.6 0.0 copy-start.1
  0.7 0.0 copy-start.2
  0.7 14.4 %bottom.1 = (f32[16,72,128]{2,1,0:T(8,128)}, f32[24,512]{1,0:T(8,128)S(1)}, f32[24,128]{1,0:T(8,128)S(1)}, f32[6144,128]{1,0:T(8,128)}) custom-call(bf16[256,24,512]{2,1,0:T(8,128)(2,1)} %h_ref.1, bf16[512,512]{1,0:T(8,128)(2,1)} %w1_ref.3, bf16[512,512]{1,0:T(8,128)(2,1)} %w2_ref.3, bf16[28,512]{1,0:T(8,128)(2,1)} %bitcast.3), custom_call_target="tpu_custom_call" | custom-call | flops 7247757312 | bytes 9437184 | tf_op jit(solution)/shard_map/bottom/pallas_call | solution.py:96
  15.1 10.0 %all-to-all-start = ((f32[16,72,128]{2,1,0:T(8,128)}), f32[16,72,128]{2,1,0:T(8,128)S(1)}, u32[]{:S(2)}, u32[]{:S(2)}) async-start(f32[16,72,128]{2,1,0:T(8,128)} %get-tuple-element.18), calls=%async_computation | async-start | bytes 1179648 | tf_op jit(solution)/shard_map/all_to_all | solution.py:300
  25.1 1.0 %collective-permute-start = (f32[24,512]{1,0:T(8,128)S(1)}, f32[24,512]{1,0:T(8,128)S(1)}, u32[]{:S(2)}, u32[]{:S(2)}) collective-permute-start(f32[24,512]{1,0:T(8,128)S(1)} %get-tuple-element.16), channel_id=1, source_target_pairs={{0,16},{16,0},{32,48},{48,32},{64,80},{80,64},{96,112},{112,96},{1... | collective-permute-start | bytes 147464 | tf_op jit(solution)/shard_map/ppermute | solution.py:304
  26.2 0.9 %collective-permute-done = f32[24,512]{1,0:T(8,128)S(1)} collective-permute-done((f32[24,512]{1,0:T(8,128)S(1)}, f32[24,512]{1,0:T(8,128)S(1)}, u32[]{:S(2)}, u32[]{:S(2)}) %collective-permute-start) | collective-permute-done | bytes 49184 | tf_op jit(solution)/shard_map/ppermute | solution.py:304
  27.1 2.5 %collective-permute-start.1 = (f32[24,512]{1,0:T(8,128)S(1)}, f32[24,512]{1,0:T(8,128)S(1)}, u32[]{:S(2)}, u32[]{:S(2)}) collective-permute-start(f32[24,512]{1,0:T(8,128)S(1)} %add.15), channel_id=1, source_target_pairs={{0,32},{16,48},{32,0},{48,16},{64,96},{80,112},{96,64},{112,80},{1... | collective-permute-start | bytes 147464 | tf_op jit(solution)/shard_map/ppermute | solution.py:304
  29.6 2.0 %collective-permute-done.1 = f32[24,512]{1,0:T(8,128)S(1)} collective-permute-done((f32[24,512]{1,0:T(8,128)S(1)}, f32[24,512]{1,0:T(8,128)S(1)}, u32[]{:S(2)}, u32[]{:S(2)}) %collective-permute-start.1) | collective-permute-done | bytes 49184 | tf_op jit(solution)/shard_map/ppermute | solution.py:304
  31.6 3.1 %collective-permute-start.4 = (f32[24,512]{1,0:T(8,128)S(1)}, f32[24,512]{1,0:T(8,128)S(1)}, u32[]{:S(2)}, u32[]{:S(2)}) collective-permute-start(f32[24,512]{1,0:T(8,128)S(1)} %add.16), channel_id=1, source_target_pairs={{0,192},{16,208},{32,224},{48,240},{64,128},{80,144},{96,160},{112... | collective-permute-start | bytes 147464 | tf_op jit(solution)/shard_map/ppermute | solution.py:304
  34.7 0.0 collective-permute-start.3
  34.7 1.3 %collective-permute-start.2 = (f32[24,512]{1,0:T(8,128)S(1)}, f32[24,512]{1,0:T(8,128)S(1)}, u32[]{:S(2)}, u32[]{:S(2)}) collective-permute-start(f32[24,512]{1,0:T(8,128)S(1)} %add.16), channel_id=1, source_target_pairs={{0,128},{16,144},{32,160},{48,176},{64,192},{80,208},{96,224},{112... | collective-permute-start | bytes 147464 | tf_op jit(solution)/shard_map/ppermute | solution.py:304
  36.0 2.9 %arrange.1.base_ref = f32[672,256]{1,0:T(8,128)S(1)} custom-call(f32[6144,128]{1,0:T(8,128)} %get-tuple-element.15.y_ref), custom_call_target="tpu_custom_call" | custom-call | flops 3145728 | bytes 3145728 | tf_op jit(solution)/shard_map/arrange/pallas_call | solution.py:153
  38.9 0.0 collective-permute-done.4
  39.0 0.0 collective-permute-done.3
  39.0 0.8 %collective-permute-done.2 = f32[24,512]{1,0:T(8,128)S(1)} collective-permute-done((f32[24,512]{1,0:T(8,128)S(1)}, f32[24,512]{1,0:T(8,128)S(1)}, u32[]{:S(2)}, u32[]{:S(2)}) %collective-permute-start.2) | collective-permute-done | bytes 49184 | tf_op jit(solution)/shard_map/ppermute | solution.py:304
  39.8 2.2 %all-to-all-done.s_ref = f32[16,72,128]{2,1,0:T(8,128)S(1)} async-done(((f32[16,72,128]{2,1,0:T(8,128)}), f32[16,72,128]{2,1,0:T(8,128)S(1)}, u32[]{:S(2)}, u32[]{:S(2)}) %all-to-all-start) | async-done | bytes 589856 | tf_op jit(solution)/shard_map/all_to_all | solution.py:300
  42.0 0.0 copy-done
  42.0 0.0 copy-done.1
  42.0 0.0 copy-done.2
  42.0 0.6 totals.1
  42.7 16.6 %all_to_all.15.got_ref.one_ref = f32[16,8,128]{2,1,0:T(8,128)S(1)} all-to-all(f32[16,8,128]{2,1,0:T(8,128)S(1)} %get-tuple-element.22), channel_id=1, replica_groups=mesh['store'=16,'dept'=16] {'store'}, dimensions={0} | all-to-all | bytes 131072 | tf_op jit(solution)/shard_map/all_to_all | solution.py:300
  59.3 10.9 %all_to_all.16.two_ref = f32[16,8,128]{2,1,0:T(8,128)S(1)} all-to-all(f32[16,8,128]{2,1,0:T(8,128)S(1)} %middle.1), channel_id=1, replica_groups=mesh['store'=16,'dept'=16] {'dept'}, dimensions={0} | all-to-all | bytes 131072 | tf_op jit(solution)/shard_map/all_to_all | solution.py:300
  70.2 1.4 %final.1 = (f32[672,256]{1,0:T(8,128)}, f32[28,256]{1,0:T(8,128)}, f32[24,28]{1,0:T(8,128)}) custom-call(f32[672,256]{1,0:T(8,128)S(1)} %arrange.1.base_ref, f32[24,128]{1,0:T(8,128)S(1)} %get-tuple-element.21.item_ref, f32[16,8,128]{2,1,0:T(8,128)S(1)} %all_to_all.15.got_ref.one_ref, f32[16,8,128]{2,1,0:T(8,128)S(1)} %all_to_all.16.two_ref), custom_call_target="tpu_custom_call" | custom-call | tf_op jit(solution)/shard_map/final/pallas_call | solution.py:284
  (4 shorter events, 0.1 us)
Async XLA Ops:
  0.6 41.4 %copy-start = (bf16[512,512]{1,0:T(8,128)(2,1)S(1)}, bf16[512,512]{1,0:T(8,128)(2,1)}, u32[]{:S(2)}) copy-start(bf16[512,512]{1,0:T(8,128)(2,1)} %w1_ref.3) | copy-start | bytes 1572868
  0.6 41.4 %copy-start.1 = (bf16[512,512]{1,0:T(8,128)(2,1)S(1)}, bf16[512,512]{1,0:T(8,128)(2,1)}, u32[]{:S(2)}) copy-start(bf16[512,512]{1,0:T(8,128)(2,1)} %w2_ref.3) | copy-start | bytes 1572868
  0.7 41.4 %copy-start.2 = (bf16[512,28]{0,1:T(8,128)(2,1)S(1)}, bf16[512,28]{0,1:T(8,128)(2,1)}, u32[]{:S(2)}) copy-start(bf16[512,28]{0,1:T(8,128)(2,1)} %param.7) | copy-start | bytes 86020
  15.1 27.0 %all-to-all-start = ((f32[16,72,128]{2,1,0:T(8,128)}), f32[16,72,128]{2,1,0:T(8,128)S(1)}, u32[]{:S(2)}, u32[]{:S(2)}) async-start(f32[16,72,128]{2,1,0:T(8,128)} %get-tuple-element.18), calls=%async_computation | async-start | bytes 1179648 | tf_op jit(solution)/shard_map/all_to_all | solution.py:300
  25.1 1.9 %collective-permute-start = (f32[24,512]{1,0:T(8,128)S(1)}, f32[24,512]{1,0:T(8,128)S(1)}, u32[]{:S(2)}, u32[]{:S(2)}) collective-permute-start(f32[24,512]{1,0:T(8,128)S(1)} %get-tuple-element.16), channel_id=1, source_target_pairs={{0,16},{16,0},{32,48},{48,32},{64,80},{80,64},{96,112},{112,96},{1... | collective-permute-start | bytes 147464 | tf_op jit(solution)/shard_map/ppermute | solution.py:304
  27.1 4.5 %collective-permute-start.1 = (f32[24,512]{1,0:T(8,128)S(1)}, f32[24,512]{1,0:T(8,128)S(1)}, u32[]{:S(2)}, u32[]{:S(2)}) collective-permute-start(f32[24,512]{1,0:T(8,128)S(1)} %add.15), channel_id=1, source_target_pairs={{0,32},{16,48},{32,0},{48,16},{64,96},{80,112},{96,64},{112,80},{1... | collective-permute-start | bytes 147464 | tf_op jit(solution)/shard_map/ppermute | solution.py:304
  31.6 7.4 %collective-permute-start.4 = (f32[24,512]{1,0:T(8,128)S(1)}, f32[24,512]{1,0:T(8,128)S(1)}, u32[]{:S(2)}, u32[]{:S(2)}) collective-permute-start(f32[24,512]{1,0:T(8,128)S(1)} %add.16), channel_id=1, source_target_pairs={{0,192},{16,208},{32,224},{48,240},{64,128},{80,144},{96,160},{112... | collective-permute-start | bytes 147464 | tf_op jit(solution)/shard_map/ppermute | solution.py:304
  34.7 4.2 %collective-permute-start.3 = (f32[24,512]{1,0:T(8,128)S(1)}, f32[24,512]{1,0:T(8,128)S(1)}, u32[]{:S(2)}, u32[]{:S(2)}) collective-permute-start(f32[24,512]{1,0:T(8,128)S(1)} %add.16), channel_id=1, source_target_pairs={{0,64},{16,80},{32,96},{48,112},{64,0},{80,16},{96,32},{112,48},{1... | collective-permute-start | bytes 147464 | tf_op jit(solution)/shard_map/ppermute | solution.py:304
  34.7 5.0 %collective-permute-start.2 = (f32[24,512]{1,0:T(8,128)S(1)}, f32[24,512]{1,0:T(8,128)S(1)}, u32[]{:S(2)}, u32[]{:S(2)}) collective-permute-start(f32[24,512]{1,0:T(8,128)S(1)} %add.16), channel_id=1, source_target_pairs={{0,128},{16,144},{32,160},{48,176},{64,192},{80,208},{96,224},{112... | collective-permute-start | bytes 147464 | tf_op jit(solution)/shard_map/ppermute | solution.py:304

commit v4 on v3

--- a/solution.py
+++ b/solution.py
@@ -54,9 +54,10 @@
     return out
 
 
-def bottom_kernel(chunk, part, h_ref, w1_ref, w2_ref, w3_ref, pay_ref, item_ref, col_ref, y_ref, w3_wide):
+def early_kernel(chunk, part, late, h_ref, w1_ref, w2_ref, w3_ref, pay_ref, item_ref, col_ref, y_ref, w3_wide):
     block, items, days = h_ref.shape
     step = pl.program_id(0)
+    tiles = days // LANES
 
     @pl.when(step == 0)
     def _():
@@ -64,49 +65,62 @@
         item_ref[...] = jnp.zeros_like(item_ref)
         col_ref[...] = jnp.zeros_like(col_ref)
 
-    w1, w2, w3 = w1_ref[...], w2_ref[...], w3_wide[...]
-    tiles = days // LANES
-    for p in range(block // part):
+    def sums(p):
         x = h_ref[p * part : (p + 1) * part].astype(F32)
         by_store = jnp.sum(x, axis=1)
         item_ref[...] += jnp.sum(x, axis=0)
-        y = forecaster(x.reshape(part * items, days), w1, w2, w3)
-        y_ref[p * part * items : (p + 1) * part * items, :] = y
-        y = y.reshape(part, items, LANES)
-        row = jnp.sum(y, axis=1)
-        col_ref[...] += jnp.sum(y, axis=0)
         for q in range(part // chunk):
-            peer = p * (part // chunk) + q
             for t in range(tiles):
-                pay_ref[peer, t * chunk : (t + 1) * chunk, :] = by_store[
+                pay_ref[p * (part // chunk) + q, t * chunk : (t + 1) * chunk, :] = by_store[
                     q * chunk : (q + 1) * chunk, t * LANES : (t + 1) * LANES
                 ]
-            pay_ref[peer, tiles * chunk : tiles * chunk + chunk // 4, :] = pack_rows(
-                row[q * chunk : (q + 1) * chunk]
-            )
-
-
-def bottom(history, w1, w2, w3, peers, block, part):
+        return x
+
+    @pl.when(step < late)
+    def _():
+        for p in range(block // part):
+            sums(p)
+        pay_ref[:, tiles * chunk :, :] = jnp.zeros((block // chunk, 8, LANES), F32)
+
+    @pl.when(step >= late)
+    def _():
+        w1, w2, w3 = w1_ref[...], w2_ref[...], w3_wide[...]
+        for p in range(block // part):
+            x = sums(p)
+            y = forecaster(x.reshape(part * items, days), w1, w2, w3)
+            y_ref[p * part * items : (p + 1) * part * items, :] = y
+            y = y.reshape(part, items, LANES)
+            row = jnp.sum(y, axis=1)
+            col_ref[...] += jnp.sum(y, axis=0)
+            for q in range(part // chunk):
+                pay_ref[p * (part // chunk) + q, tiles * chunk : tiles * chunk + chunk // 4, :] = (
+                    pack_rows(row[q * chunk : (q + 1) * chunk])
+                )
+
+
+def early(history, w1, w2, w3, peers, block, part, late):
     stores, items, days = history.shape
     hid = w1.shape[1]
-    rows = stores * items
+    blocks = stores // block
+    rows = (blocks - late) * block * items
     chunk = stores // peers
     pay_rows = (days // LANES) * chunk + 8
     fixed = lambda shape: pl.BlockSpec(shape, lambda i: (0,) * len(shape))
-    return pl.pallas_call(
-        functools.partial(bottom_kernel, chunk, part),
-        grid=(stores // block,),
+    turn = lambda i: lax.rem(i + blocks - late, blocks)
+    return pl.pallas_call(
+        functools.partial(early_kernel, chunk, part, late),
+        grid=(blocks,),
         in_specs=[
-            pl.BlockSpec((block, items, days), lambda i: (i, 0, 0)),
+            pl.BlockSpec((block, items, days), lambda i: (turn(i), 0, 0)),
             fixed(w1.shape),
             fixed(w2.shape),
             fixed(w3.shape),
         ],
         out_specs=[
-            pl.BlockSpec((block // chunk, pay_rows, LANES), lambda i: (i, 0, 0)),
+            pl.BlockSpec((block // chunk, pay_rows, LANES), lambda i: (turn(i), 0, 0)),
             fixed((items, days)),
             fixed((items, LANES)),
-            pl.BlockSpec((block * items, LANES), lambda i: (i, 0)),
+            pl.BlockSpec((block * items, LANES), lambda i: (jnp.maximum(i - late, 0), 0)),
         ],
         out_shape=[
             jax.ShapeDtypeStruct((peers, pay_rows, LANES), F32),
@@ -121,38 +135,97 @@
             bytes_accessed=2 * history.size + 4 * rows * LANES,
             transcendentals=0,
         ),
-        name="bottom",
+        name="early",
     )(stay(history), stay(w1), stay(w2), stay(w3))
 
 
-def arrange_kernel(horizon, items, y_ref, out_ref):
-    stores = y_ref.shape[0] // items
-    lane = lax.broadcasted_iota(jnp.int32, (stores, LANES), 1)
-    tiles = [None] * pl.cdiv(items * horizon, LANES)
-
-    def add(t, v):
-        tiles[t] = v if tiles[t] is None else tiles[t] + v
-
-    for i in range(items):
-        v = y_ref[pl.ds(i, stores, stride=items), :]
-        t, off = divmod(i * horizon, LANES)
-        if off:
-            v = pltpu.roll(v, off, axis=1)
-        if off + horizon > LANES:
-            add(t, jnp.where(lane >= off, v, 0.0))
-            add(t + 1, jnp.where(lane < off, v, 0.0))
-        else:
-            add(t, v)
-    for t, v in enumerate(tiles):
-        height = min(LANES, items * horizon - t * LANES)
-        out_ref[t * LANES : t * LANES + height, :] = v.T[:height]
-
-
-def arrange(y, items, horizon):
-    rows = y.shape[0]
+def late_kernel(part, h_ref, w1_ref, w2_ref, w3_ref, row_ref, col_ref, y_ref, w3_wide):
+    block, items, days = h_ref.shape
+
+    @pl.when(pl.program_id(0) == 0)
+    def _():
+        widen(w3_ref, w3_wide)
+        col_ref[...] = jnp.zeros_like(col_ref)
+
+    w1, w2, w3 = w1_ref[...], w2_ref[...], w3_wide[...]
+    rows = []
+    for p in range(block // part):
+        x = h_ref[p * part : (p + 1) * part].astype(F32).reshape(part * items, days)
+        y = forecaster(x, w1, w2, w3)
+        y_ref[p * part * items : (p + 1) * part * items, :] = y
+        y = y.reshape(part, items, LANES)
+        rows.append(jnp.sum(y, axis=1))
+        col_ref[...] += jnp.sum(y, axis=0)
+    row_ref[0] = pack_rows(jnp.concatenate(rows, axis=0))
+
+
+def late_forecasts(history, w1, w2, w3, block, part, late):
+    stores, items, days = history.shape
+    hid = w1.shape[1]
+    rows = late * block * items
+    skip = stores // block - late
+    fixed = lambda shape: pl.BlockSpec(shape, lambda i: (0,) * len(shape))
+    return pl.pallas_call(
+        functools.partial(late_kernel, part),
+        grid=(late,),
+        in_specs=[
+            pl.BlockSpec((block, items, days), lambda i: (i + skip, 0, 0)),
+            fixed(w1.shape),
+            fixed(w2.shape),
+            fixed(w3.shape),
+        ],
+        out_specs=[
+            pl.BlockSpec((1, block // 4, LANES), lambda i: (i, 0, 0)),
+            fixed((items, LANES)),
+            pl.BlockSpec((block * items, LANES), lambda i: (i, 0)),
+        ],
+        out_shape=[
+            jax.ShapeDtypeStruct((late, block // 4, LANES), F32),
+            jax.ShapeDtypeStruct((items, LANES), F32),
+            pltpu.HBM((rows, LANES), F32),
+        ],
+        scratch_shapes=[pltpu.VMEM((hid, LANES), BF16)],
+        compiler_params=params(24),
+        cost_estimate=pl.CostEstimate(
+            flops=2 * rows * (days * hid + hid * hid + hid * LANES),
+            bytes_accessed=2 * rows * days + 4 * rows * LANES,
+            transcendentals=0,
+        ),
+        name="late",
+    )(stay(history), w1, w2, w3)
+
+
+def arrange_kernel(horizon, items, early_ref, late_ref, out_ref):
+    first = 0
+    for y_ref in (early_ref, late_ref):
+        stores = y_ref.shape[0] // items
+        lane = lax.broadcasted_iota(jnp.int32, (stores, LANES), 1)
+        tiles = [None] * pl.cdiv(items * horizon, LANES)
+
+        def add(t, v):
+            tiles[t] = v if tiles[t] is None else tiles[t] + v
+
+        for i in range(items):
+            v = y_ref[pl.ds(i, stores, stride=items), :]
+            t, off = divmod(i * horizon, LANES)
+            if off:
+                v = pltpu.roll(v, off, axis=1)
+            if off + horizon > LANES:
+                add(t, jnp.where(lane >= off, v, 0.0))
+                add(t + 1, jnp.where(lane < off, v, 0.0))
+            else:
+                add(t, v)
+        for t, v in enumerate(tiles):
+            height = min(LANES, items * horizon - t * LANES)
+            out_ref[t * LANES : t * LANES + height, first : first + stores] = v.T[:height]
+        first += stores
+
+
+def arrange(early_y, late_y, items, horizon):
+    rows = early_y.shape[0] + late_y.shape[0]
     return pl.pallas_call(
         functools.partial(arrange_kernel, horizon, items),
-        in_specs=whole(1),
+        in_specs=whole(2),
         out_specs=whole(1)[0],
         out_shape=jax.ShapeDtypeStruct((items * horizon, rows // items), F32),
         compiler_params=params(12),
@@ -160,10 +233,10 @@
             flops=rows * LANES * 4, bytes_accessed=rows * LANES * 4, transcendentals=0
         ),
         name="arrange",
-    )(y)
-
-
-def totals_kernel(chunk, s_ref, i_ref, w1_ref, w2_ref, w3_ref, col_ref, err_ref, item_ref, pay_ref, w3_wide):
+    )(stay(early_y), stay(late_y))
+
+
+def totals_kernel(chunk, s_ref, i_ref, w1_ref, w2_ref, w3_ref, col_ref, col_late_ref, err_ref, item_ref, pay_ref, w3_wide):
     days = w1_ref.shape[0]
     widen(w3_ref, w3_wide)
     got = s_ref[0]
@@ -179,7 +252,7 @@
     q = chunk // 4
     err_ref[0:q, :] = pack_rows(fc) - got[tiles * chunk : tiles * chunk + q]
     err_ref[q : q + 1, :] = pltpu.roll(jnp.sum(fi, axis=0, keepdims=True), GROUP, axis=1)
-    col = col_ref[...]
+    col = col_ref[...] + col_late_ref[...]
     sums = jnp.sum(fc, axis=0, keepdims=True) + pltpu.roll(
         jnp.sum(col, axis=0, keepdims=True), 2 * GROUP, axis=1
     )
@@ -190,11 +263,11 @@
         pay_ref[p, n : n + 1, :] = sums
 
 
-def totals(store_parts, item_hist, w1, w2, w3, col, chunk, item_peers):
+def totals(store_parts, item_hist, w1, w2, w3, col, col_late, chunk, item_peers):
     items = item_hist.shape[0]
     return pl.pallas_call(
         functools.partial(totals_kernel, chunk),
-        in_specs=whole(6),
+        in_specs=whole(7),
         out_specs=whole(3),
         out_shape=[
             jax.ShapeDtypeStruct((8, LANES), F32),
@@ -204,29 +277,31 @@
         scratch_shapes=[pltpu.VMEM((w1.shape[1], LANES), BF16)],
         compiler_params=params(8),
         name="totals",
-    )(store_parts, item_hist, w1, w2, w3, col)
-
-
-def middle_kernel(chunk, n, err_ref, got_ref, pay_ref):
+    )(store_parts, item_hist, w1, w2, w3, col, col_late)
+
+
+def middle_kernel(chunk, n, err_ref, keep_ref, came_ref, got_ref, pay_ref):
     q = chunk // 4
     sums = err_ref[q : q + 1, :]
     for p in range(got_ref.shape[0]):
         sums = sums + got_ref[p, n : n + 1, :]
     err = err_ref[0:q, :]
+    late = keep_ref[...] + came_ref[...]
     for p in range(pay_ref.shape[0]):
         pay_ref[p, 0:q, :] = err
         pay_ref[p, q : q + 1, :] = sums
-
-
-def middle(err, got, chunk, items, peers):
+        pay_ref[p, 8:, :] = late
+
+
+def middle(err, keep, came, got, chunk, items, peers):
     return pl.pallas_call(
         functools.partial(middle_kernel, chunk, items // 4),
-        in_specs=whole(2),
+        in_specs=whole(4),
         out_specs=whole(1)[0],
-        out_shape=jax.ShapeDtypeStruct((peers, 8, LANES), F32),
+        out_shape=jax.ShapeDtypeStruct((peers, 8 + keep.shape[0], LANES), F32),
         compiler_params=params(2),
         name="middle",
-    )(err, got)
+    )(err, keep, came, got)
 
 
 def final_kernel(horizon, item_count, store_count, base_ref, item_ref, one_ref, two_ref, out_ref, sgap_ref, igap_ref, err_ref):
@@ -258,6 +333,14 @@
         for k in range(4):
             r = (p * 4 + k) * q
             err_ref[r : r + q, :] = group(two_ref[p, 0:q, :], k)
+    n_late = two_ref.shape[1] - 8
+    for odd in range(2):
+        row = two_ref[odd, 8:, :]
+        for p in range(odd + 2, peers, 2):
+            row = row + two_ref[p, 8:, :]
+        for k in range(4):
+            r = stores - (2 - odd) * 4 * n_late + k * n_late
+            err_ref[r : r + n_late, :] -= group(row, k)
     store_err = err_ref[...].T[:horizon]
 
     denominator = 1.0 + item_count + store_count
@@ -304,9 +387,12 @@
     return lax.ppermute(x, axis, [(i, i ^ flip) for i in range(lax.axis_size(axis))])
 
 
-def add_over_stores(x):
+def add_over_x(x):
     x = x + partner(x, "store", 1)
-    x = x + partner(x, "store", 2)
+    return x + partner(x, "store", 2)
+
+
+def add_over_y(x):
     near, far, across = (partner(x, "store", flip) for flip in (4, 12, 8))
     return (x + across) + (near + far)
 
@@ -318,13 +404,23 @@
     chunk = stores // n_dept
     w3 = final_layer_matrix.T
 
-    pay, item_part, col, y = bottom(history, w1, w2, w3, n_dept, 64, 32)
+    block, part, late = stores // 4, stores // 8, 2
+    pay, item_part, col, y = early(history, w1, w2, w3, n_dept, block, part, late)
     store_parts = exchange(pay, "dept")
-    item_hist = add_over_stores(item_part)
-    base, item_hist = lax.optimization_barrier((arrange(stay(y), items, horizon), item_hist))
-    err, item_fc, pay_one = totals(store_parts, item_hist, w1, w2, w3, col, chunk, n_store)
+    item_hist = add_over_x(item_part)
+    late_rows, late_col, late_y = late_forecasts(history, w1, w2, w3, block, part, late)
+    late_rows, late_y, item_hist = lax.optimization_barrier((late_rows, late_y, item_hist))
+    item_hist = add_over_y(item_hist)
+    odd = lax.rem(lax.axis_index("dept"), 2) == 1
+    keep = jnp.where(odd, late_rows[1], late_rows[0])
+    came = partner(jnp.where(odd, late_rows[0], late_rows[1]), "dept", 1)
+    base = arrange(y, late_y, items, horizon)
+    base, item_hist, came = lax.optimization_barrier((base, item_hist, came))
+    err, item_fc, pay_one = totals(
+        store_parts, item_hist, w1, w2, w3, col, late_col, chunk, n_store
+    )
     one = exchange(pay_one, "store")
-    pay_two = middle(err, one, chunk, items, n_dept)
+    pay_two = middle(err, keep, came, one, chunk, items, n_dept)
     two = exchange(pay_two, "dept")
     out, store_gap, item_gap = final(
         base, item_fc, one, two, horizon, float(items * n_dept), float(stores * n_store)

time: 71.8 us -> 73.8 us (1.028)
  waiting for transfers between devices: 5.95 us -> 0.9 us
  Pallas kernels: 19.4 us -> 23.1 us
  blocking collectives: 27.5 us -> 30.2 us
    pallas_call x2 -> x3, Pallas kernels: 15.1 us -> 18.8 us  [the longest x1 10.8 us: early(): pl.pallas_call(functools.partial(early_kernel, chunk, part, late), grid=(...]
    ppermute x5 -> x6, waiting for transfers between devices: 3.7 us -> 0.89 us  [partner(): lax.ppermute(x, axis, [(i, i ^ flip) for i in range(lax.axis_size(axis))])]
    all_to_all x2, blocking collectives: 27.5 us -> 30.2 us  [exchange(): return lax.all_to_all(x, axis, 0, 0, tiled=True)]
    all_to_all x1, waiting for transfers between devices: 2.25 us -> 0.01 us  [exchange(): return lax.all_to_all(x, axis, 0, 0, tiled=True)]
    ppermute x5 -> x6, starting transfers between devices: 7.97 us -> 8.32 us  [partner(): lax.ppermute(x, axis, [(i, i ^ flip) for i in range(lax.axis_size(axis))])]
  transfers between devices with their start and end apart: 6 -> 7, of which waited for: 4 -> 1; matrix products, arithmetic and copies ran while one was open for 0% -> 0% of each run, Pallas kernels for 4% -> 14%
where the time goes in v4:
time: 73.8 us; the launch traced here: 73.3 us
  blocking collectives  30.2 us (41%)
  Pallas kernels  23.1 us (31%)
  starting transfers between devices  18.3 us (25%)
  waiting for transfers between devices  0.9 us (1%)
    all_to_all x2, blocking collectives, exchange(): return lax.all_to_all(x, axis, 0, 0, tiled=True)  30.2 us
    pallas_call x1, Pallas kernels, early(): pl.pallas_call(functools.partial(early_kernel, chunk, part, late), grid=(...  10.8 us
    all_to_all x1, starting transfers between devices, exchange(): return lax.all_to_all(x, axis, 0, 0, tiled=True)  10 us
    ppermute x6, starting transfers between devices, partner(): lax.ppermute(x, axis, [(i, i ^ flip) for i in range(lax.axis_size(axis))])  8.32 us
    pallas_call x1, Pallas kernels, late_forecasts(): pl.pallas_call(functools.partial(late_kernel, part), grid=(late,), in_spe...  7.34 us
    pallas_call x1, Pallas kernels, arrange(): pl.pallas_call(functools.partial(arrange_kernel, horizon, items), in_spec...  2.93 us
  transfers between devices with their start and end apart: 7, of which 1 were waited for; matrix products, arithmetic and copies ran while one was open for 0% of the time, Pallas kernels for 14%

profile of v4, /device:TPU:1, one launch (start us, length us, event | category | flops | bytes accessed | tf_op | source)
XLA Modules:
  0.0 73.3 jit_solution(2436732005232683056)
XLA Ops:
  0.6 0.0 copy-start
  0.6 0.0 copy-start.1
  0.7 0.0 copy-start.2
  0.7 10.8 %early.1 = (f32[16,72,128]{2,1,0:T(8,128)}, f32[24,512]{1,0:T(8,128)S(1)}, f32[24,128]{1,0:T(8,128)S(1)}, f32[3072,128]{1,0:T(8,128)}) custom-call(bf16[256,24,512]{2,1,0:T(8,128)(2,1)} %h_ref.3, bf16[512,512]{1,0:T(8,128)(2,1)} %w1_ref.5, bf16[512,512]{1,0:T(8,128)(2,1)} %w2_ref.5, bf16[28,512]{1,0:T(8,128)(2,1)} %bitcast.7), custom_call_target="tpu_custom_call" | custom-call | flops 3623878656 | bytes 7864320 | tf_op jit(solution)/shard_map/early/pallas_call | solution.py:110
  11.5 10.0 %all-to-all-start = ((f32[16,72,128]{2,1,0:T(8,128)}), f32[16,72,128]{2,1,0:T(8,128)S(1)}, u32[]{:S(2)}, u32[]{:S(2)}) async-start(f32[16,72,128]{2,1,0:T(8,128)} %get-tuple-element.30), calls=%async_computation | async-start | bytes 1179648 | tf_op jit(solution)/shard_map/all_to_all | solution.py:383
  21.5 1.1 %collective-permute-start = (f32[24,512]{1,0:T(8,128)S(1)}, f32[24,512]{1,0:T(8,128)S(1)}, u32[]{:S(2)}, u32[]{:S(2)}) collective-permute-start(f32[24,512]{1,0:T(8,128)S(1)} %get-tuple-element.25), channel_id=1, source_target_pairs={{0,16},{16,0},{32,48},{48,32},{64,80},{80,64},{96,112},{112,96},{1... | collective-permute-start | bytes 147464 | tf_op jit(solution)/shard_map/ppermute | solution.py:387
  22.6 0.9 %collective-permute-done = f32[24,512]{1,0:T(8,128)S(1)} collective-permute-done((f32[24,512]{1,0:T(8,128)S(1)}, f32[24,512]{1,0:T(8,128)S(1)}, u32[]{:S(2)}, u32[]{:S(2)}) %collective-permute-start) | collective-permute-done | bytes 49184 | tf_op jit(solution)/shard_map/ppermute | solution.py:387
  23.4 2.5 %collective-permute-start.1 = (f32[24,512]{1,0:T(8,128)S(1)}, f32[24,512]{1,0:T(8,128)S(1)}, u32[]{:S(2)}, u32[]{:S(2)}) collective-permute-start(f32[24,512]{1,0:T(8,128)S(1)} %add.15), channel_id=1, source_target_pairs={{0,32},{16,48},{32,0},{48,16},{64,96},{80,112},{96,64},{112,80},{1... | collective-permute-start | bytes 147464 | tf_op jit(solution)/shard_map/ppermute | solution.py:387
  26.0 0.0 copy-done
  26.0 0.0 copy-done.1
  26.0 0.0 copy-done.2
  26.0 7.3 %late.1 = (f32[2,16,128]{2,1,0:T(8,128)S(1)}, f32[24,128]{1,0:T(8,128)S(1)}, f32[3072,128]{1,0:T(8,128)}) custom-call(bf16[256,24,512]{2,1,0:T(8,128)(2,1)} %h_ref.3, bf16[512,512]{1,0:T(8,128)(2,1)S(1)} %copy-done, bf16[512,512]{1,0:T(8,128)(2,1)S(1)} %copy-done.1, bf16[28,512]{1,0:T(8,128)(2,1)S(1)} %bitcast.8), custom_call_target="tpu_custom_call" | custom-call | flops 3623878656 | bytes 4718592 | tf_op jit(solution)/shard_map/late/pallas_call | solution.py:168
  33.3 0.0 collective-permute-done.1
  33.3 3.0 %collective-permute-start.2 = (f32[24,512]{1,0:T(8,128)S(1)}, f32[24,512]{1,0:T(8,128)S(1)}, u32[]{:S(2)}, u32[]{:S(2)}) collective-permute-start(f32[24,512]{1,0:T(8,128)S(1)} %add.16), channel_id=1, source_target_pairs={{0,128},{16,144},{32,160},{48,176},{64,192},{80,208},{96,224},{112... | collective-permute-start | bytes 147464 | tf_op jit(solution)/shard_map/ppermute | solution.py:387
  36.3 0.4 collective-permute-start.3
  36.7 0.4 collective-permute-start.4
  37.1 1.0 %collective-permute-start.5 = (f32[16,128]{1,0:T(8,128)S(1)}, f32[16,128]{1,0:T(8,128)S(1)}, u32[]{:S(2)}, u32[]{:S(2)}) collective-permute-start(f32[16,128]{1,0:T(8,128)S(1)} %get-tuple-element.42), channel_id=1, source_target_pairs={{0,1},{1,0},{2,3},{3,2},{4,5},{5,4},{6,7},{7,6},{8,9},{9,8},{10,11... | collective-permute-start | bytes 24584 | tf_op jit(solution)/shard_map/ppermute | solution.py:387
  38.1 2.9 %arrange.1.base_ref = f32[672,256]{1,0:T(8,128)S(1)} custom-call(f32[3072,128]{1,0:T(8,128)} %get-tuple-element.22.early_ref, f32[3072,128]{1,0:T(8,128)} %get-tuple-element.26.late_ref), custom_call_target="tpu_custom_call" | custom-call | flops 3145728 | bytes 3145728 | tf_op jit(solution)/shard_map/arrange/pallas_call | solution.py:226
  41.0 0.0 collective-permute-done.2
  41.0 0.0 collective-permute-done.3
  41.0 0.0 collective-permute-done.4
  41.1 0.0 collective-permute-done.5.came_ref
  41.1 0.0 all-to-all-done.s_ref
  41.1 0.6 totals.1
  41.7 14.4 %all_to_all.15.got_ref.one_ref = f32[16,8,128]{2,1,0:T(8,128)S(1)} all-to-all(f32[16,8,128]{2,1,0:T(8,128)S(1)} %get-tuple-element.35), channel_id=1, replica_groups=mesh['store'=16,'dept'=16] {'store'}, dimensions={0} | all-to-all | bytes 131072 | tf_op jit(solution)/shard_map/all_to_all | solution.py:383
  56.1 15.8 %all_to_all.16.two_ref = f32[16,24,128]{2,1,0:T(8,128)S(1)} all-to-all(f32[16,24,128]{2,1,0:T(8,128)S(1)} %middle.1), channel_id=1, replica_groups=mesh['store'=16,'dept'=16] {'dept'}, dimensions={0} | all-to-all | bytes 393216 | tf_op jit(solution)/shard_map/all_to_all | solution.py:383
  72.0 1.4 %final.1 = (f32[672,256]{1,0:T(8,128)}, f32[28,256]{1,0:T(8,128)}, f32[24,28]{1,0:T(8,128)}) custom-call(f32[672,256]{1,0:T(8,128)S(1)} %arrange.1.base_ref, f32[24,128]{1,0:T(8,128)S(1)} %get-tuple-element.34.item_ref, f32[16,8,128]{2,1,0:T(8,128)S(1)} %all_to_all.15.got_ref.one_ref, f32[16,24,128]{2,1,0:T(8,128)S(1)} %all_to_all.16.two_ref), custom_call_target="tpu_custom_call" | custom-call | tf_op jit(solution)/shard_map/final/pallas_call | solution.py:367
  (5 shorter events, 0.1 us)
Async XLA Ops:
  0.6 25.3 %copy-start = (bf16[512,512]{1,0:T(8,128)(2,1)S(1)}, bf16[512,512]{1,0:T(8,128)(2,1)}, u32[]{:S(2)}) copy-start(bf16[512,512]{1,0:T(8,128)(2,1)} %w1_ref.5) | copy-start | bytes 1572868
  0.6 25.3 %copy-start.1 = (bf16[512,512]{1,0:T(8,128)(2,1)S(1)}, bf16[512,512]{1,0:T(8,128)(2,1)}, u32[]{:S(2)}) copy-start(bf16[512,512]{1,0:T(8,128)(2,1)} %w2_ref.5) | copy-start | bytes 1572868
  0.7 25.3 %copy-start.2 = (bf16[512,28]{0,1:T(8,128)(2,1)S(1)}, bf16[512,28]{0,1:T(8,128)(2,1)}, u32[]{:S(2)}) copy-start(bf16[512,28]{0,1:T(8,128)(2,1)} %param.7) | copy-start | bytes 86020
  11.5 29.6 %all-to-all-start = ((f32[16,72,128]{2,1,0:T(8,128)}), f32[16,72,128]{2,1,0:T(8,128)S(1)}, u32[]{:S(2)}, u32[]{:S(2)}) async-start(f32[16,72,128]{2,1,0:T(8,128)} %get-tuple-element.30), calls=%async_computation | async-start | bytes 1179648 | tf_op jit(solution)/shard_map/all_to_all | solution.py:383
  21.5 1.9 %collective-permute-start = (f32[24,512]{1,0:T(8,128)S(1)}, f32[24,512]{1,0:T(8,128)S(1)}, u32[]{:S(2)}, u32[]{:S(2)}) collective-permute-start(f32[24,512]{1,0:T(8,128)S(1)} %get-tuple-element.25), channel_id=1, source_target_pairs={{0,16},{16,0},{32,48},{48,32},{64,80},{80,64},{96,112},{112,96},{1... | collective-permute-start | bytes 147464 | tf_op jit(solution)/shard_map/ppermute | solution.py:387
  23.4 9.9 %collective-permute-start.1 = (f32[24,512]{1,0:T(8,128)S(1)}, f32[24,512]{1,0:T(8,128)S(1)}, u32[]{:S(2)}, u32[]{:S(2)}) collective-permute-start(f32[24,512]{1,0:T(8,128)S(1)} %add.15), channel_id=1, source_target_pairs={{0,32},{16,48},{32,0},{48,16},{64,96},{80,112},{96,64},{112,80},{1... | collective-permute-start | bytes 147464 | tf_op jit(solution)/shard_map/ppermute | solution.py:387
  33.3 7.7 %collective-permute-start.2 = (f32[24,512]{1,0:T(8,128)S(1)}, f32[24,512]{1,0:T(8,128)S(1)}, u32[]{:S(2)}, u32[]{:S(2)}) collective-permute-start(f32[24,512]{1,0:T(8,128)S(1)} %add.16), channel_id=1, source_target_pairs={{0,128},{16,144},{32,160},{48,176},{64,192},{80,208},{96,224},{112... | collective-permute-start | bytes 147464 | tf_op jit(solution)/shard_map/ppermute | solution.py:387
  36.3 4.7 %collective-permute-start.3 = (f32[24,512]{1,0:T(8,128)S(1)}, f32[24,512]{1,0:T(8,128)S(1)}, u32[]{:S(2)}, u32[]{:S(2)}) collective-permute-start(f32[24,512]{1,0:T(8,128)S(1)} %add.16), channel_id=1, source_target_pairs={{0,64},{16,80},{32,96},{48,112},{64,0},{80,16},{96,32},{112,48},{1... | collective-permute-start | bytes 147464 | tf_op jit(solution)/shard_map/ppermute | solution.py:387
  36.7 4.3 %collective-permute-start.4 = (f32[24,512]{1,0:T(8,128)S(1)}, f32[24,512]{1,0:T(8,128)S(1)}, u32[]{:S(2)}, u32[]{:S(2)}) collective-permute-start(f32[24,512]{1,0:T(8,128)S(1)} %add.16), channel_id=1, source_target_pairs={{0,192},{16,208},{32,224},{48,240},{64,128},{80,144},{96,160},{112... | collective-permute-start | bytes 147464 | tf_op jit(solution)/shard_map/ppermute | solution.py:387
  37.1 4.0 %collective-permute-start.5 = (f32[16,128]{1,0:T(8,128)S(1)}, f32[16,128]{1,0:T(8,128)S(1)}, u32[]{:S(2)}, u32[]{:S(2)}) collective-permute-start(f32[16,128]{1,0:T(8,128)S(1)} %get-tuple-element.42), channel_id=1, source_target_pairs={{0,1},{1,0},{2,3},{3,2},{4,5},{5,4},{6,7},{7,6},{8,9},{9,8},{10,11... | collective-permute-start | bytes 24584 | tf_op jit(solution)/shard_map/ppermute | solution.py:387

commit v5 on v3

--- a/solution.py
+++ b/solution.py
@@ -40,6 +40,25 @@
     return jnp.dot(b, w3, preferred_element_type=F32) * (var * inv)
 
 
+def sum_items(x):
+    stores, items, width = x.shape
+    x = x.reshape(stores, items // 8, 8, width)
+    total = x[:, 0]
+    for k in range(1, items // 8):
+        total = total + x[:, k]
+    v = total.reshape(stores // 8, 8, 8, width)
+    row = lax.broadcasted_iota(jnp.int32, (1, 1, 8, width), 2)
+    for bit in (4, 2, 1):
+        low = lax.rem(lax.div(row, bit), 2) == 0
+        a, b = v[:, :bit], v[:, bit:]
+        there = jnp.where(low, b, a)
+        up = pltpu.roll(there, bit, axis=2)
+        if bit < 4:
+            up = jnp.where(low, pltpu.roll(there, 8 - bit, axis=2), up)
+        v = jnp.where(low, a, b) + up
+    return v.reshape(stores, width)
+
+
 def widen(w3_ref, w3_wide):
     horizon = w3_ref.shape[0]
     w3_wide[...] = jnp.zeros_like(w3_wide)
@@ -63,17 +82,18 @@
         widen(w3_ref, w3_wide)
         item_ref[...] = jnp.zeros_like(item_ref)
         col_ref[...] = jnp.zeros_like(col_ref)
+        y_ref[...] = jnp.zeros_like(y_ref)
 
     w1, w2, w3 = w1_ref[...], w2_ref[...], w3_wide[...]
     tiles = days // LANES
     for p in range(block // part):
         x = h_ref[p * part : (p + 1) * part].astype(F32)
-        by_store = jnp.sum(x, axis=1)
+        by_store = sum_items(x)
         item_ref[...] += jnp.sum(x, axis=0)
         y = forecaster(x.reshape(part * items, days), w1, w2, w3)
-        y_ref[p * part * items : (p + 1) * part * items, :] = y
+        y_ref[p * part * items : (p + 1) * part * items, :] += pltpu.roll(y, step * GROUP, axis=1)
         y = y.reshape(part, items, LANES)
-        row = jnp.sum(y, axis=1)
+        row = sum_items(y)
         col_ref[...] += jnp.sum(y, axis=0)
         for q in range(part // chunk):
             peer = p * (part // chunk) + q
@@ -106,19 +126,19 @@
             pl.BlockSpec((block // chunk, pay_rows, LANES), lambda i: (i, 0, 0)),
             fixed((items, days)),
             fixed((items, LANES)),
-            pl.BlockSpec((block * items, LANES), lambda i: (i, 0)),
+            fixed((block * items, LANES)),
         ],
         out_shape=[
             jax.ShapeDtypeStruct((peers, pay_rows, LANES), F32),
             jax.ShapeDtypeStruct((items, days), F32),
             jax.ShapeDtypeStruct((items, LANES), F32),
-            pltpu.HBM((rows, LANES), F32),
+            jax.ShapeDtypeStruct((block * items, LANES), F32),
         ],
         scratch_shapes=[pltpu.VMEM((hid, LANES), BF16)],
         compiler_params=params(24),
         cost_estimate=pl.CostEstimate(
             flops=2 * rows * (days * hid + hid * hid + hid * LANES),
-            bytes_accessed=2 * history.size + 4 * rows * LANES,
+            bytes_accessed=2 * history.size,
             transcendentals=0,
         ),
         name="bottom",
@@ -126,38 +146,24 @@
 
 
 def arrange_kernel(horizon, items, y_ref, out_ref):
-    stores = y_ref.shape[0] // items
-    lane = lax.broadcasted_iota(jnp.int32, (stores, LANES), 1)
-    tiles = [None] * pl.cdiv(items * horizon, LANES)
-
-    def add(t, v):
-        tiles[t] = v if tiles[t] is None else tiles[t] + v
-
+    block = y_ref.shape[0] // items
     for i in range(items):
-        v = y_ref[pl.ds(i, stores, stride=items), :]
-        t, off = divmod(i * horizon, LANES)
-        if off:
-            v = pltpu.roll(v, off, axis=1)
-        if off + horizon > LANES:
-            add(t, jnp.where(lane >= off, v, 0.0))
-            add(t + 1, jnp.where(lane < off, v, 0.0))
-        else:
-            add(t, v)
-    for t, v in enumerate(tiles):
-        height = min(LANES, items * horizon - t * LANES)
-        out_ref[t * LANES : t * LANES + height, :] = v.T[:height]
+        v = y_ref[pl.ds(i, block, stride=items), :].T
+        blocks = [v[k * GROUP : k * GROUP + horizon] for k in range(LANES // GROUP)]
+        out_ref[i * horizon : (i + 1) * horizon, :] = jnp.concatenate(blocks, axis=1)
 
 
 def arrange(y, items, horizon):
     rows = y.shape[0]
+    stores = rows // items * (LANES // GROUP)
     return pl.pallas_call(
         functools.partial(arrange_kernel, horizon, items),
         in_specs=whole(1),
         out_specs=whole(1)[0],
-        out_shape=jax.ShapeDtypeStruct((items * horizon, rows // items), F32),
+        out_shape=jax.ShapeDtypeStruct((items * horizon, stores), F32),
         compiler_params=params(12),
         cost_estimate=pl.CostEstimate(
-            flops=rows * LANES * 4, bytes_accessed=rows * LANES * 4, transcendentals=0
+            flops=16 * rows * LANES, bytes_accessed=12 * rows * LANES, transcendentals=0
         ),
         name="arrange",
     )(y)
@@ -304,9 +310,12 @@
     return lax.ppermute(x, axis, [(i, i ^ flip) for i in range(lax.axis_size(axis))])
 
 
-def add_over_stores(x):
+def add_over_x(x):
     x = x + partner(x, "store", 1)
-    x = x + partner(x, "store", 2)
+    return x + partner(x, "store", 2)
+
+
+def add_over_y(x):
     near, far, across = (partner(x, "store", flip) for flip in (4, 12, 8))
     return (x + across) + (near + far)
 
@@ -318,10 +327,12 @@
     chunk = stores // n_dept
     w3 = final_layer_matrix.T
 
-    pay, item_part, col, y = bottom(history, w1, w2, w3, n_dept, 64, 32)
+    pay, item_part, col, y = bottom(history, w1, w2, w3, n_dept, stores // 4, stores // 8)
     store_parts = exchange(pay, "dept")
-    item_hist = add_over_stores(item_part)
-    base, item_hist = lax.optimization_barrier((arrange(stay(y), items, horizon), item_hist))
+    item_hist = add_over_x(item_part)
+    base = arrange(y, items, horizon)
+    base, item_hist = lax.optimization_barrier((base, item_hist))
+    item_hist = add_over_y(item_hist)
     err, item_fc, pay_one = totals(store_parts, item_hist, w1, w2, w3, col, chunk, n_store)
     one = exchange(pay_one, "store")
     pay_two = middle(err, one, chunk, items, n_dept)

time: 71.8 us -> 71.4 us (level)
  Pallas kernels: 19.4 us -> 16.8 us
  waiting for transfers between devices: 5.95 us -> 8.47 us
    pallas_call x1, Pallas kernels: 2.93 us -> 0.7 us  [arrange(): pl.pallas_call(functools.partial(arrange_kernel, horizon, items), in_spec...]
    ppermute x5, waiting for transfers between devices: 3.7 us -> 5.62 us  [partner(): lax.ppermute(x, axis, [(i, i ^ flip) for i in range(lax.axis_size(axis))])]
  transfers between devices with their start and end apart: 6 -> 6, of which waited for: 4 -> 6; matrix products, arithmetic and copies ran while one was open for 0% -> 0% of each run, Pallas kernels for 4% -> 1%
where the time goes in v5:
time: 71.4 us; the launch traced here: 71.1 us
  blocking collectives  27.4 us (38%)
  starting transfers between devices  17.7 us (25%)
  Pallas kernels  16.8 us (24%)
  waiting for transfers between devices  8.47 us (12%)
    all_to_all x2, blocking collectives, exchange(): return lax.all_to_all(x, axis, 0, 0, tiled=True)  27.4 us
    pallas_call x1, Pallas kernels, bottom(): pl.pallas_call(functools.partial(bottom_kernel, chunk, part), grid=(store...  14.1 us
    all_to_all x1, starting transfers between devices, exchange(): return lax.all_to_all(x, axis, 0, 0, tiled=True)  10 us
    ppermute x5, starting transfers between devices, partner(): lax.ppermute(x, axis, [(i, i ^ flip) for i in range(lax.axis_size(axis))])  7.69 us
    ppermute x5, waiting for transfers between devices, partner(): lax.ppermute(x, axis, [(i, i ^ flip) for i in range(lax.axis_size(axis))])  5.62 us
    all_to_all x1, waiting for transfers between devices, exchange(): return lax.all_to_all(x, axis, 0, 0, tiled=True)  2.85 us
  transfers between devices with their start and end apart: 6, of which 6 were waited for; matrix products, arithmetic and copies ran while one was open for 0% of the time, Pallas kernels for 1%

profile of v5, /device:TPU:1, one launch (start us, length us, event | category | flops | bytes accessed | tf_op | source)
XLA Modules:
  0.0 71.1 jit_solution(7381854115238232331)
XLA Ops:
  0.6 0.0 copy-start
  0.6 0.0 copy-start.1
  0.7 0.0 copy-start.2
  0.7 14.1 %bottom.1 = (f32[16,72,128]{2,1,0:T(8,128)}, f32[24,512]{1,0:T(8,128)S(1)}, f32[24,128]{1,0:T(8,128)S(1)}, f32[1536,128]{1,0:T(8,128)S(1)}) custom-call(bf16[256,24,512]{2,1,0:T(8,128)(2,1)} %h_ref.1, bf16[512,512]{1,0:T(8,128)(2,1)} %w1_ref.3, bf16[512,512]{1,0:T(8,128)(2,1)} %w2_ref.3, bf16[28,512]{1,0:T(8,128)(2,1)} %bitcast.3), custom_call_target="tpu_custom_call" | custom-call | flops 7247757312 | bytes 6291456 | tf_op jit(solution)/shard_map/bottom/pallas_call | solution.py:116
  14.7 10.0 %all-to-all-start = ((f32[16,72,128]{2,1,0:T(8,128)}), f32[16,72,128]{2,1,0:T(8,128)S(1)}, u32[]{:S(2)}, u32[]{:S(2)}) async-start(f32[16,72,128]{2,1,0:T(8,128)} %get-tuple-element.18), calls=%async_computation | async-start | bytes 1179648 | tf_op jit(solution)/shard_map/all_to_all | solution.py:306
  24.8 1.0 %collective-permute-start = (f32[24,512]{1,0:T(8,128)S(1)}, f32[24,512]{1,0:T(8,128)S(1)}, u32[]{:S(2)}, u32[]{:S(2)}) collective-permute-start(f32[24,512]{1,0:T(8,128)S(1)} %get-tuple-element.16), channel_id=1, source_target_pairs={{0,16},{16,0},{32,48},{48,32},{64,80},{80,64},{96,112},{112,96},{1... | collective-permute-start | bytes 147464 | tf_op jit(solution)/shard_map/ppermute | solution.py:310
  25.8 0.9 %collective-permute-done = f32[24,512]{1,0:T(8,128)S(1)} collective-permute-done((f32[24,512]{1,0:T(8,128)S(1)}, f32[24,512]{1,0:T(8,128)S(1)}, u32[]{:S(2)}, u32[]{:S(2)}) %collective-permute-start) | collective-permute-done | bytes 49184 | tf_op jit(solution)/shard_map/ppermute | solution.py:310
  26.7 2.5 %collective-permute-start.1 = (f32[24,512]{1,0:T(8,128)S(1)}, f32[24,512]{1,0:T(8,128)S(1)}, u32[]{:S(2)}, u32[]{:S(2)}) collective-permute-start(f32[24,512]{1,0:T(8,128)S(1)} %add.15), channel_id=1, source_target_pairs={{0,32},{16,48},{32,0},{48,16},{64,96},{80,112},{96,64},{112,80},{1... | collective-permute-start | bytes 147464 | tf_op jit(solution)/shard_map/ppermute | solution.py:310
  29.3 0.7 arrange.1.base_ref
  30.0 1.3 %collective-permute-done.1 = f32[24,512]{1,0:T(8,128)S(1)} collective-permute-done((f32[24,512]{1,0:T(8,128)S(1)}, f32[24,512]{1,0:T(8,128)S(1)}, u32[]{:S(2)}, u32[]{:S(2)}) %collective-permute-start.1) | collective-permute-done | bytes 49184 | tf_op jit(solution)/shard_map/ppermute | solution.py:310
  31.3 2.8 %collective-permute-start.4 = (f32[24,512]{1,0:T(8,128)S(1)}, f32[24,512]{1,0:T(8,128)S(1)}, u32[]{:S(2)}, u32[]{:S(2)}) collective-permute-start(f32[24,512]{1,0:T(8,128)S(1)} %add.16), channel_id=1, source_target_pairs={{0,192},{16,208},{32,224},{48,240},{64,128},{80,144},{96,160},{112... | collective-permute-start | bytes 147464 | tf_op jit(solution)/shard_map/ppermute | solution.py:310
  34.1 0.0 collective-permute-start.3
  34.1 1.3 %collective-permute-start.2 = (f32[24,512]{1,0:T(8,128)S(1)}, f32[24,512]{1,0:T(8,128)S(1)}, u32[]{:S(2)}, u32[]{:S(2)}) collective-permute-start(f32[24,512]{1,0:T(8,128)S(1)} %add.16), channel_id=1, source_target_pairs={{0,128},{16,144},{32,160},{48,176},{64,192},{80,208},{96,224},{112... | collective-permute-start | bytes 147464 | tf_op jit(solution)/shard_map/ppermute | solution.py:310
  35.4 0.5 collective-permute-done.4
  35.8 1.5 %collective-permute-done.3 = f32[24,512]{1,0:T(8,128)S(1)} collective-permute-done((f32[24,512]{1,0:T(8,128)S(1)}, f32[24,512]{1,0:T(8,128)S(1)}, u32[]{:S(2)}, u32[]{:S(2)}) %collective-permute-start.3) | collective-permute-done | bytes 49184 | tf_op jit(solution)/shard_map/ppermute | solution.py:310
  37.3 1.5 %collective-permute-done.2 = f32[24,512]{1,0:T(8,128)S(1)} collective-permute-done((f32[24,512]{1,0:T(8,128)S(1)}, f32[24,512]{1,0:T(8,128)S(1)}, u32[]{:S(2)}, u32[]{:S(2)}) %collective-permute-start.2) | collective-permute-done | bytes 49184 | tf_op jit(solution)/shard_map/ppermute | solution.py:310
  38.8 2.9 %all-to-all-done.s_ref = f32[16,72,128]{2,1,0:T(8,128)S(1)} async-done(((f32[16,72,128]{2,1,0:T(8,128)}), f32[16,72,128]{2,1,0:T(8,128)S(1)}, u32[]{:S(2)}, u32[]{:S(2)}) %all-to-all-start) | async-done | bytes 589856 | tf_op jit(solution)/shard_map/all_to_all | solution.py:306
  41.7 0.0 copy-done
  41.7 0.0 copy-done.1
  41.7 0.0 copy-done.2
  41.7 0.6 totals.1
  42.4 16.6 %all_to_all.15.got_ref.one_ref = f32[16,8,128]{2,1,0:T(8,128)S(1)} all-to-all(f32[16,8,128]{2,1,0:T(8,128)S(1)} %get-tuple-element.22), channel_id=1, replica_groups=mesh['store'=16,'dept'=16] {'store'}, dimensions={0} | all-to-all | bytes 131072 | tf_op jit(solution)/shard_map/all_to_all | solution.py:306
  58.9 10.8 %all_to_all.16.two_ref = f32[16,8,128]{2,1,0:T(8,128)S(1)} all-to-all(f32[16,8,128]{2,1,0:T(8,128)S(1)} %middle.1), channel_id=1, replica_groups=mesh['store'=16,'dept'=16] {'dept'}, dimensions={0} | all-to-all | bytes 131072 | tf_op jit(solution)/shard_map/all_to_all | solution.py:306
  69.8 1.4 %final.1 = (f32[672,256]{1,0:T(8,128)}, f32[28,256]{1,0:T(8,128)}, f32[24,28]{1,0:T(8,128)}) custom-call(f32[672,256]{1,0:T(8,128)S(1)} %arrange.1.base_ref, f32[24,128]{1,0:T(8,128)S(1)} %get-tuple-element.21.item_ref, f32[16,8,128]{2,1,0:T(8,128)S(1)} %all_to_all.15.got_ref.one_ref, f32[16,8,128]{2,1,0:T(8,128)S(1)} %all_to_all.16.two_ref), custom_call_target="tpu_custom_call" | custom-call | tf_op jit(solution)/shard_map/final/pallas_call | solution.py:290
  (4 shorter events, 0.1 us)
Async XLA Ops:
  0.6 41.1 %copy-start = (bf16[512,512]{1,0:T(8,128)(2,1)S(1)}, bf16[512,512]{1,0:T(8,128)(2,1)}, u32[]{:S(2)}) copy-start(bf16[512,512]{1,0:T(8,128)(2,1)} %w1_ref.3) | copy-start | bytes 1572868
  0.6 41.1 %copy-start.1 = (bf16[512,512]{1,0:T(8,128)(2,1)S(1)}, bf16[512,512]{1,0:T(8,128)(2,1)}, u32[]{:S(2)}) copy-start(bf16[512,512]{1,0:T(8,128)(2,1)} %w2_ref.3) | copy-start | bytes 1572868
  0.7 41.0 %copy-start.2 = (bf16[512,28]{0,1:T(8,128)(2,1)S(1)}, bf16[512,28]{0,1:T(8,128)(2,1)}, u32[]{:S(2)}) copy-start(bf16[512,28]{0,1:T(8,128)(2,1)} %param.7) | copy-start | bytes 86020
  14.7 27.0 %all-to-all-start = ((f32[16,72,128]{2,1,0:T(8,128)}), f32[16,72,128]{2,1,0:T(8,128)S(1)}, u32[]{:S(2)}, u32[]{:S(2)}) async-start(f32[16,72,128]{2,1,0:T(8,128)} %get-tuple-element.18), calls=%async_computation | async-start | bytes 1179648 | tf_op jit(solution)/shard_map/all_to_all | solution.py:306
  24.8 1.9 %collective-permute-start = (f32[24,512]{1,0:T(8,128)S(1)}, f32[24,512]{1,0:T(8,128)S(1)}, u32[]{:S(2)}, u32[]{:S(2)}) collective-permute-start(f32[24,512]{1,0:T(8,128)S(1)} %get-tuple-element.16), channel_id=1, source_target_pairs={{0,16},{16,0},{32,48},{48,32},{64,80},{80,64},{96,112},{112,96},{1... | collective-permute-start | bytes 147464 | tf_op jit(solution)/shard_map/ppermute | solution.py:310
  26.7 4.5 %collective-permute-start.1 = (f32[24,512]{1,0:T(8,128)S(1)}, f32[24,512]{1,0:T(8,128)S(1)}, u32[]{:S(2)}, u32[]{:S(2)}) collective-permute-start(f32[24,512]{1,0:T(8,128)S(1)} %add.15), channel_id=1, source_target_pairs={{0,32},{16,48},{32,0},{48,16},{64,96},{80,112},{96,64},{112,80},{1... | collective-permute-start | bytes 147464 | tf_op jit(solution)/shard_map/ppermute | solution.py:310
  31.3 4.6 %collective-permute-start.4 = (f32[24,512]{1,0:T(8,128)S(1)}, f32[24,512]{1,0:T(8,128)S(1)}, u32[]{:S(2)}, u32[]{:S(2)}) collective-permute-start(f32[24,512]{1,0:T(8,128)S(1)} %add.16), channel_id=1, source_target_pairs={{0,192},{16,208},{32,224},{48,240},{64,128},{80,144},{96,160},{112... | collective-permute-start | bytes 147464 | tf_op jit(solution)/shard_map/ppermute | solution.py:310
  34.1 3.2 %collective-permute-start.3 = (f32[24,512]{1,0:T(8,128)S(1)}, f32[24,512]{1,0:T(8,128)S(1)}, u32[]{:S(2)}, u32[]{:S(2)}) collective-permute-start(f32[24,512]{1,0:T(8,128)S(1)} %add.16), channel_id=1, source_target_pairs={{0,64},{16,80},{32,96},{48,112},{64,0},{80,16},{96,32},{112,48},{1... | collective-permute-start | bytes 147464 | tf_op jit(solution)/shard_map/ppermute | solution.py:310
  34.1 4.7 %collective-permute-start.2 = (f32[24,512]{1,0:T(8,128)S(1)}, f32[24,512]{1,0:T(8,128)S(1)}, u32[]{:S(2)}, u32[]{:S(2)}) collective-permute-start(f32[24,512]{1,0:T(8,128)S(1)} %add.16), channel_id=1, source_target_pairs={{0,128},{16,144},{32,160},{48,176},{64,192},{80,208},{96,224},{112... | collective-permute-start | bytes 147464 | tf_op jit(solution)/shard_map/ppermute | solution.py:310

commit v6 on v5

--- a/solution.py
+++ b/solution.py
@@ -73,8 +73,9 @@
     return out
 
 
-def bottom_kernel(chunk, part, h_ref, w1_ref, w2_ref, w3_ref, pay_ref, item_ref, col_ref, y_ref, w3_wide):
+def bottom_kernel(chunk, part, h_ref, w1_ref, w2_ref, w3_ref, keep_ref, send_ref, item_ref, col_ref, y_ref, w3_wide):
     block, items, days = h_ref.shape
+    even = lax.rem(lax.axis_index("dept"), 2) == 0
     step = pl.program_id(0)
 
     @pl.when(step == 0)
@@ -95,14 +96,25 @@
         y = y.reshape(part, items, LANES)
         row = sum_items(y)
         col_ref[...] += jnp.sum(y, axis=0)
-        for q in range(part // chunk):
-            peer = p * (part // chunk) + q
+        for q in range(0, part // chunk, 2):
+            pair = (p * (part // chunk) + q) // 2
+            first, second = q * chunk, (q + 1) * chunk
+
+            def put(where, a, b):
+                keep_ref[pair, where, :] = jnp.where(even, a, b)
+                send_ref[pair, where, :] = jnp.where(even, b, a)
+
             for t in range(tiles):
-                pay_ref[peer, t * chunk : (t + 1) * chunk, :] = by_store[
-                    q * chunk : (q + 1) * chunk, t * LANES : (t + 1) * LANES
-                ]
-            pay_ref[peer, tiles * chunk : tiles * chunk + chunk // 4, :] = pack_rows(
-                row[q * chunk : (q + 1) * chunk]
+                day = slice(t * LANES, (t + 1) * LANES)
+                put(
+                    slice(t * chunk, (t + 1) * chunk),
+                    by_store[first : first + chunk, day],
+                    by_store[second : second + chunk, day],
+                )
+            put(
+                slice(tiles * chunk, tiles * chunk + chunk // 4),
+                pack_rows(row[first : first + chunk]),
+                pack_rows(row[second : second + chunk]),
             )
 
 
@@ -123,13 +135,15 @@
             fixed(w3.shape),
         ],
         out_specs=[
-            pl.BlockSpec((block // chunk, pay_rows, LANES), lambda i: (i, 0, 0)),
+            pl.BlockSpec((block // chunk // 2, pay_rows, LANES), lambda i: (i, 0, 0)),
+            pl.BlockSpec((block // chunk // 2, pay_rows, LANES), lambda i: (i, 0, 0)),
             fixed((items, days)),
             fixed((items, LANES)),
             fixed((block * items, LANES)),
         ],
         out_shape=[
-            jax.ShapeDtypeStruct((peers, pay_rows, LANES), F32),
+            jax.ShapeDtypeStruct((peers // 2, pay_rows, LANES), F32),
+            jax.ShapeDtypeStruct((peers // 2, pay_rows, LANES), F32),
             jax.ShapeDtypeStruct((items, days), F32),
             jax.ShapeDtypeStruct((items, LANES), F32),
             jax.ShapeDtypeStruct((block * items, LANES), F32),
@@ -302,8 +316,8 @@
     )(base, item_fc, one, two)
 
 
-def exchange(x, axis):
-    return lax.all_to_all(x, axis, 0, 0, tiled=True)
+def exchange(x, axis, groups=None):
+    return lax.all_to_all(x, axis, 0, 0, axis_index_groups=groups, tiled=True)
 
 
 def partner(x, axis, flip):
@@ -327,11 +341,13 @@
     chunk = stores // n_dept
     w3 = final_layer_matrix.T
 
-    pay, item_part, col, y = bottom(history, w1, w2, w3, n_dept, stores // 4, stores // 8)
-    store_parts = exchange(pay, "dept")
+    keep, send, item_part, col, y = bottom(history, w1, w2, w3, n_dept, stores // 4, stores // 8)
+    came = partner(send, "dept", 1)
     item_hist = add_over_x(item_part)
     base = arrange(y, items, horizon)
-    base, item_hist = lax.optimization_barrier((base, item_hist))
+    came, item_hist, base = lax.optimization_barrier((came, item_hist, base))
+    along_z = [list(range(k, n_dept, 2)) for k in range(2)]
+    store_parts = exchange(keep + came, "dept", along_z)
     item_hist = add_over_y(item_hist)
     err, item_fc, pay_one = totals(store_parts, item_hist, w1, w2, w3, col, chunk, n_store)
     one = exchange(pay_one, "store")

time: 71.4 us -> 73.3 us (1.027)
  waiting for transfers between devices: 8.47 us -> 11 us
  blocking collectives: 27.4 us -> 26.6 us
  other arithmetic: 0.03 us -> 0.78 us
    ppermute x5 -> x6, waiting for transfers between devices: 5.62 us -> 8.66 us  [partner(): lax.ppermute(x, axis, [(i, i ^ flip) for i in range(lax.axis_size(axis))])]
    ppermute x5 -> x6, starting transfers between devices: 7.69 us -> 9.6 us  [partner(): lax.ppermute(x, axis, [(i, i ^ flip) for i in range(lax.axis_size(axis))])]
    all_to_all x1, starting transfers between devices: 10 us -> 8.2 us  [exchange(): return lax.all_to_all(x, axis, 0, 0, axis_index_groups=groups, tiled=True)]
    all_to_all x2, blocking collectives: 27.4 us -> 26.6 us  [exchange(): return lax.all_to_all(x, axis, 0, 0, axis_index_groups=groups, tiled=True)]
    add x0 -> x1, other arithmetic: none -> 0.75 us  [body(): store_parts = exchange(keep + came, 'dept', along_z)]
  transfers between devices with their start and end apart: 6 -> 7, of which waited for: 6 -> 6; matrix products, arithmetic and copies ran while one was open for 0% -> 0% of each run, Pallas kernels for 1% -> 1%
where the time goes in v6:
time: 73.3 us; the launch traced here: 73.1 us
  blocking collectives  26.6 us (36%)
  starting transfers between devices  17.8 us (24%)
  Pallas kernels  16.2 us (22%)
  waiting for transfers between devices  11 us (15%)
  other arithmetic  0.78 us (1%)
    all_to_all x2, blocking collectives, exchange(): return lax.all_to_all(x, axis, 0, 0, axis_index_groups=groups, tiled=True)  26.6 us
    pallas_call x1, Pallas kernels, bottom(): pl.pallas_call(functools.partial(bottom_kernel, chunk, part), grid=(store...  13.5 us
    ppermute x6, starting transfers between devices, partner(): lax.ppermute(x, axis, [(i, i ^ flip) for i in range(lax.axis_size(axis))])  9.6 us
    ppermute x6, waiting for transfers between devices, partner(): lax.ppermute(x, axis, [(i, i ^ flip) for i in range(lax.axis_size(axis))])  8.66 us
    all_to_all x1, starting transfers between devices, exchange(): return lax.all_to_all(x, axis, 0, 0, axis_index_groups=groups, tiled=True)  8.2 us
    all_to_all x1, waiting for transfers between devices, exchange(): return lax.all_to_all(x, axis, 0, 0, axis_index_groups=groups, tiled=True)  2.33 us
  transfers between devices with their start and end apart: 7, of which 6 were waited for; matrix products, arithmetic and copies ran while one was open for 0% of the time, Pallas kernels for 1%

profile of v6, /device:TPU:1, one launch (start us, length us, event | category | flops | bytes accessed | tf_op | source)
XLA Modules:
  0.0 73.1 jit_solution(1342458744866658564)
XLA Ops:
  0.6 0.0 copy-start
  0.6 0.0 copy-start.1
  0.7 0.0 copy-start.2
  0.7 13.5 %bottom.1 = (f32[8,72,128]{2,1,0:T(8,128)S(1)}, f32[8,72,128]{2,1,0:T(8,128)S(1)}, f32[24,512]{1,0:T(8,128)S(1)}, f32[24,128]{1,0:T(8,128)S(1)}, f32[1536,128]{1,0:T(8,128)S(1)}) custom-call(bf16[256,24,512]{2,1,0:T(8,128)(2,1)} %h_ref.1, bf16[512,512]{1,0:T(8,128)(2,1)} %w1_ref.3, bf16[512,512]{1,0:T(8,128)(2,1)} %w2_ref.3, bf16[28,512]{1,0:T(8,128)(2,1)} %bitcast.3), custom_call_target="tpu_custom_call" | custom-call | flops 7247757312 | bytes 6291456 | tf_op jit(solution)/shard_map/bottom/pallas_call | solution.py:128
  14.2 2.1 %collective-permute-start = (f32[8,72,128]{2,1,0:T(8,128)S(1)}, f32[8,72,128]{2,1,0:T(8,128)S(1)}, u32[]{:S(2)}, u32[]{:S(2)}) collective-permute-start(f32[8,72,128]{2,1,0:T(8,128)S(1)} %get-tuple-element.17), channel_id=1, source_target_pairs={{0,1},{1,0},{2,3},{3,2},{4,5},{5,4},{6,7},{7,6},{8,9},{9,8},{10,11... | collective-permute-start | bytes 884744 | tf_op jit(solution)/shard_map/ppermute | solution.py:324
  16.3 1.3 %collective-permute-start.1 = (f32[24,512]{1,0:T(8,128)S(1)}, f32[24,512]{1,0:T(8,128)S(1)}, u32[]{:S(2)}, u32[]{:S(2)}) collective-permute-start(f32[24,512]{1,0:T(8,128)S(1)} %get-tuple-element.18), channel_id=1, source_target_pairs={{0,16},{16,0},{32,48},{48,32},{64,80},{80,64},{96,112},{112,96},{1... | collective-permute-start | bytes 147464 | tf_op jit(solution)/shard_map/ppermute | solution.py:324
  17.6 0.9 %collective-permute-done.1 = f32[24,512]{1,0:T(8,128)S(1)} collective-permute-done((f32[24,512]{1,0:T(8,128)S(1)}, f32[24,512]{1,0:T(8,128)S(1)}, u32[]{:S(2)}, u32[]{:S(2)}) %collective-permute-start.1) | collective-permute-done | bytes 49184 | tf_op jit(solution)/shard_map/ppermute | solution.py:324
  18.5 2.2 %collective-permute-start.2 = (f32[24,512]{1,0:T(8,128)S(1)}, f32[24,512]{1,0:T(8,128)S(1)}, u32[]{:S(2)}, u32[]{:S(2)}) collective-permute-start(f32[24,512]{1,0:T(8,128)S(1)} %add.18), channel_id=1, source_target_pairs={{0,32},{16,48},{32,0},{48,16},{64,96},{80,112},{96,64},{112,80},{1... | collective-permute-start | bytes 147464 | tf_op jit(solution)/shard_map/ppermute | solution.py:324
  20.7 0.7 arrange.1.base_ref
  21.4 4.5 %collective-permute-done.2 = f32[24,512]{1,0:T(8,128)S(1)} collective-permute-done((f32[24,512]{1,0:T(8,128)S(1)}, f32[24,512]{1,0:T(8,128)S(1)}, u32[]{:S(2)}, u32[]{:S(2)}) %collective-permute-start.2) | collective-permute-done | bytes 49184 | tf_op jit(solution)/shard_map/ppermute | solution.py:324
  25.9 0.0 collective-permute-done
  25.9 0.7 %add.20 = f32[8,72,128]{2,1,0:T(8,128)} add(f32[8,72,128]{2,1,0:T(8,128)S(1)} %get-tuple-element.21, f32[8,72,128]{2,1,0:T(8,128)S(1)} %collective-permute-done) | non-fusion elementwise | flops 73728 | bytes 884736 | tf_op jit(solution)/shard_map/add | solution.py:350
  26.7 8.2 %all-to-all-start = ((f32[8,72,128]{2,1,0:T(8,128)}), f32[8,72,128]{2,1,0:T(8,128)S(1)}, u32[]{:S(2)}, u32[]{:S(2)}) async-start(f32[8,72,128]{2,1,0:T(8,128)} %add.20), calls=%async_computation | async-start | bytes 589824 | tf_op jit(solution)/shard_map/all_to_all | solution.py:320
  34.9 2.7 %collective-permute-start.5 = (f32[24,512]{1,0:T(8,128)S(1)}, f32[24,512]{1,0:T(8,128)S(1)}, u32[]{:S(2)}, u32[]{:S(2)}) collective-permute-start(f32[24,512]{1,0:T(8,128)S(1)} %add.19), channel_id=1, source_target_pairs={{0,192},{16,208},{32,224},{48,240},{64,128},{80,144},{96,160},{112... | collective-permute-start | bytes 147464 | tf_op jit(solution)/shard_map/ppermute | solution.py:324
  37.6 0.0 collective-permute-start.4
  37.6 1.3 %collective-permute-start.3 = (f32[24,512]{1,0:T(8,128)S(1)}, f32[24,512]{1,0:T(8,128)S(1)}, u32[]{:S(2)}, u32[]{:S(2)}) collective-permute-start(f32[24,512]{1,0:T(8,128)S(1)} %add.19), channel_id=1, source_target_pairs={{0,128},{16,144},{32,160},{48,176},{64,192},{80,208},{96,224},{112... | collective-permute-start | bytes 147464 | tf_op jit(solution)/shard_map/ppermute | solution.py:324
  38.9 0.2 collective-permute-done.5
  39.1 1.8 %collective-permute-done.4 = f32[24,512]{1,0:T(8,128)S(1)} collective-permute-done((f32[24,512]{1,0:T(8,128)S(1)}, f32[24,512]{1,0:T(8,128)S(1)}, u32[]{:S(2)}, u32[]{:S(2)}) %collective-permute-start.4) | collective-permute-done | bytes 49184 | tf_op jit(solution)/shard_map/ppermute | solution.py:324
  40.8 1.3 %collective-permute-done.3 = f32[24,512]{1,0:T(8,128)S(1)} collective-permute-done((f32[24,512]{1,0:T(8,128)S(1)}, f32[24,512]{1,0:T(8,128)S(1)}, u32[]{:S(2)}, u32[]{:S(2)}) %collective-permute-start.3) | collective-permute-done | bytes 49184 | tf_op jit(solution)/shard_map/ppermute | solution.py:324
  42.1 2.3 %all-to-all-done.s_ref = f32[8,72,128]{2,1,0:T(8,128)S(1)} async-done(((f32[8,72,128]{2,1,0:T(8,128)}), f32[8,72,128]{2,1,0:T(8,128)S(1)}, u32[]{:S(2)}, u32[]{:S(2)}) %all-to-all-start) | async-done | bytes 294944 | tf_op jit(solution)/shard_map/all_to_all | solution.py:320
  44.5 0.0 copy-done
  44.5 0.0 copy-done.1
  44.5 0.0 copy-done.2
  44.5 0.6 totals.1
  45.1 15.8 %all_to_all.15.got_ref.one_ref = f32[16,8,128]{2,1,0:T(8,128)S(1)} all-to-all(f32[16,8,128]{2,1,0:T(8,128)S(1)} %get-tuple-element.26), channel_id=1, replica_groups=mesh['store'=16,'dept'=16] {'store'}, dimensions={0} | all-to-all | bytes 131072 | tf_op jit(solution)/shard_map/all_to_all | solution.py:320
  60.9 10.8 %all_to_all.16.two_ref = f32[16,8,128]{2,1,0:T(8,128)S(1)} all-to-all(f32[16,8,128]{2,1,0:T(8,128)S(1)} %middle.1), channel_id=1, replica_groups=mesh['store'=16,'dept'=16] {'dept'}, dimensions={0} | all-to-all | bytes 131072 | tf_op jit(solution)/shard_map/all_to_all | solution.py:320
  71.7 1.4 %final.1 = (f32[672,256]{1,0:T(8,128)}, f32[28,256]{1,0:T(8,128)}, f32[24,28]{1,0:T(8,128)}) custom-call(f32[672,256]{1,0:T(8,128)S(1)} %arrange.1.base_ref, f32[24,128]{1,0:T(8,128)S(1)} %get-tuple-element.25.item_ref, f32[16,8,128]{2,1,0:T(8,128)S(1)} %all_to_all.15.got_ref.one_ref, f32[16,8,128]{2,1,0:T(8,128)S(1)} %all_to_all.16.two_ref), custom_call_target="tpu_custom_call" | custom-call | tf_op jit(solution)/shard_map/final/pallas_call | solution.py:304
  (4 shorter events, 0.1 us)
Async XLA Ops:
  0.6 43.8 %copy-start = (bf16[512,512]{1,0:T(8,128)(2,1)S(1)}, bf16[512,512]{1,0:T(8,128)(2,1)}, u32[]{:S(2)}) copy-start(bf16[512,512]{1,0:T(8,128)(2,1)} %w1_ref.3) | copy-start | bytes 1572868
  0.6 43.8 %copy-start.1 = (bf16[512,512]{1,0:T(8,128)(2,1)S(1)}, bf16[512,512]{1,0:T(8,128)(2,1)}, u32[]{:S(2)}) copy-start(bf16[512,512]{1,0:T(8,128)(2,1)} %w2_ref.3) | copy-start | bytes 1572868
  0.7 43.8 %copy-start.2 = (bf16[512,28]{0,1:T(8,128)(2,1)S(1)}, bf16[512,28]{0,1:T(8,128)(2,1)}, u32[]{:S(2)}) copy-start(bf16[512,28]{0,1:T(8,128)(2,1)} %param.7) | copy-start | bytes 86020
  14.2 11.7 %collective-permute-start = (f32[8,72,128]{2,1,0:T(8,128)S(1)}, f32[8,72,128]{2,1,0:T(8,128)S(1)}, u32[]{:S(2)}, u32[]{:S(2)}) collective-permute-start(f32[8,72,128]{2,1,0:T(8,128)S(1)} %get-tuple-element.17), channel_id=1, source_target_pairs={{0,1},{1,0},{2,3},{3,2},{4,5},{5,4},{6,7},{7,6},{8,9},{9,8},{10,11... | collective-permute-start | bytes 884744 | tf_op jit(solution)/shard_map/ppermute | solution.py:324
  16.3 2.2 %collective-permute-start.1 = (f32[24,512]{1,0:T(8,128)S(1)}, f32[24,512]{1,0:T(8,128)S(1)}, u32[]{:S(2)}, u32[]{:S(2)}) collective-permute-start(f32[24,512]{1,0:T(8,128)S(1)} %get-tuple-element.18), channel_id=1, source_target_pairs={{0,16},{16,0},{32,48},{48,32},{64,80},{80,64},{96,112},{112,96},{1... | collective-permute-start | bytes 147464 | tf_op jit(solution)/shard_map/ppermute | solution.py:324
  18.5 7.4 %collective-permute-start.2 = (f32[24,512]{1,0:T(8,128)S(1)}, f32[24,512]{1,0:T(8,128)S(1)}, u32[]{:S(2)}, u32[]{:S(2)}) collective-permute-start(f32[24,512]{1,0:T(8,128)S(1)} %add.18), channel_id=1, source_target_pairs={{0,32},{16,48},{32,0},{48,16},{64,96},{80,112},{96,64},{112,80},{1... | collective-permute-start | bytes 147464 | tf_op jit(solution)/shard_map/ppermute | solution.py:324
  26.7 17.8 %all-to-all-start = ((f32[8,72,128]{2,1,0:T(8,128)}), f32[8,72,128]{2,1,0:T(8,128)S(1)}, u32[]{:S(2)}, u32[]{:S(2)}) async-start(f32[8,72,128]{2,1,0:T(8,128)} %add.20), calls=%async_computation | async-start | bytes 589824 | tf_op jit(solution)/shard_map/all_to_all | solution.py:320
  34.9 4.2 %collective-permute-start.5 = (f32[24,512]{1,0:T(8,128)S(1)}, f32[24,512]{1,0:T(8,128)S(1)}, u32[]{:S(2)}, u32[]{:S(2)}) collective-permute-start(f32[24,512]{1,0:T(8,128)S(1)} %add.19), channel_id=1, source_target_pairs={{0,192},{16,208},{32,224},{48,240},{64,128},{80,144},{96,160},{112... | collective-permute-start | bytes 147464 | tf_op jit(solution)/shard_map/ppermute | solution.py:324
  37.6 3.2 %collective-permute-start.4 = (f32[24,512]{1,0:T(8,128)S(1)}, f32[24,512]{1,0:T(8,128)S(1)}, u32[]{:S(2)}, u32[]{:S(2)}) collective-permute-start(f32[24,512]{1,0:T(8,128)S(1)} %add.19), channel_id=1, source_target_pairs={{0,64},{16,80},{32,96},{48,112},{64,0},{80,16},{96,32},{112,48},{1... | collective-permute-start | bytes 147464 | tf_op jit(solution)/shard_map/ppermute | solution.py:324
  37.6 4.5 %collective-permute-start.3 = (f32[24,512]{1,0:T(8,128)S(1)}, f32[24,512]{1,0:T(8,128)S(1)}, u32[]{:S(2)}, u32[]{:S(2)}) collective-permute-start(f32[24,512]{1,0:T(8,128)S(1)} %add.19), channel_id=1, source_target_pairs={{0,128},{16,144},{32,160},{48,176},{64,192},{80,208},{96,224},{112... | collective-permute-start | bytes 147464 | tf_op jit(solution)/shard_map/ppermute | solution.py:324

commit v7 on v6

--- a/solution.py
+++ b/solution.py
@@ -324,11 +324,6 @@
     return lax.ppermute(x, axis, [(i, i ^ flip) for i in range(lax.axis_size(axis))])
 
 
-def add_over_x(x):
-    x = x + partner(x, "store", 1)
-    return x + partner(x, "store", 2)
-
-
 def add_over_y(x):
     near, far, across = (partner(x, "store", flip) for flip in (4, 12, 8))
     return (x + across) + (near + far)
@@ -343,12 +338,12 @@
 
     keep, send, item_part, col, y = bottom(history, w1, w2, w3, n_dept, stores // 4, stores // 8)
     came = partner(send, "dept", 1)
-    item_hist = add_over_x(item_part)
+    item_hist = add_over_y(item_part + partner(item_part, "store", 1))
     base = arrange(y, items, horizon)
     came, item_hist, base = lax.optimization_barrier((came, item_hist, base))
     along_z = [list(range(k, n_dept, 2)) for k in range(2)]
     store_parts = exchange(keep + came, "dept", along_z)
-    item_hist = add_over_y(item_hist)
+    item_hist = item_hist + partner(item_hist, "store", 2)
     err, item_fc, pay_one = totals(store_parts, item_hist, w1, w2, w3, col, chunk, n_store)
     one = exchange(pay_one, "store")
     pay_two = middle(err, one, chunk, items, n_dept)

time: 73.3 us -> 73.7 us (level)
  blocking collectives: 26.6 us -> 28.5 us
  starting transfers between devices: 17.8 us -> 16.5 us
    ppermute x6, waiting for transfers between devices: 8.66 us -> 5.58 us  [partner(): lax.ppermute(x, axis, [(i, i ^ flip) for i in range(lax.axis_size(axis))])]
    all_to_all x1, waiting for transfers between devices: 2.33 us -> 5.12 us  [exchange(): return lax.all_to_all(x, axis, 0, 0, axis_index_groups=groups, tiled=True)]
    all_to_all x2, blocking collectives: 26.6 us -> 28.5 us  [exchange(): return lax.all_to_all(x, axis, 0, 0, axis_index_groups=groups, tiled=True)]
    all_to_all x1, starting transfers between devices: 8.2 us -> 6.44 us  [exchange(): return lax.all_to_all(x, axis, 0, 0, axis_index_groups=groups, tiled=True)]
  transfers between devices with their start and end apart: 7 -> 7, of which waited for: 6 -> 5; matrix products, arithmetic and copies ran while one was open for 0% -> 0% of each run, Pallas kernels for 1% -> 1%
where the time goes in v7:
time: 73.7 us; the launch traced here: 73.4 us
  blocking collectives  28.5 us (39%)
  starting transfers between devices  16.5 us (22%)
  Pallas kernels  16.2 us (22%)
  waiting for transfers between devices  10.7 us (15%)
  other arithmetic  0.78 us (1%)
    all_to_all x2, blocking collectives, exchange(): return lax.all_to_all(x, axis, 0, 0, axis_index_groups=groups, tiled=True)  28.5 us
    pallas_call x1, Pallas kernels, bottom(): pl.pallas_call(functools.partial(bottom_kernel, chunk, part), grid=(store...  13.5 us
    ppermute x6, starting transfers between devices, partner(): lax.ppermute(x, axis, [(i, i ^ flip) for i in range(lax.axis_size(axis))])  10 us
    all_to_all x1, starting transfers between devices, exchange(): return lax.all_to_all(x, axis, 0, 0, axis_index_groups=groups, tiled=True)  6.44 us
    ppermute x6, waiting for transfers between devices, partner(): lax.ppermute(x, axis, [(i, i ^ flip) for i in range(lax.axis_size(axis))])  5.58 us
    all_to_all x1, waiting for transfers between devices, exchange(): return lax.all_to_all(x, axis, 0, 0, axis_index_groups=groups, tiled=True)  5.12 us
  transfers between devices with their start and end apart: 7, of which 5 were waited for; matrix products, arithmetic and copies ran while one was open for 0% of the time, Pallas kernels for 1%

profile of v7, /device:TPU:1, one launch (start us, length us, event | category | flops | bytes accessed | tf_op | source)
XLA Modules:
  0.0 73.4 jit_solution(4867383717495805311)
XLA Ops:
  0.6 0.0 copy-start
  0.6 0.0 copy-start.1
  0.7 0.0 copy-start.2
  0.7 13.5 %bottom.1 = (f32[8,72,128]{2,1,0:T(8,128)S(1)}, f32[8,72,128]{2,1,0:T(8,128)S(1)}, f32[24,512]{1,0:T(8,128)S(1)}, f32[24,128]{1,0:T(8,128)S(1)}, f32[1536,128]{1,0:T(8,128)S(1)}) custom-call(bf16[256,24,512]{2,1,0:T(8,128)(2,1)} %h_ref.1, bf16[512,512]{1,0:T(8,128)(2,1)} %w1_ref.3, bf16[512,512]{1,0:T(8,128)(2,1)} %w2_ref.3, bf16[28,512]{1,0:T(8,128)(2,1)} %bitcast.3), custom_call_target="tpu_custom_call" | custom-call | flops 7247757312 | bytes 6291456 | tf_op jit(solution)/shard_map/bottom/pallas_call | solution.py:128
  14.2 3.3 %collective-permute-start.1 = (f32[24,512]{1,0:T(8,128)S(1)}, f32[24,512]{1,0:T(8,128)S(1)}, u32[]{:S(2)}, u32[]{:S(2)}) collective-permute-start(f32[24,512]{1,0:T(8,128)S(1)} %get-tuple-element.18), channel_id=1, source_target_pairs={{0,16},{16,0},{32,48},{48,32},{64,80},{80,64},{96,112},{112,96},{1... | collective-permute-start | bytes 147464 | tf_op jit(solution)/shard_map/ppermute | solution.py:324
  17.5 0.0 collective-permute-start
  17.5 0.9 %collective-permute-done.1 = f32[24,512]{1,0:T(8,128)S(1)} collective-permute-done((f32[24,512]{1,0:T(8,128)S(1)}, f32[24,512]{1,0:T(8,128)S(1)}, u32[]{:S(2)}, u32[]{:S(2)}) %collective-permute-start.1) | collective-permute-done | bytes 49184 | tf_op jit(solution)/shard_map/ppermute | solution.py:324
  18.4 1.4 %collective-permute-start.4 = (f32[24,512]{1,0:T(8,128)S(1)}, f32[24,512]{1,0:T(8,128)S(1)}, u32[]{:S(2)}, u32[]{:S(2)}) collective-permute-start(f32[24,512]{1,0:T(8,128)S(1)} %add.18), channel_id=1, source_target_pairs={{0,192},{16,208},{32,224},{48,240},{64,128},{80,144},{96,160},{112... | collective-permute-start | bytes 147464 | tf_op jit(solution)/shard_map/ppermute | solution.py:324
  19.8 0.0 collective-permute-start.3
  19.8 2.5 %collective-permute-start.2 = (f32[24,512]{1,0:T(8,128)S(1)}, f32[24,512]{1,0:T(8,128)S(1)}, u32[]{:S(2)}, u32[]{:S(2)}) collective-permute-start(f32[24,512]{1,0:T(8,128)S(1)} %add.18), channel_id=1, source_target_pairs={{0,128},{16,144},{32,160},{48,176},{64,192},{80,208},{96,224},{112... | collective-permute-start | bytes 147464 | tf_op jit(solution)/shard_map/ppermute | solution.py:324
  22.3 0.7 arrange.1.base_ref
  23.0 0.0 collective-permute-done.4
  23.0 0.0 collective-permute-done.3
  23.1 1.3 %collective-permute-done.2 = f32[24,512]{1,0:T(8,128)S(1)} collective-permute-done((f32[24,512]{1,0:T(8,128)S(1)}, f32[24,512]{1,0:T(8,128)S(1)}, u32[]{:S(2)}, u32[]{:S(2)}) %collective-permute-start.2) | collective-permute-done | bytes 49184 | tf_op jit(solution)/shard_map/ppermute | solution.py:324
  24.4 1.7 %collective-permute-done = f32[8,72,128]{2,1,0:T(8,128)S(1)} collective-permute-done((f32[8,72,128]{2,1,0:T(8,128)S(1)}, f32[8,72,128]{2,1,0:T(8,128)S(1)}, u32[]{:S(2)}, u32[]{:S(2)}) %collective-permute-start) | collective-permute-done | bytes 294944 | tf_op jit(solution)/shard_map/ppermute | solution.py:324
  26.1 0.7 %add.22 = f32[8,72,128]{2,1,0:T(8,128)} add(f32[8,72,128]{2,1,0:T(8,128)S(1)} %get-tuple-element.21, f32[8,72,128]{2,1,0:T(8,128)S(1)} %collective-permute-done) | non-fusion elementwise | flops 73728 | bytes 884736 | tf_op jit(solution)/shard_map/add | solution.py:345
  26.8 6.4 %all-to-all-start = ((f32[8,72,128]{2,1,0:T(8,128)}), f32[8,72,128]{2,1,0:T(8,128)S(1)}, u32[]{:S(2)}, u32[]{:S(2)}) async-start(f32[8,72,128]{2,1,0:T(8,128)} %add.22), calls=%async_computation | async-start | bytes 589824 | tf_op jit(solution)/shard_map/all_to_all | solution.py:320
  33.3 2.7 %collective-permute-start.5 = (f32[24,512]{1,0:T(8,128)S(1)}, f32[24,512]{1,0:T(8,128)S(1)}, u32[]{:S(2)}, u32[]{:S(2)}) collective-permute-start(f32[24,512]{1,0:T(8,128)S(1)} %add_add_fusion), channel_id=1, source_target_pairs={{0,32},{16,48},{32,0},{48,16},{64,96},{80,112},{96,64},{112,80},{1... | collective-permute-start | bytes 147464 | tf_op jit(solution)/shard_map/ppermute | solution.py:324
  36.0 1.7 %collective-permute-done.5 = f32[24,512]{1,0:T(8,128)S(1)} collective-permute-done((f32[24,512]{1,0:T(8,128)S(1)}, f32[24,512]{1,0:T(8,128)S(1)}, u32[]{:S(2)}, u32[]{:S(2)}) %collective-permute-start.5) | collective-permute-done | bytes 49184 | tf_op jit(solution)/shard_map/ppermute | solution.py:324
  37.7 5.1 %all-to-all-done.s_ref = f32[8,72,128]{2,1,0:T(8,128)S(1)} async-done(((f32[8,72,128]{2,1,0:T(8,128)}), f32[8,72,128]{2,1,0:T(8,128)S(1)}, u32[]{:S(2)}, u32[]{:S(2)}) %all-to-all-start) | async-done | bytes 294944 | tf_op jit(solution)/shard_map/all_to_all | solution.py:320
  42.8 0.0 copy-done
  42.8 0.0 copy-done.1
  42.8 0.0 copy-done.2
  42.8 0.6 totals.1
  43.5 18.0 %all_to_all.15.got_ref.one_ref = f32[16,8,128]{2,1,0:T(8,128)S(1)} all-to-all(f32[16,8,128]{2,1,0:T(8,128)S(1)} %get-tuple-element.26), channel_id=1, replica_groups=mesh['store'=16,'dept'=16] {'store'}, dimensions={0} | all-to-all | bytes 131072 | tf_op jit(solution)/shard_map/all_to_all | solution.py:320
  61.5 10.5 %all_to_all.16.two_ref = f32[16,8,128]{2,1,0:T(8,128)S(1)} all-to-all(f32[16,8,128]{2,1,0:T(8,128)S(1)} %middle.1), channel_id=1, replica_groups=mesh['store'=16,'dept'=16] {'dept'}, dimensions={0} | all-to-all | bytes 131072 | tf_op jit(solution)/shard_map/all_to_all | solution.py:320
  72.1 1.4 %final.1 = (f32[672,256]{1,0:T(8,128)}, f32[28,256]{1,0:T(8,128)}, f32[24,28]{1,0:T(8,128)}) custom-call(f32[672,256]{1,0:T(8,128)S(1)} %arrange.1.base_ref, f32[24,128]{1,0:T(8,128)S(1)} %get-tuple-element.25.item_ref, f32[16,8,128]{2,1,0:T(8,128)S(1)} %all_to_all.15.got_ref.one_ref, f32[16,8,128]{2,1,0:T(8,128)S(1)} %all_to_all.16.two_ref), custom_call_target="tpu_custom_call" | custom-call | tf_op jit(solution)/shard_map/final/pallas_call | solution.py:304
  (4 shorter events, 0.1 us)
Async XLA Ops:
  0.6 42.2 %copy-start = (bf16[512,512]{1,0:T(8,128)(2,1)S(1)}, bf16[512,512]{1,0:T(8,128)(2,1)}, u32[]{:S(2)}) copy-start(bf16[512,512]{1,0:T(8,128)(2,1)} %w1_ref.3) | copy-start | bytes 1572868
  0.6 42.2 %copy-start.1 = (bf16[512,512]{1,0:T(8,128)(2,1)S(1)}, bf16[512,512]{1,0:T(8,128)(2,1)}, u32[]{:S(2)}) copy-start(bf16[512,512]{1,0:T(8,128)(2,1)} %w2_ref.3) | copy-start | bytes 1572868
  0.7 42.2 %copy-start.2 = (bf16[512,28]{0,1:T(8,128)(2,1)S(1)}, bf16[512,28]{0,1:T(8,128)(2,1)}, u32[]{:S(2)}) copy-start(bf16[512,28]{0,1:T(8,128)(2,1)} %param.7) | copy-start | bytes 86020
  14.2 4.2 %collective-permute-start.1 = (f32[24,512]{1,0:T(8,128)S(1)}, f32[24,512]{1,0:T(8,128)S(1)}, u32[]{:S(2)}, u32[]{:S(2)}) collective-permute-start(f32[24,512]{1,0:T(8,128)S(1)} %get-tuple-element.18), channel_id=1, source_target_pairs={{0,16},{16,0},{32,48},{48,32},{64,80},{80,64},{96,112},{112,96},{1... | collective-permute-start | bytes 147464 | tf_op jit(solution)/shard_map/ppermute | solution.py:324
  17.5 8.6 %collective-permute-start = (f32[8,72,128]{2,1,0:T(8,128)S(1)}, f32[8,72,128]{2,1,0:T(8,128)S(1)}, u32[]{:S(2)}, u32[]{:S(2)}) collective-permute-start(f32[8,72,128]{2,1,0:T(8,128)S(1)} %get-tuple-element.17), channel_id=1, source_target_pairs={{0,1},{1,0},{2,3},{3,2},{4,5},{5,4},{6,7},{7,6},{8,9},{9,8},{10,11... | collective-permute-start | bytes 884744 | tf_op jit(solution)/shard_map/ppermute | solution.py:324
  18.4 4.6 %collective-permute-start.4 = (f32[24,512]{1,0:T(8,128)S(1)}, f32[24,512]{1,0:T(8,128)S(1)}, u32[]{:S(2)}, u32[]{:S(2)}) collective-permute-start(f32[24,512]{1,0:T(8,128)S(1)} %add.18), channel_id=1, source_target_pairs={{0,192},{16,208},{32,224},{48,240},{64,128},{80,144},{96,160},{112... | collective-permute-start | bytes 147464 | tf_op jit(solution)/shard_map/ppermute | solution.py:324
  19.8 3.2 %collective-permute-start.3 = (f32[24,512]{1,0:T(8,128)S(1)}, f32[24,512]{1,0:T(8,128)S(1)}, u32[]{:S(2)}, u32[]{:S(2)}) collective-permute-start(f32[24,512]{1,0:T(8,128)S(1)} %add.18), channel_id=1, source_target_pairs={{0,64},{16,80},{32,96},{48,112},{64,0},{80,16},{96,32},{112,48},{1... | collective-permute-start | bytes 147464 | tf_op jit(solution)/shard_map/ppermute | solution.py:324
  19.8 4.5 %collective-permute-start.2 = (f32[24,512]{1,0:T(8,128)S(1)}, f32[24,512]{1,0:T(8,128)S(1)}, u32[]{:S(2)}, u32[]{:S(2)}) collective-permute-start(f32[24,512]{1,0:T(8,128)S(1)} %add.18), channel_id=1, source_target_pairs={{0,128},{16,144},{32,160},{48,176},{64,192},{80,208},{96,224},{112... | collective-permute-start | bytes 147464 | tf_op jit(solution)/shard_map/ppermute | solution.py:324
  26.8 16.0 %all-to-all-start = ((f32[8,72,128]{2,1,0:T(8,128)}), f32[8,72,128]{2,1,0:T(8,128)S(1)}, u32[]{:S(2)}, u32[]{:S(2)}) async-start(f32[8,72,128]{2,1,0:T(8,128)} %add.22), calls=%async_computation | async-start | bytes 589824 | tf_op jit(solution)/shard_map/all_to_all | solution.py:320
  33.3 4.4 %collective-permute-start.5 = (f32[24,512]{1,0:T(8,128)S(1)}, f32[24,512]{1,0:T(8,128)S(1)}, u32[]{:S(2)}, u32[]{:S(2)}) collective-permute-start(f32[24,512]{1,0:T(8,128)S(1)} %add_add_fusion), channel_id=1, source_target_pairs={{0,32},{16,48},{32,0},{48,16},{64,96},{80,112},{96,64},{112,80},{1... | collective-permute-start | bytes 147464 | tf_op jit(solution)/shard_map/ppermute | solution.py:324

commit v8 on v5

--- a/solution.py
+++ b/solution.py
@@ -13,6 +13,7 @@
 LANES = 128
 GROUP = 32
 MIB = 1024 * 1024
+PIECES = 3
 
 
 def whole(n):
@@ -73,7 +74,7 @@
     return out
 
 
-def bottom_kernel(chunk, part, h_ref, w1_ref, w2_ref, w3_ref, pay_ref, item_ref, col_ref, y_ref, w3_wide):
+def bottom_kernel(chunk, part, h_ref, w1_ref, w2_ref, w3_ref, pay_ref, item_ref, col_ref, y_ref, w1_out, w2_out, w3_wide):
     block, items, days = h_ref.shape
     step = pl.program_id(0)
 
@@ -83,6 +84,8 @@
         item_ref[...] = jnp.zeros_like(item_ref)
         col_ref[...] = jnp.zeros_like(col_ref)
         y_ref[...] = jnp.zeros_like(y_ref)
+        w1_out[...] = w1_ref[...]
+        w2_out[...] = w2_ref[...]
 
     w1, w2, w3 = w1_ref[...], w2_ref[...], w3_wide[...]
     tiles = days // LANES
@@ -127,12 +130,16 @@
             fixed((items, days)),
             fixed((items, LANES)),
             fixed((block * items, LANES)),
+            fixed(w1.shape),
+            fixed(w2.shape),
         ],
         out_shape=[
             jax.ShapeDtypeStruct((peers, pay_rows, LANES), F32),
             jax.ShapeDtypeStruct((items, days), F32),
             jax.ShapeDtypeStruct((items, LANES), F32),
             jax.ShapeDtypeStruct((block * items, LANES), F32),
+            jax.ShapeDtypeStruct(w1.shape, BF16),
+            jax.ShapeDtypeStruct(w2.shape, BF16),
         ],
         scratch_shapes=[pltpu.VMEM((hid, LANES), BF16)],
         compiler_params=params(24),
@@ -235,7 +242,7 @@
     )(err, got)
 
 
-def final_kernel(horizon, item_count, store_count, base_ref, item_ref, one_ref, two_ref, out_ref, sgap_ref, igap_ref, err_ref):
+def final_kernel(horizon, item_count, store_count, base_ref, item_ref, one_ref, two_ref, out_hbm, sgap_ref, igap_ref, err_ref, out_ref, sem):
     width, stores = base_ref.shape
     items = width // horizon
     peers = two_ref.shape[0]
@@ -277,11 +284,20 @@
 
     a = jnp.concatenate([store_shift, store_shift], axis=0)
     b = jnp.concatenate([columns, pltpu.roll(columns, LANES - 1, axis=1)], axis=0)
+    each = items // 2 // PIECES
+    copies = []
     for j in range(items // 2):
         rows = slice(2 * j * horizon, (2 * j + 2) * horizon)
         out_ref[rows, :] = base_ref[rows, :] + a + b[:, 2 * j : 2 * j + 1]
+        if (j + 1) % each == 0:
+            piece = pl.ds((j + 1 - each) * 2 * horizon, each * 2 * horizon)
+            copy = pltpu.make_async_copy(out_ref.at[piece], out_hbm.at[piece], sem.at[j // each])
+            copy.start()
+            copies.append(copy)
     sgap_ref[...] = store_err * (1.0 / math.sqrt(item_count))
     igap_ref[...] = item_err[:, :horizon] * (1.0 / math.sqrt(store_count))
+    for copy in copies:
+        copy.wait()
 
 
 def final(base, item_fc, one, two, horizon, item_count, store_count):
@@ -290,13 +306,17 @@
     return pl.pallas_call(
         functools.partial(final_kernel, horizon, item_count, store_count),
         in_specs=whole(4),
-        out_specs=whole(3),
+        out_specs=[pl.BlockSpec(memory_space=pltpu.HBM)] + whole(2),
         out_shape=[
-            jax.ShapeDtypeStruct((width, stores), F32),
+            pltpu.HBM((width, stores), F32),
             jax.ShapeDtypeStruct((horizon, stores), F32),
             jax.ShapeDtypeStruct((items, horizon), F32),
         ],
-        scratch_shapes=[pltpu.VMEM((stores, LANES), F32)],
+        scratch_shapes=[
+            pltpu.VMEM((stores, LANES), F32),
+            pltpu.VMEM((width, stores), F32),
+            pltpu.SemaphoreType.DMA((PIECES,)),
+        ],
         compiler_params=params(6),
         name="final",
     )(base, item_fc, one, two)
@@ -327,13 +347,13 @@
     chunk = stores // n_dept
     w3 = final_layer_matrix.T
 
-    pay, item_part, col, y = bottom(history, w1, w2, w3, n_dept, stores // 4, stores // 8)
+    pay, item_part, col, y, w1_near, w2_near = bottom(history, w1, w2, w3, n_dept, stores // 4, stores // 8)
     store_parts = exchange(pay, "dept")
     item_hist = add_over_x(item_part)
     base = arrange(y, items, horizon)
     base, item_hist = lax.optimization_barrier((base, item_hist))
     item_hist = add_over_y(item_hist)
-    err, item_fc, pay_one = totals(store_parts, item_hist, w1, w2, w3, col, chunk, n_store)
+    err, item_fc, pay_one = totals(store_parts, item_hist, w1_near, w2_near, w3, col, chunk, n_store)
     one = exchange(pay_one, "store")
     pay_two = middle(err, one, chunk, items, n_dept)
     two = exchange(pay_two, "dept")

time: 71.4 us -> 72 us (level)
  no operation moved by 1% of the time
where the time goes in v8:
time: 72 us; the launch traced here: 71.7 us
  blocking collectives  27.4 us (38%)
  starting transfers between devices  17.7 us (25%)
  Pallas kernels  17.4 us (24%)
  waiting for transfers between devices  8.49 us (12%)
    all_to_all x2, blocking collectives, exchange(): return lax.all_to_all(x, axis, 0, 0, tiled=True)  27.4 us
    pallas_call x1, Pallas kernels, bottom(): pl.pallas_call(functools.partial(bottom_kernel, chunk, part), grid=(store...  14.1 us
    all_to_all x1, starting transfers between devices, exchange(): return lax.all_to_all(x, axis, 0, 0, tiled=True)  10.1 us
    ppermute x5, starting transfers between devices, partner(): lax.ppermute(x, axis, [(i, i ^ flip) for i in range(lax.axis_size(axis))])  7.68 us
    ppermute x5, waiting for transfers between devices, partner(): lax.ppermute(x, axis, [(i, i ^ flip) for i in range(lax.axis_size(axis))])  5.63 us
    all_to_all x1, waiting for transfers between devices, exchange(): return lax.all_to_all(x, axis, 0, 0, tiled=True)  2.86 us
    pallas_call x1, Pallas kernels, final(): pl.pallas_call(functools.partial(final_kernel, horizon, item_count, store...  1.95 us
  transfers between devices with their start and end apart: 6, of which 6 were waited for; matrix products, arithmetic and copies ran while one was open for 0% of the time, Pallas kernels for 1%

profile of v8, /device:TPU:1, one launch (start us, length us, event | category | flops | bytes accessed | tf_op | source)
XLA Modules:
  0.0 71.7 jit_solution(15011813965638209548)
XLA Ops:
  0.6 0.0 copy-start
  0.6 14.1 %bottom.1 = (f32[16,72,128]{2,1,0:T(8,128)}, f32[24,512]{1,0:T(8,128)S(1)}, f32[24,128]{1,0:T(8,128)S(1)}, f32[1536,128]{1,0:T(8,128)S(1)}, bf16[512,512]{1,0:T(8,128)(2,1)S(1)}, /*index=5*/bf16[512,512]{1,0:T(8,128)(2,1)S(1)}) custom-call(bf16[256,24,512]{2,1,0:T(8,128)(2,1)} %h_ref.1, bf16[512,512]{1,0:T(8,128)(2,1)} %w1_ref.1, bf16[512,512]{1,0:T(8,128)(2,1)} %w2_ref.1, ...), custom_call_target="tpu_custom_call" | custom-call | flops 7247757312 | bytes 6291456 | tf_op jit(solution)/shard_map/bottom/pallas_call | solution.py:119
  14.8 10.1 %all-to-all-start = ((f32[16,72,128]{2,1,0:T(8,128)}), f32[16,72,128]{2,1,0:T(8,128)S(1)}, u32[]{:S(2)}, u32[]{:S(2)}) async-start(f32[16,72,128]{2,1,0:T(8,128)} %get-tuple-element.20), calls=%async_computation | async-start | bytes 1179648 | tf_op jit(solution)/shard_map/all_to_all | solution.py:326
  24.8 1.0 %collective-permute-start = (f32[24,512]{1,0:T(8,128)S(1)}, f32[24,512]{1,0:T(8,128)S(1)}, u32[]{:S(2)}, u32[]{:S(2)}) collective-permute-start(f32[24,512]{1,0:T(8,128)S(1)} %get-tuple-element.18), channel_id=1, source_target_pairs={{0,16},{16,0},{32,48},{48,32},{64,80},{80,64},{96,112},{112,96},{1... | collective-permute-start | bytes 147464 | tf_op jit(solution)/shard_map/ppermute | solution.py:330
  25.8 0.9 %collective-permute-done = f32[24,512]{1,0:T(8,128)S(1)} collective-permute-done((f32[24,512]{1,0:T(8,128)S(1)}, f32[24,512]{1,0:T(8,128)S(1)}, u32[]{:S(2)}, u32[]{:S(2)}) %collective-permute-start) | collective-permute-done | bytes 49184 | tf_op jit(solution)/shard_map/ppermute | solution.py:330
  26.7 2.5 %collective-permute-start.1 = (f32[24,512]{1,0:T(8,128)S(1)}, f32[24,512]{1,0:T(8,128)S(1)}, u32[]{:S(2)}, u32[]{:S(2)}) collective-permute-start(f32[24,512]{1,0:T(8,128)S(1)} %add.15), channel_id=1, source_target_pairs={{0,32},{16,48},{32,0},{48,16},{64,96},{80,112},{96,64},{112,80},{1... | collective-permute-start | bytes 147464 | tf_op jit(solution)/shard_map/ppermute | solution.py:330
  29.3 0.7 arrange.1.base_ref
  30.0 1.3 %collective-permute-done.1 = f32[24,512]{1,0:T(8,128)S(1)} collective-permute-done((f32[24,512]{1,0:T(8,128)S(1)}, f32[24,512]{1,0:T(8,128)S(1)}, u32[]{:S(2)}, u32[]{:S(2)}) %collective-permute-start.1) | collective-permute-done | bytes 49184 | tf_op jit(solution)/shard_map/ppermute | solution.py:330
  31.3 2.8 %collective-permute-start.4 = (f32[24,512]{1,0:T(8,128)S(1)}, f32[24,512]{1,0:T(8,128)S(1)}, u32[]{:S(2)}, u32[]{:S(2)}) collective-permute-start(f32[24,512]{1,0:T(8,128)S(1)} %add.16), channel_id=1, source_target_pairs={{0,192},{16,208},{32,224},{48,240},{64,128},{80,144},{96,160},{112... | collective-permute-start | bytes 147464 | tf_op jit(solution)/shard_map/ppermute | solution.py:330
  34.1 0.0 collective-permute-start.3
  34.1 1.3 %collective-permute-start.2 = (f32[24,512]{1,0:T(8,128)S(1)}, f32[24,512]{1,0:T(8,128)S(1)}, u32[]{:S(2)}, u32[]{:S(2)}) collective-permute-start(f32[24,512]{1,0:T(8,128)S(1)} %add.16), channel_id=1, source_target_pairs={{0,128},{16,144},{32,160},{48,176},{64,192},{80,208},{96,224},{112... | collective-permute-start | bytes 147464 | tf_op jit(solution)/shard_map/ppermute | solution.py:330
  35.4 0.5 collective-permute-done.4
  35.9 1.5 %collective-permute-done.3 = f32[24,512]{1,0:T(8,128)S(1)} collective-permute-done((f32[24,512]{1,0:T(8,128)S(1)}, f32[24,512]{1,0:T(8,128)S(1)}, u32[]{:S(2)}, u32[]{:S(2)}) %collective-permute-start.3) | collective-permute-done | bytes 49184 | tf_op jit(solution)/shard_map/ppermute | solution.py:330
  37.3 1.5 %collective-permute-done.2 = f32[24,512]{1,0:T(8,128)S(1)} collective-permute-done((f32[24,512]{1,0:T(8,128)S(1)}, f32[24,512]{1,0:T(8,128)S(1)}, u32[]{:S(2)}, u32[]{:S(2)}) %collective-permute-start.2) | collective-permute-done | bytes 49184 | tf_op jit(solution)/shard_map/ppermute | solution.py:330
  38.9 2.9 %all-to-all-done.s_ref = f32[16,72,128]{2,1,0:T(8,128)S(1)} async-done(((f32[16,72,128]{2,1,0:T(8,128)}), f32[16,72,128]{2,1,0:T(8,128)S(1)}, u32[]{:S(2)}, u32[]{:S(2)}) %all-to-all-start) | async-done | bytes 589856 | tf_op jit(solution)/shard_map/all_to_all | solution.py:326
  41.7 0.0 copy-done
  41.7 0.6 totals.1
  42.4 16.6 %all_to_all.15.got_ref.one_ref = f32[16,8,128]{2,1,0:T(8,128)S(1)} all-to-all(f32[16,8,128]{2,1,0:T(8,128)S(1)} %get-tuple-element.26), channel_id=1, replica_groups=mesh['store'=16,'dept'=16] {'store'}, dimensions={0} | all-to-all | bytes 131072 | tf_op jit(solution)/shard_map/all_to_all | solution.py:326
  59.0 10.8 %all_to_all.16.two_ref = f32[16,8,128]{2,1,0:T(8,128)S(1)} all-to-all(f32[16,8,128]{2,1,0:T(8,128)S(1)} %middle.1), channel_id=1, replica_groups=mesh['store'=16,'dept'=16] {'dept'}, dimensions={0} | all-to-all | bytes 131072 | tf_op jit(solution)/shard_map/all_to_all | solution.py:326
  69.8 1.9 %final.1 = (f32[672,256]{1,0:T(8,128)}, f32[28,256]{1,0:T(8,128)}, f32[24,28]{1,0:T(8,128)}) custom-call(f32[672,256]{1,0:T(8,128)S(1)} %arrange.1.base_ref, f32[24,128]{1,0:T(8,128)S(1)} %get-tuple-element.25.item_ref, f32[16,8,128]{2,1,0:T(8,128)S(1)} %all_to_all.15.got_ref.one_ref, f32[16,8,128]{2,1,0:T(8,128)S(1)} %all_to_all.16.two_ref), custom_call_target="tpu_custom_call" | custom-call | tf_op jit(solution)/shard_map/final/pallas_call | solution.py:306
  (4 shorter events, 0.1 us)
Async XLA Ops:
  0.6 41.1 %copy-start = (bf16[512,28]{0,1:T(8,128)(2,1)S(1)}, bf16[512,28]{0,1:T(8,128)(2,1)}, u32[]{:S(2)}) copy-start(bf16[512,28]{0,1:T(8,128)(2,1)} %param.7) | copy-start | bytes 86020
  14.8 27.0 %all-to-all-start = ((f32[16,72,128]{2,1,0:T(8,128)}), f32[16,72,128]{2,1,0:T(8,128)S(1)}, u32[]{:S(2)}, u32[]{:S(2)}) async-start(f32[16,72,128]{2,1,0:T(8,128)} %get-tuple-element.20), calls=%async_computation | async-start | bytes 1179648 | tf_op jit(solution)/shard_map/all_to_all | solution.py:326
  24.8 1.9 %collective-permute-start = (f32[24,512]{1,0:T(8,128)S(1)}, f32[24,512]{1,0:T(8,128)S(1)}, u32[]{:S(2)}, u32[]{:S(2)}) collective-permute-start(f32[24,512]{1,0:T(8,128)S(1)} %get-tuple-element.18), channel_id=1, source_target_pairs={{0,16},{16,0},{32,48},{48,32},{64,80},{80,64},{96,112},{112,96},{1... | collective-permute-start | bytes 147464 | tf_op jit(solution)/shard_map/ppermute | solution.py:330
  26.7 4.5 %collective-permute-start.1 = (f32[24,512]{1,0:T(8,128)S(1)}, f32[24,512]{1,0:T(8,128)S(1)}, u32[]{:S(2)}, u32[]{:S(2)}) collective-permute-start(f32[24,512]{1,0:T(8,128)S(1)} %add.15), channel_id=1, source_target_pairs={{0,32},{16,48},{32,0},{48,16},{64,96},{80,112},{96,64},{112,80},{1... | collective-permute-start | bytes 147464 | tf_op jit(solution)/shard_map/ppermute | solution.py:330
  31.3 4.6 %collective-permute-start.4 = (f32[24,512]{1,0:T(8,128)S(1)}, f32[24,512]{1,0:T(8,128)S(1)}, u32[]{:S(2)}, u32[]{:S(2)}) collective-permute-start(f32[24,512]{1,0:T(8,128)S(1)} %add.16), channel_id=1, source_target_pairs={{0,192},{16,208},{32,224},{48,240},{64,128},{80,144},{96,160},{112... | collective-permute-start | bytes 147464 | tf_op jit(solution)/shard_map/ppermute | solution.py:330
  34.1 3.2 %collective-permute-start.3 = (f32[24,512]{1,0:T(8,128)S(1)}, f32[24,512]{1,0:T(8,128)S(1)}, u32[]{:S(2)}, u32[]{:S(2)}) collective-permute-start(f32[24,512]{1,0:T(8,128)S(1)} %add.16), channel_id=1, source_target_pairs={{0,64},{16,80},{32,96},{48,112},{64,0},{80,16},{96,32},{112,48},{1... | collective-permute-start | bytes 147464 | tf_op jit(solution)/shard_map/ppermute | solution.py:330
  34.1 4.7 %collective-permute-start.2 = (f32[24,512]{1,0:T(8,128)S(1)}, f32[24,512]{1,0:T(8,128)S(1)}, u32[]{:S(2)}, u32[]{:S(2)}) collective-permute-start(f32[24,512]{1,0:T(8,128)S(1)} %add.16), channel_id=1, source_target_pairs={{0,128},{16,144},{32,160},{48,176},{64,192},{80,208},{96,224},{112... | collective-permute-start | bytes 147464 | tf_op jit(solution)/shard_map/ppermute | solution.py:330

commit v9 on v5

--- a/solution.py
+++ b/solution.py
@@ -310,11 +310,6 @@
     return lax.ppermute(x, axis, [(i, i ^ flip) for i in range(lax.axis_size(axis))])
 
 
-def add_over_x(x):
-    x = x + partner(x, "store", 1)
-    return x + partner(x, "store", 2)
-
-
 def add_over_y(x):
     near, far, across = (partner(x, "store", flip) for flip in (4, 12, 8))
     return (x + across) + (near + far)
@@ -329,10 +324,10 @@
 
     pay, item_part, col, y = bottom(history, w1, w2, w3, n_dept, stores // 4, stores // 8)
     store_parts = exchange(pay, "dept")
-    item_hist = add_over_x(item_part)
+    item_hist = add_over_y(item_part + partner(item_part, "store", 1))
     base = arrange(y, items, horizon)
     base, item_hist = lax.optimization_barrier((base, item_hist))
-    item_hist = add_over_y(item_hist)
+    item_hist = item_hist + partner(item_hist, "store", 2)
     err, item_fc, pay_one = totals(store_parts, item_hist, w1, w2, w3, col, chunk, n_store)
     one = exchange(pay_one, "store")
     pay_two = middle(err, one, chunk, items, n_dept)

time: 71.4 us -> 71.8 us (level)
  transfers between devices with their start and end apart: 6 -> 6, of which waited for: 6 -> 5; matrix products, arithmetic and copies ran while one was open for 0% -> 0% of each run, Pallas kernels for 1% -> 1%
where the time goes in v9:
time: 71.8 us; the launch traced here: 71.6 us
  blocking collectives  27.8 us (39%)
  starting transfers between devices  17.7 us (25%)
  Pallas kernels  16.8 us (23%)
  waiting for transfers between devices  8.48 us (12%)
    all_to_all x2, blocking collectives, exchange(): return lax.all_to_all(x, axis, 0, 0, tiled=True)  27.8 us
    pallas_call x1, Pallas kernels, bottom(): pl.pallas_call(functools.partial(bottom_kernel, chunk, part), grid=(store...  14.1 us
    all_to_all x1, starting transfers between devices, exchange(): return lax.all_to_all(x, axis, 0, 0, tiled=True)  10 us
    ppermute x5, starting transfers between devices, partner(): lax.ppermute(x, axis, [(i, i ^ flip) for i in range(lax.axis_size(axis))])  7.68 us
    ppermute x5, waiting for transfers between devices, partner(): lax.ppermute(x, axis, [(i, i ^ flip) for i in range(lax.axis_size(axis))])  5.78 us
    all_to_all x1, waiting for transfers between devices, exchange(): return lax.all_to_all(x, axis, 0, 0, tiled=True)  2.7 us
  transfers between devices with their start and end apart: 6, of which 5 were waited for; matrix products, arithmetic and copies ran while one was open for 0% of the time, Pallas kernels for 1%

profile of v9, /device:TPU:1, one launch (start us, length us, event | category | flops | bytes accessed | tf_op | source)
XLA Modules:
  0.0 71.6 jit_solution(13033746760012014594)
XLA Ops:
  0.6 0.0 copy-start
  0.6 0.0 copy-start.1
  0.7 0.0 copy-start.2
  0.7 14.1 %bottom.1 = (f32[16,72,128]{2,1,0:T(8,128)}, f32[24,512]{1,0:T(8,128)S(1)}, f32[24,128]{1,0:T(8,128)S(1)}, f32[1536,128]{1,0:T(8,128)S(1)}) custom-call(bf16[256,24,512]{2,1,0:T(8,128)(2,1)} %h_ref.1, bf16[512,512]{1,0:T(8,128)(2,1)} %w1_ref.3, bf16[512,512]{1,0:T(8,128)(2,1)} %w2_ref.3, bf16[28,512]{1,0:T(8,128)(2,1)} %bitcast.3), custom_call_target="tpu_custom_call" | custom-call | flops 7247757312 | bytes 6291456 | tf_op jit(solution)/shard_map/bottom/pallas_call | solution.py:116
  14.7 10.0 %all-to-all-start = ((f32[16,72,128]{2,1,0:T(8,128)}), f32[16,72,128]{2,1,0:T(8,128)S(1)}, u32[]{:S(2)}, u32[]{:S(2)}) async-start(f32[16,72,128]{2,1,0:T(8,128)} %get-tuple-element.18), calls=%async_computation | async-start | bytes 1179648 | tf_op jit(solution)/shard_map/all_to_all | solution.py:306
  24.8 1.0 %collective-permute-start = (f32[24,512]{1,0:T(8,128)S(1)}, f32[24,512]{1,0:T(8,128)S(1)}, u32[]{:S(2)}, u32[]{:S(2)}) collective-permute-start(f32[24,512]{1,0:T(8,128)S(1)} %get-tuple-element.16), channel_id=1, source_target_pairs={{0,16},{16,0},{32,48},{48,32},{64,80},{80,64},{96,112},{112,96},{1... | collective-permute-start | bytes 147464 | tf_op jit(solution)/shard_map/ppermute | solution.py:310
  25.8 0.9 %collective-permute-done = f32[24,512]{1,0:T(8,128)S(1)} collective-permute-done((f32[24,512]{1,0:T(8,128)S(1)}, f32[24,512]{1,0:T(8,128)S(1)}, u32[]{:S(2)}, u32[]{:S(2)}) %collective-permute-start) | collective-permute-done | bytes 49184 | tf_op jit(solution)/shard_map/ppermute | solution.py:310
  26.7 2.8 %collective-permute-start.3 = (f32[24,512]{1,0:T(8,128)S(1)}, f32[24,512]{1,0:T(8,128)S(1)}, u32[]{:S(2)}, u32[]{:S(2)}) collective-permute-start(f32[24,512]{1,0:T(8,128)S(1)} %add.15), channel_id=1, source_target_pairs={{0,192},{16,208},{32,224},{48,240},{64,128},{80,144},{96,160},{112... | collective-permute-start | bytes 147464 | tf_op jit(solution)/shard_map/ppermute | solution.py:310
  29.5 0.0 collective-permute-start.2
  29.5 1.3 %collective-permute-start.1 = (f32[24,512]{1,0:T(8,128)S(1)}, f32[24,512]{1,0:T(8,128)S(1)}, u32[]{:S(2)}, u32[]{:S(2)}) collective-permute-start(f32[24,512]{1,0:T(8,128)S(1)} %add.15), channel_id=1, source_target_pairs={{0,128},{16,144},{32,160},{48,176},{64,192},{80,208},{96,224},{112... | collective-permute-start | bytes 147464 | tf_op jit(solution)/shard_map/ppermute | solution.py:310
  30.8 0.7 arrange.1.base_ref
  31.5 0.0 collective-permute-done.3
  31.5 1.2 %collective-permute-done.2 = f32[24,512]{1,0:T(8,128)S(1)} collective-permute-done((f32[24,512]{1,0:T(8,128)S(1)}, f32[24,512]{1,0:T(8,128)S(1)}, u32[]{:S(2)}, u32[]{:S(2)}) %collective-permute-start.2) | collective-permute-done | bytes 49184 | tf_op jit(solution)/shard_map/ppermute | solution.py:310
  32.8 1.2 %collective-permute-done.1 = f32[24,512]{1,0:T(8,128)S(1)} collective-permute-done((f32[24,512]{1,0:T(8,128)S(1)}, f32[24,512]{1,0:T(8,128)S(1)}, u32[]{:S(2)}, u32[]{:S(2)}) %collective-permute-start.1) | collective-permute-done | bytes 49184 | tf_op jit(solution)/shard_map/ppermute | solution.py:310
  34.0 2.5 %collective-permute-start.4 = (f32[24,512]{1,0:T(8,128)S(1)}, f32[24,512]{1,0:T(8,128)S(1)}, u32[]{:S(2)}, u32[]{:S(2)}) collective-permute-start(f32[24,512]{1,0:T(8,128)S(1)} %add_add_fusion), channel_id=1, source_target_pairs={{0,32},{16,48},{32,0},{48,16},{64,96},{80,112},{96,64},{112,80},{1... | collective-permute-start | bytes 147464 | tf_op jit(solution)/shard_map/ppermute | solution.py:310
  36.5 2.4 %collective-permute-done.4 = f32[24,512]{1,0:T(8,128)S(1)} collective-permute-done((f32[24,512]{1,0:T(8,128)S(1)}, f32[24,512]{1,0:T(8,128)S(1)}, u32[]{:S(2)}, u32[]{:S(2)}) %collective-permute-start.4) | collective-permute-done | bytes 49184 | tf_op jit(solution)/shard_map/ppermute | solution.py:310
  39.0 2.7 %all-to-all-done.s_ref = f32[16,72,128]{2,1,0:T(8,128)S(1)} async-done(((f32[16,72,128]{2,1,0:T(8,128)}), f32[16,72,128]{2,1,0:T(8,128)S(1)}, u32[]{:S(2)}, u32[]{:S(2)}) %all-to-all-start) | async-done | bytes 589856 | tf_op jit(solution)/shard_map/all_to_all | solution.py:306
  41.7 0.0 copy-done
  41.7 0.0 copy-done.1
  41.7 0.0 copy-done.2
  41.7 0.6 totals.1
  42.4 16.6 %all_to_all.15.got_ref.one_ref = f32[16,8,128]{2,1,0:T(8,128)S(1)} all-to-all(f32[16,8,128]{2,1,0:T(8,128)S(1)} %get-tuple-element.22), channel_id=1, replica_groups=mesh['store'=16,'dept'=16] {'store'}, dimensions={0} | all-to-all | bytes 131072 | tf_op jit(solution)/shard_map/all_to_all | solution.py:306
  58.9 11.3 %all_to_all.16.two_ref = f32[16,8,128]{2,1,0:T(8,128)S(1)} all-to-all(f32[16,8,128]{2,1,0:T(8,128)S(1)} %middle.1), channel_id=1, replica_groups=mesh['store'=16,'dept'=16] {'dept'}, dimensions={0} | all-to-all | bytes 131072 | tf_op jit(solution)/shard_map/all_to_all | solution.py:306
  70.2 1.4 %final.1 = (f32[672,256]{1,0:T(8,128)}, f32[28,256]{1,0:T(8,128)}, f32[24,28]{1,0:T(8,128)}) custom-call(f32[672,256]{1,0:T(8,128)S(1)} %arrange.1.base_ref, f32[24,128]{1,0:T(8,128)S(1)} %get-tuple-element.21.item_ref, f32[16,8,128]{2,1,0:T(8,128)S(1)} %all_to_all.15.got_ref.one_ref, f32[16,8,128]{2,1,0:T(8,128)S(1)} %all_to_all.16.two_ref), custom_call_target="tpu_custom_call" | custom-call | tf_op jit(solution)/shard_map/final/pallas_call | solution.py:290
  (4 shorter events, 0.1 us)
Async XLA Ops:
  0.6 41.1 %copy-start = (bf16[512,512]{1,0:T(8,128)(2,1)S(1)}, bf16[512,512]{1,0:T(8,128)(2,1)}, u32[]{:S(2)}) copy-start(bf16[512,512]{1,0:T(8,128)(2,1)} %w1_ref.3) | copy-start | bytes 1572868
  0.6 41.1 %copy-start.1 = (bf16[512,512]{1,0:T(8,128)(2,1)S(1)}, bf16[512,512]{1,0:T(8,128)(2,1)}, u32[]{:S(2)}) copy-start(bf16[512,512]{1,0:T(8,128)(2,1)} %w2_ref.3) | copy-start | bytes 1572868
  0.7 41.0 %copy-start.2 = (bf16[512,28]{0,1:T(8,128)(2,1)S(1)}, bf16[512,28]{0,1:T(8,128)(2,1)}, u32[]{:S(2)}) copy-start(bf16[512,28]{0,1:T(8,128)(2,1)} %param.7) | copy-start | bytes 86020
  14.7 27.0 %all-to-all-start = ((f32[16,72,128]{2,1,0:T(8,128)}), f32[16,72,128]{2,1,0:T(8,128)S(1)}, u32[]{:S(2)}, u32[]{:S(2)}) async-start(f32[16,72,128]{2,1,0:T(8,128)} %get-tuple-element.18), calls=%async_computation | async-start | bytes 1179648 | tf_op jit(solution)/shard_map/all_to_all | solution.py:306
  24.8 1.9 %collective-permute-start = (f32[24,512]{1,0:T(8,128)S(1)}, f32[24,512]{1,0:T(8,128)S(1)}, u32[]{:S(2)}, u32[]{:S(2)}) collective-permute-start(f32[24,512]{1,0:T(8,128)S(1)} %get-tuple-element.16), channel_id=1, source_target_pairs={{0,16},{16,0},{32,48},{48,32},{64,80},{80,64},{96,112},{112,96},{1... | collective-permute-start | bytes 147464 | tf_op jit(solution)/shard_map/ppermute | solution.py:310
  26.7 4.8 %collective-permute-start.3 = (f32[24,512]{1,0:T(8,128)S(1)}, f32[24,512]{1,0:T(8,128)S(1)}, u32[]{:S(2)}, u32[]{:S(2)}) collective-permute-start(f32[24,512]{1,0:T(8,128)S(1)} %add.15), channel_id=1, source_target_pairs={{0,192},{16,208},{32,224},{48,240},{64,128},{80,144},{96,160},{112... | collective-permute-start | bytes 147464 | tf_op jit(solution)/shard_map/ppermute | solution.py:310
  29.5 3.2 %collective-permute-start.2 = (f32[24,512]{1,0:T(8,128)S(1)}, f32[24,512]{1,0:T(8,128)S(1)}, u32[]{:S(2)}, u32[]{:S(2)}) collective-permute-start(f32[24,512]{1,0:T(8,128)S(1)} %add.15), channel_id=1, source_target_pairs={{0,64},{16,80},{32,96},{48,112},{64,0},{80,16},{96,32},{112,48},{1... | collective-permute-start | bytes 147464 | tf_op jit(solution)/shard_map/ppermute | solution.py:310
  29.5 4.4 %collective-permute-start.1 = (f32[24,512]{1,0:T(8,128)S(1)}, f32[24,512]{1,0:T(8,128)S(1)}, u32[]{:S(2)}, u32[]{:S(2)}) collective-permute-start(f32[24,512]{1,0:T(8,128)S(1)} %add.15), channel_id=1, source_target_pairs={{0,128},{16,144},{32,160},{48,176},{64,192},{80,208},{96,224},{112... | collective-permute-start | bytes 147464 | tf_op jit(solution)/shard_map/ppermute | solution.py:310
  34.0 5.0 %collective-permute-start.4 = (f32[24,512]{1,0:T(8,128)S(1)}, f32[24,512]{1,0:T(8,128)S(1)}, u32[]{:S(2)}, u32[]{:S(2)}) collective-permute-start(f32[24,512]{1,0:T(8,128)S(1)} %add_add_fusion), channel_id=1, source_target_pairs={{0,32},{16,48},{32,0},{48,16},{64,96},{80,112},{96,64},{112,80},{1... | collective-permute-start | bytes 147464 | tf_op jit(solution)/shard_map/ppermute | solution.py:310

commit v10 on v5

--- a/solution.py
+++ b/solution.py
@@ -316,8 +316,8 @@
 
 
 def add_over_y(x):
-    near, far, across = (partner(x, "store", flip) for flip in (4, 12, 8))
-    return (x + across) + (near + far)
+    x = x + partner(x, "store", 4)
+    return x + partner(x, "store", 12)
 
 
 def body(history, w1, w2, final_layer_matrix):

time: 71.4 us -> 73.2 us (1.025)
  blocking collectives: 27.4 us -> 29.3 us
    all_to_all x2, blocking collectives: 27.4 us -> 29.3 us  [exchange(): return lax.all_to_all(x, axis, 0, 0, tiled=True)]
    ppermute x5 -> x4, waiting for transfers between devices: 5.62 us -> 5.87 us  [partner(): lax.ppermute(x, axis, [(i, i ^ flip) for i in range(lax.axis_size(axis))])]
    ppermute x5 -> x4, starting transfers between devices: 7.69 us -> 7.79 us  [partner(): lax.ppermute(x, axis, [(i, i ^ flip) for i in range(lax.axis_size(axis))])]
  transfers between devices with their start and end apart: 6 -> 5, of which waited for: 6 -> 5; matrix products, arithmetic and copies ran while one was open for 0% -> 0% of each run, Pallas kernels for 1% -> 1%
where the time goes in v10:
time: 73.2 us; the launch traced here: 73 us
  blocking collectives  29.3 us (40%)
  starting transfers between devices  17.8 us (24%)
  Pallas kernels  16.8 us (23%)
  waiting for transfers between devices  8.37 us (11%)
    all_to_all x2, blocking collectives, exchange(): return lax.all_to_all(x, axis, 0, 0, tiled=True)  29.3 us
    pallas_call x1, Pallas kernels, bottom(): pl.pallas_call(functools.partial(bottom_kernel, chunk, part), grid=(store...  14.1 us
    all_to_all x1, starting transfers between devices, exchange(): return lax.all_to_all(x, axis, 0, 0, tiled=True)  10 us
    ppermute x4, starting transfers between devices, partner(): lax.ppermute(x, axis, [(i, i ^ flip) for i in range(lax.axis_size(axis))])  7.79 us
    ppermute x4, waiting for transfers between devices, partner(): lax.ppermute(x, axis, [(i, i ^ flip) for i in range(lax.axis_size(axis))])  5.87 us
    all_to_all x1, waiting for transfers between devices, exchange(): return lax.all_to_all(x, axis, 0, 0, tiled=True)  2.5 us
  transfers between devices with their start and end apart: 5, of which 5 were waited for; matrix products, arithmetic and copies ran while one was open for 0% of the time, Pallas kernels for 1%

profile of v10, /device:TPU:1, one launch (start us, length us, event | category | flops | bytes accessed | tf_op | source)
XLA Modules:
  0.0 73.0 jit_solution(1006174683812386734)
XLA Ops:
  0.6 0.0 copy-start
  0.6 0.0 copy-start.1
  0.7 0.0 copy-start.2
  0.7 14.1 %bottom.1 = (f32[16,72,128]{2,1,0:T(8,128)}, f32[24,512]{1,0:T(8,128)S(1)}, f32[24,128]{1,0:T(8,128)S(1)}, f32[1536,128]{1,0:T(8,128)S(1)}) custom-call(bf16[256,24,512]{2,1,0:T(8,128)(2,1)} %h_ref.1, bf16[512,512]{1,0:T(8,128)(2,1)} %w1_ref.3, bf16[512,512]{1,0:T(8,128)(2,1)} %w2_ref.3, bf16[28,512]{1,0:T(8,128)(2,1)} %bitcast.3), custom_call_target="tpu_custom_call" | custom-call | flops 7247757312 | bytes 6291456 | tf_op jit(solution)/shard_map/bottom/pallas_call | solution.py:116
  14.7 10.0 %all-to-all-start = ((f32[16,72,128]{2,1,0:T(8,128)}), f32[16,72,128]{2,1,0:T(8,128)S(1)}, u32[]{:S(2)}, u32[]{:S(2)}) async-start(f32[16,72,128]{2,1,0:T(8,128)} %get-tuple-element.18), calls=%async_computation | async-start | bytes 1179648 | tf_op jit(solution)/shard_map/all_to_all | solution.py:306
  24.8 1.0 %collective-permute-start = (f32[24,512]{1,0:T(8,128)S(1)}, f32[24,512]{1,0:T(8,128)S(1)}, u32[]{:S(2)}, u32[]{:S(2)}) collective-permute-start(f32[24,512]{1,0:T(8,128)S(1)} %get-tuple-element.16), channel_id=1, source_target_pairs={{0,16},{16,0},{32,48},{48,32},{64,80},{80,64},{96,112},{112,96},{1... | collective-permute-start | bytes 147464 | tf_op jit(solution)/shard_map/ppermute | solution.py:310
  25.8 0.9 %collective-permute-done = f32[24,512]{1,0:T(8,128)S(1)} collective-permute-done((f32[24,512]{1,0:T(8,128)S(1)}, f32[24,512]{1,0:T(8,128)S(1)}, u32[]{:S(2)}, u32[]{:S(2)}) %collective-permute-start) | collective-permute-done | bytes 49184 | tf_op jit(solution)/shard_map/ppermute | solution.py:310
  26.7 2.5 %collective-permute-start.1 = (f32[24,512]{1,0:T(8,128)S(1)}, f32[24,512]{1,0:T(8,128)S(1)}, u32[]{:S(2)}, u32[]{:S(2)}) collective-permute-start(f32[24,512]{1,0:T(8,128)S(1)} %add.12), channel_id=1, source_target_pairs={{0,32},{16,48},{32,0},{48,16},{64,96},{80,112},{96,64},{112,80},{1... | collective-permute-start | bytes 147464 | tf_op jit(solution)/shard_map/ppermute | solution.py:310
  29.3 0.7 arrange.1.base_ref
  30.0 1.3 %collective-permute-done.1 = f32[24,512]{1,0:T(8,128)S(1)} collective-permute-done((f32[24,512]{1,0:T(8,128)S(1)}, f32[24,512]{1,0:T(8,128)S(1)}, u32[]{:S(2)}, u32[]{:S(2)}) %collective-permute-start.1) | collective-permute-done | bytes 49184 | tf_op jit(solution)/shard_map/ppermute | solution.py:310
  31.3 1.4 %collective-permute-start.2 = (f32[24,512]{1,0:T(8,128)S(1)}, f32[24,512]{1,0:T(8,128)S(1)}, u32[]{:S(2)}, u32[]{:S(2)}) collective-permute-start(f32[24,512]{1,0:T(8,128)S(1)} %add.13), channel_id=1, source_target_pairs={{0,64},{16,80},{32,96},{48,112},{64,0},{80,16},{96,32},{112,48},{1... | collective-permute-start | bytes 147464 | tf_op jit(solution)/shard_map/ppermute | solution.py:310
  32.6 1.9 %collective-permute-done.2 = f32[24,512]{1,0:T(8,128)S(1)} collective-permute-done((f32[24,512]{1,0:T(8,128)S(1)}, f32[24,512]{1,0:T(8,128)S(1)}, u32[]{:S(2)}, u32[]{:S(2)}) %collective-permute-start.2) | collective-permute-done | bytes 49184 | tf_op jit(solution)/shard_map/ppermute | solution.py:310
  34.6 2.8 %collective-permute-start.3 = (f32[24,512]{1,0:T(8,128)S(1)}, f32[24,512]{1,0:T(8,128)S(1)}, u32[]{:S(2)}, u32[]{:S(2)}) collective-permute-start(f32[24,512]{1,0:T(8,128)S(1)} %add.14), channel_id=1, source_target_pairs={{0,192},{16,208},{32,224},{48,240},{64,128},{80,144},{96,160},{112... | collective-permute-start | bytes 147464 | tf_op jit(solution)/shard_map/ppermute | solution.py:310
  37.4 1.8 %collective-permute-done.3 = f32[24,512]{1,0:T(8,128)S(1)} collective-permute-done((f32[24,512]{1,0:T(8,128)S(1)}, f32[24,512]{1,0:T(8,128)S(1)}, u32[]{:S(2)}, u32[]{:S(2)}) %collective-permute-start.3) | collective-permute-done | bytes 49184 | tf_op jit(solution)/shard_map/ppermute | solution.py:310
  39.2 2.5 %all-to-all-done.s_ref = f32[16,72,128]{2,1,0:T(8,128)S(1)} async-done(((f32[16,72,128]{2,1,0:T(8,128)}), f32[16,72,128]{2,1,0:T(8,128)S(1)}, u32[]{:S(2)}, u32[]{:S(2)}) %all-to-all-start) | async-done | bytes 589856 | tf_op jit(solution)/shard_map/all_to_all | solution.py:306
  41.7 0.0 copy-done
  41.7 0.0 copy-done.1
  41.7 0.0 copy-done.2
  41.7 0.6 totals.1
  42.4 16.6 %all_to_all.15.got_ref.one_ref = f32[16,8,128]{2,1,0:T(8,128)S(1)} all-to-all(f32[16,8,128]{2,1,0:T(8,128)S(1)} %get-tuple-element.22), channel_id=1, replica_groups=mesh['store'=16,'dept'=16] {'store'}, dimensions={0} | all-to-all | bytes 131072 | tf_op jit(solution)/shard_map/all_to_all | solution.py:306
  58.9 12.7 %all_to_all.16.two_ref = f32[16,8,128]{2,1,0:T(8,128)S(1)} all-to-all(f32[16,8,128]{2,1,0:T(8,128)S(1)} %middle.1), channel_id=1, replica_groups=mesh['store'=16,'dept'=16] {'dept'}, dimensions={0} | all-to-all | bytes 131072 | tf_op jit(solution)/shard_map/all_to_all | solution.py:306
  71.6 1.4 %final.1 = (f32[672,256]{1,0:T(8,128)}, f32[28,256]{1,0:T(8,128)}, f32[24,28]{1,0:T(8,128)}) custom-call(f32[672,256]{1,0:T(8,128)S(1)} %arrange.1.base_ref, f32[24,128]{1,0:T(8,128)S(1)} %get-tuple-element.21.item_ref, f32[16,8,128]{2,1,0:T(8,128)S(1)} %all_to_all.15.got_ref.one_ref, f32[16,8,128]{2,1,0:T(8,128)S(1)} %all_to_all.16.two_ref), custom_call_target="tpu_custom_call" | custom-call | tf_op jit(solution)/shard_map/final/pallas_call | solution.py:290
  (5 shorter events, 0.1 us)
Async XLA Ops:
  0.6 41.1 %copy-start = (bf16[512,512]{1,0:T(8,128)(2,1)S(1)}, bf16[512,512]{1,0:T(8,128)(2,1)}, u32[]{:S(2)}) copy-start(bf16[512,512]{1,0:T(8,128)(2,1)} %w1_ref.3) | copy-start | bytes 1572868
  0.6 41.1 %copy-start.1 = (bf16[512,512]{1,0:T(8,128)(2,1)S(1)}, bf16[512,512]{1,0:T(8,128)(2,1)}, u32[]{:S(2)}) copy-start(bf16[512,512]{1,0:T(8,128)(2,1)} %w2_ref.3) | copy-start | bytes 1572868
  0.7 41.0 %copy-start.2 = (bf16[512,28]{0,1:T(8,128)(2,1)S(1)}, bf16[512,28]{0,1:T(8,128)(2,1)}, u32[]{:S(2)}) copy-start(bf16[512,28]{0,1:T(8,128)(2,1)} %param.7) | copy-start | bytes 86020
  14.7 27.0 %all-to-all-start = ((f32[16,72,128]{2,1,0:T(8,128)}), f32[16,72,128]{2,1,0:T(8,128)S(1)}, u32[]{:S(2)}, u32[]{:S(2)}) async-start(f32[16,72,128]{2,1,0:T(8,128)} %get-tuple-element.18), calls=%async_computation | async-start | bytes 1179648 | tf_op jit(solution)/shard_map/all_to_all | solution.py:306
  24.8 1.9 %collective-permute-start = (f32[24,512]{1,0:T(8,128)S(1)}, f32[24,512]{1,0:T(8,128)S(1)}, u32[]{:S(2)}, u32[]{:S(2)}) collective-permute-start(f32[24,512]{1,0:T(8,128)S(1)} %get-tuple-element.16), channel_id=1, source_target_pairs={{0,16},{16,0},{32,48},{48,32},{64,80},{80,64},{96,112},{112,96},{1... | collective-permute-start | bytes 147464 | tf_op jit(solution)/shard_map/ppermute | solution.py:310
  26.7 4.5 %collective-permute-start.1 = (f32[24,512]{1,0:T(8,128)S(1)}, f32[24,512]{1,0:T(8,128)S(1)}, u32[]{:S(2)}, u32[]{:S(2)}) collective-permute-start(f32[24,512]{1,0:T(8,128)S(1)} %add.12), channel_id=1, source_target_pairs={{0,32},{16,48},{32,0},{48,16},{64,96},{80,112},{96,64},{112,80},{1... | collective-permute-start | bytes 147464 | tf_op jit(solution)/shard_map/ppermute | solution.py:310
  31.3 3.3 %collective-permute-start.2 = (f32[24,512]{1,0:T(8,128)S(1)}, f32[24,512]{1,0:T(8,128)S(1)}, u32[]{:S(2)}, u32[]{:S(2)}) collective-permute-start(f32[24,512]{1,0:T(8,128)S(1)} %add.13), channel_id=1, source_target_pairs={{0,64},{16,80},{32,96},{48,112},{64,0},{80,16},{96,32},{112,48},{1... | collective-permute-start | bytes 147464 | tf_op jit(solution)/shard_map/ppermute | solution.py:310
  34.6 4.6 %collective-permute-start.3 = (f32[24,512]{1,0:T(8,128)S(1)}, f32[24,512]{1,0:T(8,128)S(1)}, u32[]{:S(2)}, u32[]{:S(2)}) collective-permute-start(f32[24,512]{1,0:T(8,128)S(1)} %add.14), channel_id=1, source_target_pairs={{0,192},{16,208},{32,224},{48,240},{64,128},{80,144},{96,160},{112... | collective-permute-start | bytes 147464 | tf_op jit(solution)/shard_map/ppermute | solution.py:310
